TPU v7x, 32 devices: a whole 2x2x4 slice. The times are simulated.
32 devices in a mesh: row: 4 (over y, x), col: 8 (over z, core).
Axes of the slice: x: 2, y: 2, z: 4, core: 2. Of those that a mesh axis runs over, the one named last changes fastest.
Arguments:
- source: float32 [8192, 128], P(('row', 'col')), may hold values from -6 to 6
- value: bfloat16 [8192, 8192], P('row', 'col'), may hold values from -128 to 127, as said below
- occupancy: int32 [64, 64], P('row', 'col'), may hold values 0 or 1
- exponent: int32 [64, 64], P('row', 'col'), may hold values from -3 to 3, as said below
Outputs:
- diffused: float32 [8192, 128], P(('row', 'col'))
Inputs may be any that keep to these rules, and one draw needn't show every extreme that they name: `value`: whole numbers, drawn independently; both ends of the range occur. `exponent`: tile exponents; every value of the range occurs.
All inputs are finite; a program needn't handle non-finite values. No bound on the sum of `occupancy` on one device may be relied on, other than what follows from the above.
Results may differ from a plain program's by a relative error of at most 0.0003.
Values sent between devices are 32-bit elements; how exact they have to be, the bound alone decides.
No kernel may reach another device: no remote copies, remote signals or barrier semaphores. Data moves between devices by JAX's collectives and lax.ppermute only.
A program may use at most 128 MiB of HBM per device.

v0:
```python
import jax
import jax.numpy as jnp
from jax import lax
from jax.sharding import PartitionSpec as P

STEPS = 3


EPSILON = 1e-05
RETAIN = 0.8
TELEPORT = 0.2


def expand_tile(value, occupancy, exponent):
    row_count = value.shape[0]
    col_count = value.shape[1]
    scales = occupancy.astype(jnp.float32) * jnp.exp2(exponent.astype(jnp.float32))
    blocked = (
        value.astype(jnp.float32).reshape(row_count // 128, 128, col_count // 128, 128)
        * scales[:, None, :, None]
    )
    return blocked.reshape(row_count, col_count).astype(jnp.bfloat16)


def shards(source, value, occupancy, exponent):
    adjacency = expand_tile(value, occupancy, exponent)
    row_count = adjacency.shape[0]
    node_count = row_count * lax.axis_size("row")
    wide_tile = adjacency.astype(jnp.float32)
    energy = lax.psum_scatter(
        jnp.sum(wide_tile * wide_tile, axis=1), "col", scatter_dimension=0, tiled=True
    )
    inverse = 1.0 / (jnp.sqrt(node_count * 1.0) * jnp.sqrt(energy / node_count + EPSILON))
    current = source
    for iteration in range(STEPS):
        mixing = jnp.dot(
            adjacency,
            lax.all_gather(current, "row", axis=0, tiled=True),
            precision=lax.Precision.HIGH,
            preferred_element_type=jnp.float32,
        )
        shares = lax.psum_scatter(mixing, "col", scatter_dimension=0, tiled=True)
        current = jnp.tanh(RETAIN * shares * inverse[:, None] + TELEPORT * source)
    return current


def solution(mesh):
    placed = (P(("row", "col"), None), P("row", "col"), P("row", "col"), P("row", "col"))
    return jax.shard_map(
        shards, mesh=mesh, in_specs=placed, out_specs=P(("row", "col"), None), check_vma=False
    )
```

profile of v0, /device:TPU:0, one launch (start us, length us, event | category | flops | bytes accessed | tf_op | source)
XLA Modules:
  0.0 163.6 jit_solution(9083952559043931574)
XLA Ops:
  6.5 0.0 reduce-scatter.4.cloned.1.call-start
  6.5 0.7 exponential_multiply_fusion
  7.2 0.1 copy.6
  7.3 11.9 %all_gather.9 = f32[1024,128]{1,0:T(8,128)S(1)} all-gather(f32[256,128]{1,0:T(8,128)} %param.4), channel_id=1, replica_groups=mesh['row'=4,'col'=8] {'row'}, dimensions={0}, use_global_device_ids=true | all-gather | bytes 655360 | tf_op jit(solution)/shard_map/all_gather | solution.py:38
  19.2 0.0 copy-start.1
  19.2 0.6 mul.56
  19.8 1.6 copy-done.1
  21.4 1.7 %multiply_reduce_fusion = (f32[2048]{0:T(1024)S(1)}, bf16[2048,1024]{1,0:T(8,128)(2,1)S(1)}) fusion(f32[256,8,8,128]{3,2,1,0:T(8,128)S(1)} %bitcast.14, bf16[2048,1024]{1,0:T(8,128)(2,1)S(1)} %copy-done.1), kind=kLoop, calls=%fused_computation.2 | loop fusion | flops 12580864 | bytes 16785408 | tf_op jit(solution)/shard_map/reduce_sum | solution.py:31
  23.0 0.0 copy-start
  23.1 0.0 copy-start.3
  23.1 0.0 copy-start.2
  23.1 1.9 %copy-done = bf16[2048,1024]{1,0:T(8,128)(2,1)} copy-done((bf16[2048,1024]{1,0:T(8,128)(2,1)}, bf16[2048,1024]{1,0:T(8,128)(2,1)S(1)}, u32[]{:S(2)}) %copy-start) | copy-done | bytes 4194328
  25.0 3.3 %fusion.5 = f32[2048,128]{1,0:T(8,128)} fusion(bf16[2048,1024]{1,0:T(8,128)(2,1)S(1)} %get-tuple-element.6, f32[1024,128]{1,0:T(8,128)S(1)} %all_gather.9), kind=kOutput, calls=%fused_computation.12 | convolution fusion | flops 1610612736 | bytes 5767168 | tf_op jit(solution)/shard_map/dot_general | solution.py:36
  28.3 0.0 reduce-scatter.4.cloned.1.call-update
  28.3 0.0 reduce-scatter.6.cloned.1.call-start
  28.4 0.0 copy-done.3
  28.4 0.6 dynamic-slice
  29.6 15.5 %all-reduce = f32[2048]{0:T(1024)S(1)} all-reduce(f32[2048]{0:T(1024)S(1)} %get-tuple-element.5), channel_id=3, replica_groups=mesh['row'=4,'col'=8] {'col'}, use_global_device_ids=true, to_apply=%region_2.0.clone | all-reduce | flops 2048 | bytes 16384
  45.2 0.1 divide_multiply_fusion
  45.3 16.3 %reduce-scatter.4.cloned.1.call-done = f32[256,128]{1,0:T(8,128)} async-done(((f32[2048,128]{1,0:T(8,128)}), f32[256,128]{1,0:T(8,128)}) %reduce-scatter.4.cloned.1.call-update) | async-done | bytes 131088 | tf_op jit(solution)/shard_map/reduce_scatter | solution.py:42
  61.5 0.0 copy-done.2
  61.5 1.0 add_tanh_fusion.2
  62.6 10.0 %all_gather.10 = f32[1024,128]{1,0:T(8,128)S(1)} all-gather(f32[256,128]{1,0:T(8,128)S(1)} %add_tanh_fusion.2), channel_id=1, replica_groups=mesh['row'=4,'col'=8] {'row'}, dimensions={0}, use_global_device_ids=true | all-gather | bytes 655360 | tf_op jit(solution)/shard_map/all_gather | solution.py:38
  72.5 5.5 %fusion.6 = f32[2048,128]{1,0:T(8,128)} fusion(bf16[2048,1024]{1,0:T(8,128)(2,1)} %copy-done, f32[1024,128]{1,0:T(8,128)S(1)} %all_gather.10), kind=kOutput, calls=%fused_computation.13 | convolution fusion | flops 1610612736 | bytes 5767168 | tf_op jit(solution)/shard_map/dot_general | solution.py:36
  78.1 0.0 reduce-scatter.6.cloned.1.call-update
  78.1 0.0 reduce-scatter.8.cloned.1.call-start
  78.1 30.3 %reduce-scatter.6.cloned.1.call-done = f32[256,128]{1,0:T(8,128)} async-done(((f32[2048,128]{1,0:T(8,128)}), f32[256,128]{1,0:T(8,128)}) %reduce-scatter.6.cloned.1.call-update) | async-done | bytes 131088 | tf_op jit(solution)/shard_map/reduce_scatter | solution.py:42
  108.4 1.0 add_tanh_fusion.1
  109.5 10.0 %all_gather.11 = f32[1024,128]{1,0:T(8,128)S(1)} all-gather(f32[256,128]{1,0:T(8,128)S(1)} %add_tanh_fusion.1), channel_id=1, replica_groups=mesh['row'=4,'col'=8] {'row'}, dimensions={0}, use_global_device_ids=true | all-gather | bytes 655360 | tf_op jit(solution)/shard_map/all_gather | solution.py:38
  119.4 5.5 %fusion.7 = f32[2048,128]{1,0:T(8,128)} fusion(bf16[2048,1024]{1,0:T(8,128)(2,1)} %copy-done, f32[1024,128]{1,0:T(8,128)S(1)} %all_gather.11), kind=kOutput, calls=%fused_computation.14 | convolution fusion | flops 1610612736 | bytes 5767168 | tf_op jit(solution)/shard_map/dot_general | solution.py:36
  124.9 0.0 reduce-scatter.8.cloned.1.call-update
  124.9 30.4 %reduce-scatter.8.cloned.1.call-done = f32[256,128]{1,0:T(8,128)} async-done(((f32[2048,128]{1,0:T(8,128)}), f32[256,128]{1,0:T(8,128)}) %reduce-scatter.8.cloned.1.call-update) | async-done | bytes 131088 | tf_op jit(solution)/shard_map/reduce_scatter | solution.py:42
  155.4 1.7 %add_tanh_fusion = f32[256,128]{1,0:T(8,128)} fusion(f32[256,128]{1,0:T(8,128)} %reduce-scatter.8.cloned.1.call-done, f32[256,128]{1,0:T(8,128)S(1)} %copy-done.2, f32[256]{0:T(256)S(1)} %divide_multiply_fusion), kind=kLoop, calls=%fused_computation.3 | loop fusion | flops 98304 | bytes 394240 | tf_op jit(solution)/shard_map/tanh | solution.py:43
Async XLA Ops:
  6.5 55.0 %reduce-scatter.4.cloned.1.call-start = ((), (), s32[]{:S(2)}) async-start(), calls=%async_computation.3 | async-start | bytes 1179648 | tf_op jit(solution)/shard_map/reduce_scatter | solution.py:42
  19.2 2.2 %copy-start.1 = (bf16[2048,1024]{1,0:T(8,128)(2,1)S(1)}, bf16[2048,1024]{1,0:T(8,128)(2,1)}, u32[]{:S(2)}) copy-start(bf16[2048,1024]{1,0:T(8,128)(2,1)} %param.5) | copy-start | bytes 12582916
  23.0 1.9 %copy-start = (bf16[2048,1024]{1,0:T(8,128)(2,1)}, bf16[2048,1024]{1,0:T(8,128)(2,1)S(1)}, u32[]{:S(2)}) copy-start(bf16[2048,1024]{1,0:T(8,128)(2,1)S(1)} %get-tuple-element.6) | copy-start | bytes 12582916
  23.1 5.3 %copy-start.3 = (u32[32]{0:T(128)S(1)}, u32[32]{0:T(128)}, u32[]{:S(2)}) copy-start(u32[32]{0:T(128)} %constant.19) | copy-start | bytes 388
  23.1 38.5 %copy-start.2 = (f32[256,128]{1,0:T(8,128)S(1)}, f32[256,128]{1,0:T(8,128)}, u32[]{:S(2)}) copy-start(f32[256,128]{1,0:T(8,128)} %param.4) | copy-start | bytes 393220
  28.3 80.1 %reduce-scatter.6.cloned.1.call-start = ((), (), s32[]{:S(2)}) async-start(), calls=%async_computation.4 | async-start | bytes 1179648 | tf_op jit(solution)/shard_map/reduce_scatter | solution.py:42
  78.1 77.3 %reduce-scatter.8.cloned.1.call-start = ((), (), s32[]{:S(2)}) async-start(), calls=%async_computation.5 | async-start | bytes 1179648 | tf_op jit(solution)/shard_map/reduce_scatter | solution.py:42
Sparse Core Ops, SparseCore 0:
  28.5 33.0 reduce-scatter.3
  78.2 30.2 reduce-scatter.5
  125.1 30.2 reduce-scatter.7
where the time goes:
time: 164 us
  waiting for transfers between devices  77.1 us (47%)
  blocking collectives  47.3 us (29%)
  matrix products  14.4 us (9%)
  between operations  13.8 us (8%)
  other arithmetic  6.14 us (4%)
  local copies, waits for them, and re-layouts  4.75 us (3%)
    reduce_scatter x3, waiting for transfers between devices, shards(): shares = lax.psum_scatter(mixing, 'col', scatter_dimension=0, tiled=True)  77 us
    all_gather x3, blocking collectives, shards(): lax.all_gather(current, 'row', axis=0, tiled=True)  31.8 us
    unnamed x1, blocking collectives  15.5 us
    dot_general x3, matrix products, shards(): jnp.dot(adjacency, lax.all_gather(current, 'row', axis=0, tiled=True), pr...  14.4 us
    unnamed x9, local copies, waits for them, and re-layouts  4.07 us
    tanh x3, other arithmetic, shards(): current = jnp.tanh(RETAIN * shares * inverse[:, None] + TELEPORT * source)  3.68 us
  transfers between devices with their start and end apart: 3, of which 3 were waited for; matrix products, arithmetic and copies ran while one was open for 0% of the time, Pallas kernels for 0%

commit v1 on v0

v1 whole, which is shorter than its diff:
```python
import functools

import jax
import jax.numpy as jnp
from jax import lax
from jax.experimental import pallas as pl
from jax.experimental.pallas import tpu as pltpu
from jax.sharding import PartitionSpec as P

STEPS = 3
TILE = 128
EPSILON = 1e-05
RETAIN = 0.8
TELEPORT = 0.2
VMEM = pl.BlockSpec(memory_space=pltpu.VMEM)


def params(mib):
    return pltpu.CompilerParams(vmem_limit_bytes=mib * 1024 * 1024)


def swap(array, axis, size, offset):
    return lax.ppermute(array, axis, [(i, i ^ offset) for i in range(size)])


def prepare_kernel(chunks, span, rows_ref, cols_ref, scale_ref, value_ref, out_ref, energy_ref):
    block = rows_ref[pl.program_id(0)]
    parts = span // TILE
    for half in range(parts):
        rows = slice(half * TILE, (half + 1) * TILE)
        total = jnp.zeros((TILE, TILE), jnp.float32)
        for chunk in range(chunks):
            for part in range(parts):
                tile = cols_ref[chunk] * parts + part
                scale = scale_ref[block * parts + half, tile]
                source = pl.ds(pl.multiple_of(tile * TILE, TILE), TILE)
                scaled = value_ref[rows, source].astype(jnp.float32) * scale
                total += scaled * scaled
                target = chunk * span + part * TILE
                out_ref[rows, target : target + TILE] = scaled.astype(jnp.bfloat16)
        energy_ref[0, :, rows] = lax.dot_general(
            jnp.ones((8, TILE), jnp.float32),
            total,
            (((1,), (1,)), ((), ())),
            precision=lax.Precision.HIGHEST,
            preferred_element_type=jnp.float32,
        )


def prepare(value, scales, row_order, col_order, span):
    row_count, col_count = value.shape
    blocks = row_count // span
    return pl.pallas_call(
        functools.partial(prepare_kernel, col_count // span, span),
        grid_spec=pltpu.PrefetchScalarGridSpec(
            num_scalar_prefetch=3,
            grid=(blocks,),
            in_specs=[pl.BlockSpec((span, col_count), lambda i, rows, cols, scale: (rows[i], 0))],
            out_specs=[
                pl.BlockSpec((span, col_count), lambda i, rows, cols, scale: (i, 0)),
                pl.BlockSpec((1, 8, span), lambda i, rows, cols, scale: (i, 0, 0)),
            ],
        ),
        out_shape=[
            jax.ShapeDtypeStruct(value.shape, jnp.bfloat16),
            jax.ShapeDtypeStruct((blocks, 8, span), jnp.float32),
        ],
        compiler_params=params(12),
        name="prepare",
    )(row_order, col_order, scales, value)


def inverse_kernel(nodes, energy_ref, out_ref):
    energy = lax.dot_general(
        energy_ref[...],
        jnp.full((8, TILE), 0.125, jnp.float32),
        (((0,), (0,)), ((), ())),
        precision=lax.Precision.HIGHEST,
        preferred_element_type=jnp.float32,
    )
    norm = jnp.sqrt(jnp.float32(nodes)) * jnp.sqrt(energy / nodes + EPSILON)
    out_ref[...] = 1.0 / norm


def inverse_of(energy, nodes):
    return pl.pallas_call(
        functools.partial(inverse_kernel, nodes),
        out_shape=jax.ShapeDtypeStruct((energy.shape[1], TILE), jnp.float32),
        in_specs=[VMEM],
        out_specs=VMEM,
        compiler_params=params(4),
        name="inverse",
    )(energy)


def multiply_kernel(first_row, first, count, add, adjacency_ref, *refs):
    features, refs = refs[:count], refs[count:]
    total_ref = refs[0] if add else None
    out_ref, both_ref = refs[-2:]
    span, width = features[0].shape
    for i in range(count):
        x = features[i][...]
        high = x.astype(jnp.bfloat16)
        rows = slice(i * span, (i + 1) * span)
        both_ref[rows, :width] = high
        both_ref[rows, width:] = (x - high.astype(jnp.float32)).astype(jnp.bfloat16)
    tile = 256

    def body(i, carry):
        here = pl.ds(pl.multiple_of(i * tile, tile), tile)
        rows = pl.ds(pl.multiple_of(first_row + i * tile, tile), tile)
        both = jnp.dot(
            adjacency_ref[rows, first * span : (first + count) * span],
            both_ref[...],
            preferred_element_type=jnp.float32,
        )
        sums = both[:, :width] + both[:, width:]
        if add:
            sums += total_ref[rows, :]
        out_ref[here, :] = sums
        return carry

    lax.fori_loop(0, out_ref.shape[0] // tile, body, 0)


def multiply(adjacency, first_row, row_count, first, features, total=None):
    span, width = features[0].shape
    count = len(features)
    add = total is not None
    return pl.pallas_call(
        functools.partial(multiply_kernel, first_row, first, count, add),
        out_shape=jax.ShapeDtypeStruct((row_count, width), jnp.float32),
        in_specs=[VMEM] * (1 + count + add),
        out_specs=VMEM,
        scratch_shapes=[pltpu.VMEM((count * span, 2 * width), jnp.bfloat16)],
        compiler_params=params(4),
        cost_estimate=pl.CostEstimate(
            flops=4 * row_count * count * span * width,
            bytes_accessed=2 * row_count * count * span,
            transcendentals=0,
        ),
        name="multiply",
    )(adjacency, *features, *([total] if add else []))


def shards(source, value, occupancy, exponent):
    row_size, col_size = lax.axis_size("row"), lax.axis_size("col")
    span = source.shape[0]
    nodes = value.shape[0] * row_size
    row, col = lax.axis_index("row"), lax.axis_index("col")
    groups = col_size // 2
    offsets = jnp.arange(groups, dtype=jnp.int32) * 2
    row_order = jnp.concatenate([(col ^ 1) ^ offsets, col ^ offsets])
    col_order = row ^ jnp.arange(row_size, dtype=jnp.int32)
    scales = occupancy.astype(jnp.float32) * jnp.exp2(exponent.astype(jnp.float32))
    adjacency, energy = prepare(value, scales, row_order, col_order, span)
    half = groups * span

    def gather(current):
        return [current] + [swap(current, "row", row_size, d) for d in range(1, row_size)]

    pair = swap(energy[:groups], "col", col_size, 1) + energy[groups:]
    total = pair[0]
    for d in range(1, groups):
        total += swap(pair[d], "col", col_size, 2 * d)
    inverse = inverse_of(total, nodes)

    current = source
    for step in range(STEPS):
        features = gather(current)
        first = multiply(adjacency, 0, 2 * half, 0, features[:1])
        if row_size > 2:
            first = multiply(adjacency, 0, 2 * half, 1, features[1:-1], first)
        last = features[-1:]
        other = multiply(adjacency, 0, half, row_size - 1, last, first)
        moved = swap(other, "col", col_size, 1)
        mine = multiply(adjacency, half, half, row_size - 1, last, first)
        sums = [
            mine[d * span : (d + 1) * span] + moved[d * span : (d + 1) * span] for d in range(groups)
        ]
        product = sums[0]
        for d in range(1, groups):
            product += swap(sums[d], "col", col_size, 2 * d)
        current = jnp.tanh(RETAIN * (product * inverse) + TELEPORT * source)
    return current


def solution(mesh):
    placed = (P(("row", "col"), None), P("row", "col"), P("row", "col"), P("row", "col"))
    return jax.shard_map(
        shards, mesh=mesh, in_specs=placed, out_specs=P(("row", "col"), None), check_vma=False
    )
```

time: 164 us -> 95.1 us (0.58)
  blocking collectives: 47.3 us -> 0 us
  waiting for transfers between devices: 77.1 us -> 41.6 us
  starting transfers between devices: 0.09 us -> 28.4 us
  Pallas kernels: 0 us -> 19.8 us
  matrix products: 14.4 us -> 0 us
  between operations: 13.8 us -> 0.27 us
  other arithmetic: 6.14 us -> 1.75 us
  local copies, waits for them, and re-layouts: 4.75 us -> 3.04 us
    reduce_scatter x3 -> x0, waiting for transfers between devices: 77 us -> none  [shards(): shares = lax.psum_scatter(mixing, 'col', scatter_dimension=0, tiled=True)]
    ppermute x0 -> x25, waiting for transfers between devices: none -> 41.6 us  [swap(): return lax.ppermute(array, axis, [(i, i ^ offset) for i in range(size)])]
    all_gather x3 -> x0, blocking collectives: 31.8 us -> none  [shards(): lax.all_gather(current, 'row', axis=0, tiled=True)]
    ppermute x0 -> x25, starting transfers between devices: none -> 28.4 us  [swap(): return lax.ppermute(array, axis, [(i, i ^ offset) for i in range(size)])]
    pallas_call x0 -> x14, Pallas kernels: none -> 19.8 us  [the longest x12 15 us: multiply(): pl.pallas_call(functools.partial(multiply_kernel, first_row, first, count...]
    unnamed x1 -> x0, blocking collectives: 15.5 us -> none
    dot_general x3 -> x0, matrix products: 14.4 us -> none  [shards(): jnp.dot(adjacency, lax.all_gather(current, 'row', axis=0, tiled=True), pr...]
    tanh x3, other arithmetic: 3.68 us -> 0.83 us  [shards(): current = jnp.tanh(RETAIN * (product * inverse) + TELEPORT * source)]
  transfers between devices with their start and end apart: 3 -> 25, of which waited for: 3 -> 15; matrix products, arithmetic and copies ran while one was open for 0% -> 2% of each run, Pallas kernels for 0% -> 18%
where the time goes in v1:
time: 95.1 us; the launch traced here: 94.9 us
  waiting for transfers between devices  41.6 us (44%)
  starting transfers between devices  28.4 us (30%)
  Pallas kernels  19.8 us (21%)
  local copies, waits for them, and re-layouts  3.04 us (3%)
  other arithmetic  1.75 us (2%)
    ppermute x25, waiting for transfers between devices, swap(): return lax.ppermute(array, axis, [(i, i ^ offset) for i in range(size)])  41.6 us
    ppermute x25, starting transfers between devices, swap(): return lax.ppermute(array, axis, [(i, i ^ offset) for i in range(size)])  28.4 us
    pallas_call x12, Pallas kernels, multiply(): pl.pallas_call(functools.partial(multiply_kernel, first_row, first, count...  15 us
    pallas_call x1, Pallas kernels, prepare(): pl.pallas_call(functools.partial(prepare_kernel, col_count // span, span)...  4.47 us
    unnamed x5, local copies, waits for them, and re-layouts  2.95 us
  transfers between devices with their start and end apart: 25, of which 15 were waited for; matrix products, arithmetic and copies ran while one was open for 2% of the time, Pallas kernels for 18%

profile of v1, /device:TPU:0, one launch (start us, length us, event | category | flops | bytes accessed | tf_op | source)
XLA Modules:
  0.0 94.9 jit_solution(14837678431559162465)
XLA Ops:
  0.0 3.0 %collective-permute-start.2 = (f32[256,128]{1,0:T(8,128)}, f32[256,128]{1,0:T(8,128)S(1)}, u32[]{:S(2)}, u32[]{:S(2)}) collective-permute-start(f32[256,128]{1,0:T(8,128)} %refs_0_.1), channel_id=1, source_target_pairs={{0,16},{8,24},{16,0},{24,8},{1,17},{9,25},{17,1},{25,9},{2,18},{10... | collective-permute-start | bytes 393224 | tf_op jit(solution)/shard_map/ppermute | solution.py:23
  3.0 1.5 %collective-permute-start.1 = (f32[256,128]{1,0:T(8,128)}, f32[256,128]{1,0:T(8,128)S(1)}, u32[]{:S(2)}, u32[]{:S(2)}) collective-permute-start(f32[256,128]{1,0:T(8,128)} %refs_0_.1), channel_id=1, source_target_pairs={{0,8},{8,0},{16,24},{24,16},{1,9},{9,1},{17,25},{25,17},{2,10},{10... | collective-permute-start | bytes 393224 | tf_op jit(solution)/shard_map/ppermute | solution.py:23
  4.5 0.7 convert_element_type.6
  5.2 0.1 copy.8
  5.3 0.8 copy.7
  6.0 0.1 pad_add_fusion.rows_ref
  6.1 2.2 %copy-done = bf16[2048,1024]{1,0:T(8,128)(2,1)S(1)} copy-done((bf16[2048,1024]{1,0:T(8,128)(2,1)S(1)}, bf16[2048,1024]{1,0:T(8,128)(2,1)}, u32[]{:S(2)}) %copy-start) | copy-done | bytes 4194328
  8.3 4.5 %prepare.1 = (bf16[2048,1024]{1,0:T(8,128)(2,1)S(1)}, f32[8,8,256]{2,1,0:T(8,128)S(1)}) custom-call(s32[8]{0:T(128)S(1)} %pad_add_fusion.rows_ref, s32[4]{0:T(128)S(1)} %iota_xor_fusion.cols_ref, f32[16,8]{1,0:T(8,128)S(1)} %exponential_multiply_fusion.scale_ref, bf16[2048,1024]{1,0:T(8,128)(2,1)S(1)} %copy-done), custom_call_target="tpu_custom_call" | custom-call | tf_op jit(solution)/shard_map/prepare/pallas_call | solution.py:53
  12.8 1.6 %multiply.12.refs_2_ = f32[2048,128]{1,0:T(8,128)S(1)} custom-call(bf16[2048,1024]{1,0:T(8,128)(2,1)S(1)} %get-tuple-element.7.adjacency_ref, f32[256,128]{1,0:T(8,128)S(1)} %copy-done.1), custom_call_target="tpu_custom_call" | custom-call | flops 268435456 | bytes 1048576 | tf_op jit(solution)/shard_map/multiply/pallas_call | solution.py:130
  14.3 0.0 collective-permute-done.2.refs_1_
  14.4 1.9 %multiply.13.refs_1_ = f32[2048,128]{1,0:T(8,128)S(1)} custom-call(bf16[2048,1024]{1,0:T(8,128)(2,1)S(1)} %get-tuple-element.7.adjacency_ref, f32[256,128]{1,0:T(8,128)S(1)} %collective-permute-done.1.refs_0_, f32[256,128]{1,0:T(8,128)S(1)} %collective-permute-done.2.refs_1_, f32[2048,128]{1,0:T(8,128)S(1)} %multiply.12.refs_2_), custom_call_target="tpu_custom_call" | custom-call | flops 536870912 | bytes 2097152 | tf_op jit(solution)/shard_map/multiply/pallas_call | solution.py:130
  16.3 0.8 multiply.15
  17.1 0.1 collective-permute-start.3
  17.2 0.5 collective-permute-start.7
  17.6 1.4 %collective-permute-done.7 = f32[4,8,256]{2,1,0:T(8,128)S(1)} collective-permute-done((f32[4,8,256]{2,1,0:T(8,128)S(1)}, f32[4,8,256]{2,1,0:T(8,128)S(1)}, u32[]{:S(2)}, u32[]{:S(2)}) %collective-permute-start.7) | collective-permute-done | bytes 32800 | tf_op jit(solution)/shard_map/ppermute | solution.py:23
  19.1 2.1 %collective-permute-start.8 = (f32[8,256]{1,0:T(8,128)S(1)}, f32[8,256]{1,0:T(8,128)S(1)}, u32[]{:S(2)}, u32[]{:S(2)}) collective-permute-start(f32[8,256]{1,0:T(8,128)S(1)} %get-tuple-element.18), channel_id=1, source_target_pairs={{0,2},{1,3},{2,0},{3,1},{4,6},{5,7},{6,4},{7,5},{8,10},{9,11},{10,... | collective-permute-start | bytes 24584 | tf_op jit(solution)/shard_map/ppermute | solution.py:23
  21.2 2.5 %collective-permute-start.10 = (f32[8,256]{1,0:T(8,128)S(1)}, f32[8,256]{1,0:T(8,128)S(1)}, u32[]{:S(2)}, u32[]{:S(2)}) collective-permute-start(f32[8,256]{1,0:T(8,128)S(1)} %get-tuple-element.19), channel_id=1, source_target_pairs={{0,6},{1,7},{2,4},{3,5},{4,2},{5,3},{6,0},{7,1},{8,14},{9,15},{10,... | collective-permute-start | bytes 24584 | tf_op jit(solution)/shard_map/ppermute | solution.py:23
  23.7 0.1 collective-permute-start.9
  23.8 0.8 multiply.14
  24.6 0.0 collective-permute-done.3
  24.7 1.9 %collective-permute-start.4 = (f32[256,128]{1,0:T(8,128)S(1)}, f32[256,128]{1,0:T(8,128)S(1)}, u32[]{:S(2)}, u32[]{:S(2)}) collective-permute-start(f32[256,128]{1,0:T(8,128)S(1)} %get-tuple-element.15), channel_id=1, source_target_pairs={{0,2},{1,3},{2,0},{3,1},{4,6},{5,7},{6,4},{7,5},{8,10},{9,11},{10,... | collective-permute-start | bytes 393224 | tf_op jit(solution)/shard_map/ppermute | solution.py:23
  26.5 2.5 %collective-permute-start.6 = (f32[256,128]{1,0:T(8,128)S(1)}, f32[256,128]{1,0:T(8,128)S(1)}, u32[]{:S(2)}, u32[]{:S(2)}) collective-permute-start(f32[256,128]{1,0:T(8,128)S(1)} %get-tuple-element.16), channel_id=1, source_target_pairs={{0,6},{1,7},{2,4},{3,5},{4,2},{5,3},{6,0},{7,1},{8,14},{9,15},{10,... | collective-permute-start | bytes 393224 | tf_op jit(solution)/shard_map/ppermute | solution.py:23
  29.0 0.0 collective-permute-done.8
  29.0 0.0 collective-permute-start.5
  29.0 0.4 inverse.1
  29.4 0.5 collective-permute-done.4
  29.9 6.0 %collective-permute-done.6 = f32[256,128]{1,0:T(8,128)S(1)} collective-permute-done((f32[256,128]{1,0:T(8,128)S(1)}, f32[256,128]{1,0:T(8,128)S(1)}, u32[]{:S(2)}, u32[]{:S(2)}) %collective-permute-start.6) | collective-permute-done | bytes 131104 | tf_op jit(solution)/shard_map/ppermute | solution.py:23
  35.9 3.7 %collective-permute-done.5 = f32[256,128]{1,0:T(8,128)S(1)} collective-permute-done((f32[256,128]{1,0:T(8,128)S(1)}, f32[256,128]{1,0:T(8,128)S(1)}, u32[]{:S(2)}, u32[]{:S(2)}) %collective-permute-start.5) | collective-permute-done | bytes 131104 | tf_op jit(solution)/shard_map/ppermute | solution.py:23
  39.6 0.1 fusion.20.refs_0_
  39.7 1.6 %collective-permute-start.13 = (f32[256,128]{1,0:T(8,128)S(1)}, f32[256,128]{1,0:T(8,128)S(1)}, u32[]{:S(2)}, u32[]{:S(2)}) collective-permute-start(f32[256,128]{1,0:T(8,128)S(1)} %fusion.20.refs_0_), channel_id=1, source_target_pairs={{0,16},{8,24},{16,0},{24,8},{1,17},{9,25},{17,1},{25,9},{2,18},{10... | collective-permute-start | bytes 393224 | tf_op jit(solution)/shard_map/ppermute | solution.py:23
  41.2 1.5 %collective-permute-start.12 = (f32[256,128]{1,0:T(8,128)S(1)}, f32[256,128]{1,0:T(8,128)S(1)}, u32[]{:S(2)}, u32[]{:S(2)}) collective-permute-start(f32[256,128]{1,0:T(8,128)S(1)} %fusion.20.refs_0_), channel_id=1, source_target_pairs={{0,8},{8,0},{16,24},{24,16},{1,9},{9,1},{17,25},{25,17},{2,10},{10... | collective-permute-start | bytes 393224 | tf_op jit(solution)/shard_map/ppermute | solution.py:23
  42.7 0.5 collective-permute-start.11
  43.2 1.5 %multiply.16.refs_2_ = f32[2048,128]{1,0:T(8,128)S(1)} custom-call(bf16[2048,1024]{1,0:T(8,128)(2,1)S(1)} %get-tuple-element.7.adjacency_ref, f32[256,128]{1,0:T(8,128)S(1)} %fusion.20.refs_0_), custom_call_target="tpu_custom_call" | custom-call | flops 268435456 | bytes 1048576 | tf_op jit(solution)/shard_map/multiply/pallas_call | solution.py:130
  44.8 2.6 %collective-permute-done.12.refs_0_ = f32[256,128]{1,0:T(8,128)S(1)} collective-permute-done((f32[256,128]{1,0:T(8,128)S(1)}, f32[256,128]{1,0:T(8,128)S(1)}, u32[]{:S(2)}, u32[]{:S(2)}) %collective-permute-start.12) | collective-permute-done | bytes 131104 | tf_op jit(solution)/shard_map/ppermute | solution.py:23
  47.3 1.9 %multiply.17.refs_1_ = f32[2048,128]{1,0:T(8,128)S(1)} custom-call(bf16[2048,1024]{1,0:T(8,128)(2,1)S(1)} %get-tuple-element.7.adjacency_ref, f32[256,128]{1,0:T(8,128)S(1)} %collective-permute-done.12.refs_0_, f32[256,128]{1,0:T(8,128)S(1)} %collective-permute-done.13.refs_1_, f32[2048,128]{1,0:T(8,128)S(1)} %multiply.16.refs_2_), custom_call_target="tpu_custom_call" | custom-call | flops 536870912 | bytes 2097152 | tf_op jit(solution)/shard_map/multiply/pallas_call | solution.py:130
  49.2 0.8 multiply.19
  50.0 0.1 collective-permute-start.14
  50.1 0.8 multiply.18
  50.9 1.1 %collective-permute-done.14 = f32[1024,128]{1,0:T(8,128)S(1)} collective-permute-done((f32[1024,128]{1,0:T(8,128)S(1)}, f32[1024,128]{1,0:T(8,128)S(1)}, u32[]{:S(2)}, u32[]{:S(2)}) %collective-permute-start.14) | collective-permute-done | bytes 524320 | tf_op jit(solution)/shard_map/ppermute | solution.py:23
  52.1 0.1 collective-permute-start.15
  52.1 2.2 %collective-permute-start.17 = (f32[256,128]{1,0:T(8,128)S(1)}, f32[256,128]{1,0:T(8,128)S(1)}, u32[]{:S(2)}, u32[]{:S(2)}) collective-permute-start(f32[256,128]{1,0:T(8,128)S(1)} %get-tuple-element.13), channel_id=1, source_target_pairs={{0,6},{1,7},{2,4},{3,5},{4,2},{5,3},{6,0},{7,1},{8,14},{9,15},{10,... | collective-permute-start | bytes 393224 | tf_op jit(solution)/shard_map/ppermute | solution.py:23
  54.3 1.3 %collective-permute-start.16 = (f32[256,128]{1,0:T(8,128)S(1)}, f32[256,128]{1,0:T(8,128)S(1)}, u32[]{:S(2)}, u32[]{:S(2)}) collective-permute-start(f32[256,128]{1,0:T(8,128)S(1)} %get-tuple-element.14), channel_id=1, source_target_pairs={{0,4},{1,5},{2,6},{3,7},{4,0},{5,1},{6,2},{7,3},{8,12},{9,13},{10,... | collective-permute-start | bytes 393224 | tf_op jit(solution)/shard_map/ppermute | solution.py:23
  55.6 2.2 %collective-permute-done.15 = f32[256,128]{1,0:T(8,128)S(1)} collective-permute-done((f32[256,128]{1,0:T(8,128)S(1)}, f32[256,128]{1,0:T(8,128)S(1)}, u32[]{:S(2)}, u32[]{:S(2)}) %collective-permute-start.15) | collective-permute-done | bytes 131104 | tf_op jit(solution)/shard_map/ppermute | solution.py:23
  57.8 3.6 %collective-permute-done.17 = f32[256,128]{1,0:T(8,128)S(1)} collective-permute-done((f32[256,128]{1,0:T(8,128)S(1)}, f32[256,128]{1,0:T(8,128)S(1)}, u32[]{:S(2)}, u32[]{:S(2)}) %collective-permute-start.17) | collective-permute-done | bytes 131104 | tf_op jit(solution)/shard_map/ppermute | solution.py:23
  61.5 5.8 %collective-permute-done.16 = f32[256,128]{1,0:T(8,128)S(1)} collective-permute-done((f32[256,128]{1,0:T(8,128)S(1)}, f32[256,128]{1,0:T(8,128)S(1)}, u32[]{:S(2)}, u32[]{:S(2)}) %collective-permute-start.16) | collective-permute-done | bytes 131104 | tf_op jit(solution)/shard_map/ppermute | solution.py:23
  67.3 0.1 fusion.13.refs_0_
  67.3 1.0 %collective-permute-start.20 = (f32[256,128]{1,0:T(8,128)S(1)}, f32[256,128]{1,0:T(8,128)S(1)}, u32[]{:S(2)}, u32[]{:S(2)}) collective-permute-start(f32[256,128]{1,0:T(8,128)S(1)} %fusion.13.refs_0_), channel_id=1, source_target_pairs={{0,16},{8,24},{16,0},{24,8},{1,17},{9,25},{17,1},{25,9},{2,18},{10... | collective-permute-start | bytes 393224 | tf_op jit(solution)/shard_map/ppermute | solution.py:23
  68.3 1.5 %collective-permute-start.19 = (f32[256,128]{1,0:T(8,128)S(1)}, f32[256,128]{1,0:T(8,128)S(1)}, u32[]{:S(2)}, u32[]{:S(2)}) collective-permute-start(f32[256,128]{1,0:T(8,128)S(1)} %fusion.13.refs_0_), channel_id=1, source_target_pairs={{0,8},{8,0},{16,24},{24,16},{1,9},{9,1},{17,25},{25,17},{2,10},{10... | collective-permute-start | bytes 393224 | tf_op jit(solution)/shard_map/ppermute | solution.py:23
  69.8 1.0 %collective-permute-start.18 = (f32[256,128]{1,0:T(8,128)S(1)}, f32[256,128]{1,0:T(8,128)S(1)}, u32[]{:S(2)}, u32[]{:S(2)}) collective-permute-start(f32[256,128]{1,0:T(8,128)S(1)} %fusion.13.refs_0_), channel_id=1, source_target_pairs={{0,24},{8,16},{16,8},{24,0},{1,25},{9,17},{17,9},{25,1},{2,26},{10... | collective-permute-start | bytes 393224 | tf_op jit(solution)/shard_map/ppermute | solution.py:23
  70.9 1.5 %multiply.20.refs_2_ = f32[2048,128]{1,0:T(8,128)S(1)} custom-call(bf16[2048,1024]{1,0:T(8,128)(2,1)S(1)} %get-tuple-element.7.adjacency_ref, f32[256,128]{1,0:T(8,128)S(1)} %fusion.13.refs_0_), custom_call_target="tpu_custom_call" | custom-call | flops 268435456 | bytes 1048576 | tf_op jit(solution)/shard_map/multiply/pallas_call | solution.py:130
  72.4 1.2 %collective-permute-done.20.refs_1_ = f32[256,128]{1,0:T(8,128)S(1)} collective-permute-done((f32[256,128]{1,0:T(8,128)S(1)}, f32[256,128]{1,0:T(8,128)S(1)}, u32[]{:S(2)}, u32[]{:S(2)}) %collective-permute-start.20) | collective-permute-done | bytes 131104 | tf_op jit(solution)/shard_map/ppermute | solution.py:23
  73.6 0.7 collective-permute-done.19.refs_0_
  74.3 1.9 %multiply.21.refs_1_ = f32[2048,128]{1,0:T(8,128)S(1)} custom-call(bf16[2048,1024]{1,0:T(8,128)(2,1)S(1)} %get-tuple-element.7.adjacency_ref, f32[256,128]{1,0:T(8,128)S(1)} %collective-permute-done.19.refs_0_, f32[256,128]{1,0:T(8,128)S(1)} %collective-permute-done.20.refs_1_, f32[2048,128]{1,0:T(8,128)S(1)} %multiply.20.refs_2_), custom_call_target="tpu_custom_call" | custom-call | flops 536870912 | bytes 2097152 | tf_op jit(solution)/shard_map/multiply/pallas_call | solution.py:130
  76.2 0.8 multiply.23
  77.0 0.1 collective-permute-start.21
  77.0 0.8 multiply.22
  77.8 1.1 %collective-permute-done.21 = f32[1024,128]{1,0:T(8,128)S(1)} collective-permute-done((f32[1024,128]{1,0:T(8,128)S(1)}, f32[1024,128]{1,0:T(8,128)S(1)}, u32[]{:S(2)}, u32[]{:S(2)}) %collective-permute-start.21) | collective-permute-done | bytes 524320 | tf_op jit(solution)/shard_map/ppermute | solution.py:23
  79.0 0.1 collective-permute-start.22
  79.1 1.9 %collective-permute-start.24 = (f32[256,128]{1,0:T(8,128)S(1)}, f32[256,128]{1,0:T(8,128)S(1)}, u32[]{:S(2)}, u32[]{:S(2)}) collective-permute-start(f32[256,128]{1,0:T(8,128)S(1)} %get-tuple-element.10), channel_id=1, source_target_pairs={{0,6},{1,7},{2,4},{3,5},{4,2},{5,3},{6,0},{7,1},{8,14},{9,15},{10,... | collective-permute-start | bytes 393224 | tf_op jit(solution)/shard_map/ppermute | solution.py:23
  81.0 1.5 %collective-permute-start.23 = (f32[256,128]{1,0:T(8,128)S(1)}, f32[256,128]{1,0:T(8,128)S(1)}, u32[]{:S(2)}, u32[]{:S(2)}) collective-permute-start(f32[256,128]{1,0:T(8,128)S(1)} %get-tuple-element.11), channel_id=1, source_target_pairs={{0,4},{1,5},{2,6},{3,7},{4,0},{5,1},{6,2},{7,3},{8,12},{9,13},{10,... | collective-permute-start | bytes 393224 | tf_op jit(solution)/shard_map/ppermute | solution.py:23
  82.5 2.5 %collective-permute-done.22 = f32[256,128]{1,0:T(8,128)S(1)} collective-permute-done((f32[256,128]{1,0:T(8,128)S(1)}, f32[256,128]{1,0:T(8,128)S(1)}, u32[]{:S(2)}, u32[]{:S(2)}) %collective-permute-start.22) | collective-permute-done | bytes 131104 | tf_op jit(solution)/shard_map/ppermute | solution.py:23
  85.0 3.2 %collective-permute-done.24 = f32[256,128]{1,0:T(8,128)S(1)} collective-permute-done((f32[256,128]{1,0:T(8,128)S(1)}, f32[256,128]{1,0:T(8,128)S(1)}, u32[]{:S(2)}, u32[]{:S(2)}) %collective-permute-start.24) | collective-permute-done | bytes 131104 | tf_op jit(solution)/shard_map/ppermute | solution.py:23
  88.2 6.0 %collective-permute-done.23 = f32[256,128]{1,0:T(8,128)S(1)} collective-permute-done((f32[256,128]{1,0:T(8,128)S(1)}, f32[256,128]{1,0:T(8,128)S(1)}, u32[]{:S(2)}, u32[]{:S(2)}) %collective-permute-start.23) | collective-permute-done | bytes 131104 | tf_op jit(solution)/shard_map/ppermute | solution.py:23
  94.2 0.7 fusion.6
  (21 shorter events, 0.2 us)
Async XLA Ops:
  0.0 14.3 %collective-permute-start.2 = (f32[256,128]{1,0:T(8,128)}, f32[256,128]{1,0:T(8,128)S(1)}, u32[]{:S(2)}, u32[]{:S(2)}) collective-permute-start(f32[256,128]{1,0:T(8,128)} %refs_0_.1), channel_id=1, source_target_pairs={{0,16},{8,24},{16,0},{24,8},{1,17},{9,25},{17,1},{25,9},{2,18},{10... | collective-permute-start | bytes 393224 | tf_op jit(solution)/shard_map/ppermute | solution.py:23
  3.0 11.4 %collective-permute-start.1 = (f32[256,128]{1,0:T(8,128)}, f32[256,128]{1,0:T(8,128)S(1)}, u32[]{:S(2)}, u32[]{:S(2)}) collective-permute-start(f32[256,128]{1,0:T(8,128)} %refs_0_.1), channel_id=1, source_target_pairs={{0,8},{8,0},{16,24},{24,16},{1,9},{9,1},{17,25},{25,17},{2,10},{10... | collective-permute-start | bytes 393224 | tf_op jit(solution)/shard_map/ppermute | solution.py:23
  4.5 11.8 %collective-permute-start = (f32[256,128]{1,0:T(8,128)}, f32[256,128]{1,0:T(8,128)S(1)}, u32[]{:S(2)}, u32[]{:S(2)}) collective-permute-start(f32[256,128]{1,0:T(8,128)} %refs_0_.1), channel_id=1, source_target_pairs={{0,24},{8,16},{16,8},{24,0},{1,25},{9,17},{17,9},{25,1},{2,26},{10... | collective-permute-start | bytes 393224 | tf_op jit(solution)/shard_map/ppermute | solution.py:23
  6.1 2.2 %copy-start = (bf16[2048,1024]{1,0:T(8,128)(2,1)S(1)}, bf16[2048,1024]{1,0:T(8,128)(2,1)}, u32[]{:S(2)}) copy-start(bf16[2048,1024]{1,0:T(8,128)(2,1)} %value_ref.1) | copy-start | bytes 12582916
  8.3 4.5 %copy-start.1 = (f32[256,128]{1,0:T(8,128)S(1)}, f32[256,128]{1,0:T(8,128)}, u32[]{:S(2)}) copy-start(f32[256,128]{1,0:T(8,128)} %refs_0_.1) | copy-start | bytes 393220
  17.1 7.5 %collective-permute-start.3 = (f32[1024,128]{1,0:T(8,128)S(1)}, f32[1024,128]{1,0:T(8,128)S(1)}, u32[]{:S(2)}, u32[]{:S(2)}) collective-permute-start(f32[1024,128]{1,0:T(8,128)S(1)} %multiply.15), channel_id=1, source_target_pairs={{0,1},{1,0},{2,3},{3,2},{4,5},{5,4},{6,7},{7,6},{8,9},{9,8},{10,11... | collective-permute-start | bytes 1572872 | tf_op jit(solution)/shard_map/ppermute | solution.py:23
  17.2 1.9 %collective-permute-start.7 = (f32[4,8,256]{2,1,0:T(8,128)S(1)}, f32[4,8,256]{2,1,0:T(8,128)S(1)}, u32[]{:S(2)}, u32[]{:S(2)}) collective-permute-start(f32[4,8,256]{2,1,0:T(8,128)S(1)} %slice.98), channel_id=1, source_target_pairs={{0,1},{1,0},{2,3},{3,2},{4,5},{5,4},{6,7},{7,6},{8,9},{9,8},{10,11... | collective-permute-start | bytes 98312 | tf_op jit(solution)/shard_map/ppermute | solution.py:23
  19.1 9.9 %collective-permute-start.8 = (f32[8,256]{1,0:T(8,128)S(1)}, f32[8,256]{1,0:T(8,128)S(1)}, u32[]{:S(2)}, u32[]{:S(2)}) collective-permute-start(f32[8,256]{1,0:T(8,128)S(1)} %get-tuple-element.18), channel_id=1, source_target_pairs={{0,2},{1,3},{2,0},{3,1},{4,6},{5,7},{6,4},{7,5},{8,10},{9,11},{10,... | collective-permute-start | bytes 24584 | tf_op jit(solution)/shard_map/ppermute | solution.py:23
  21.2 7.8 %collective-permute-start.10 = (f32[8,256]{1,0:T(8,128)S(1)}, f32[8,256]{1,0:T(8,128)S(1)}, u32[]{:S(2)}, u32[]{:S(2)}) collective-permute-start(f32[8,256]{1,0:T(8,128)S(1)} %get-tuple-element.19), channel_id=1, source_target_pairs={{0,6},{1,7},{2,4},{3,5},{4,2},{5,3},{6,0},{7,1},{8,14},{9,15},{10,... | collective-permute-start | bytes 24584 | tf_op jit(solution)/shard_map/ppermute | solution.py:23
  23.7 5.3 %collective-permute-start.9 = (f32[8,256]{1,0:T(8,128)S(1)}, f32[8,256]{1,0:T(8,128)S(1)}, u32[]{:S(2)}, u32[]{:S(2)}) collective-permute-start(f32[8,256]{1,0:T(8,128)S(1)} %get-tuple-element.20), channel_id=1, source_target_pairs={{0,4},{1,5},{2,6},{3,7},{4,0},{5,1},{6,2},{7,3},{8,12},{9,13},{10,... | collective-permute-start | bytes 24584 | tf_op jit(solution)/shard_map/ppermute | solution.py:23
  24.7 5.2 %collective-permute-start.4 = (f32[256,128]{1,0:T(8,128)S(1)}, f32[256,128]{1,0:T(8,128)S(1)}, u32[]{:S(2)}, u32[]{:S(2)}) collective-permute-start(f32[256,128]{1,0:T(8,128)S(1)} %get-tuple-element.15), channel_id=1, source_target_pairs={{0,2},{1,3},{2,0},{3,1},{4,6},{5,7},{6,4},{7,5},{8,10},{9,11},{10,... | collective-permute-start | bytes 393224 | tf_op jit(solution)/shard_map/ppermute | solution.py:23
  26.5 9.4 %collective-permute-start.6 = (f32[256,128]{1,0:T(8,128)S(1)}, f32[256,128]{1,0:T(8,128)S(1)}, u32[]{:S(2)}, u32[]{:S(2)}) collective-permute-start(f32[256,128]{1,0:T(8,128)S(1)} %get-tuple-element.16), channel_id=1, source_target_pairs={{0,6},{1,7},{2,4},{3,5},{4,2},{5,3},{6,0},{7,1},{8,14},{9,15},{10,... | collective-permute-start | bytes 393224 | tf_op jit(solution)/shard_map/ppermute | solution.py:23
  29.0 10.6 %collective-permute-start.5 = (f32[256,128]{1,0:T(8,128)S(1)}, f32[256,128]{1,0:T(8,128)S(1)}, u32[]{:S(2)}, u32[]{:S(2)}) collective-permute-start(f32[256,128]{1,0:T(8,128)S(1)} %get-tuple-element.17), channel_id=1, source_target_pairs={{0,4},{1,5},{2,6},{3,7},{4,0},{5,1},{6,2},{7,3},{8,12},{9,13},{10,... | collective-permute-start | bytes 393224 | tf_op jit(solution)/shard_map/ppermute | solution.py:23
  39.7 5.1 %collective-permute-start.13 = (f32[256,128]{1,0:T(8,128)S(1)}, f32[256,128]{1,0:T(8,128)S(1)}, u32[]{:S(2)}, u32[]{:S(2)}) collective-permute-start(f32[256,128]{1,0:T(8,128)S(1)} %fusion.20.refs_0_), channel_id=1, source_target_pairs={{0,16},{8,24},{16,0},{24,8},{1,17},{9,25},{17,1},{25,9},{2,18},{10... | collective-permute-start | bytes 393224 | tf_op jit(solution)/shard_map/ppermute | solution.py:23
  41.2 6.1 %collective-permute-start.12 = (f32[256,128]{1,0:T(8,128)S(1)}, f32[256,128]{1,0:T(8,128)S(1)}, u32[]{:S(2)}, u32[]{:S(2)}) collective-permute-start(f32[256,128]{1,0:T(8,128)S(1)} %fusion.20.refs_0_), channel_id=1, source_target_pairs={{0,8},{8,0},{16,24},{24,16},{1,9},{9,1},{17,25},{25,17},{2,10},{10... | collective-permute-start | bytes 393224 | tf_op jit(solution)/shard_map/ppermute | solution.py:23
  42.7 6.5 %collective-permute-start.11 = (f32[256,128]{1,0:T(8,128)S(1)}, f32[256,128]{1,0:T(8,128)S(1)}, u32[]{:S(2)}, u32[]{:S(2)}) collective-permute-start(f32[256,128]{1,0:T(8,128)S(1)} %fusion.20.refs_0_), channel_id=1, source_target_pairs={{0,24},{8,16},{16,8},{24,0},{1,25},{9,17},{17,9},{25,1},{2,26},{10... | collective-permute-start | bytes 393224 | tf_op jit(solution)/shard_map/ppermute | solution.py:23
  50.0 2.0 %collective-permute-start.14 = (f32[1024,128]{1,0:T(8,128)S(1)}, f32[1024,128]{1,0:T(8,128)S(1)}, u32[]{:S(2)}, u32[]{:S(2)}) collective-permute-start(f32[1024,128]{1,0:T(8,128)S(1)} %multiply.19), channel_id=1, source_target_pairs={{0,1},{1,0},{2,3},{3,2},{4,5},{5,4},{6,7},{7,6},{8,9},{9,8},{10,11... | collective-permute-start | bytes 1572872 | tf_op jit(solution)/shard_map/ppermute | solution.py:23
  52.1 5.8 %collective-permute-start.15 = (f32[256,128]{1,0:T(8,128)S(1)}, f32[256,128]{1,0:T(8,128)S(1)}, u32[]{:S(2)}, u32[]{:S(2)}) collective-permute-start(f32[256,128]{1,0:T(8,128)S(1)} %get-tuple-element.12), channel_id=1, source_target_pairs={{0,2},{1,3},{2,0},{3,1},{4,6},{5,7},{6,4},{7,5},{8,10},{9,11},{10,... | collective-permute-start | bytes 393224 | tf_op jit(solution)/shard_map/ppermute | solution.py:23
  52.1 9.3 %collective-permute-start.17 = (f32[256,128]{1,0:T(8,128)S(1)}, f32[256,128]{1,0:T(8,128)S(1)}, u32[]{:S(2)}, u32[]{:S(2)}) collective-permute-start(f32[256,128]{1,0:T(8,128)S(1)} %get-tuple-element.13), channel_id=1, source_target_pairs={{0,6},{1,7},{2,4},{3,5},{4,2},{5,3},{6,0},{7,1},{8,14},{9,15},{10,... | collective-permute-start | bytes 393224 | tf_op jit(solution)/shard_map/ppermute | solution.py:23
  54.3 13.0 %collective-permute-start.16 = (f32[256,128]{1,0:T(8,128)S(1)}, f32[256,128]{1,0:T(8,128)S(1)}, u32[]{:S(2)}, u32[]{:S(2)}) collective-permute-start(f32[256,128]{1,0:T(8,128)S(1)} %get-tuple-element.14), channel_id=1, source_target_pairs={{0,4},{1,5},{2,6},{3,7},{4,0},{5,1},{6,2},{7,3},{8,12},{9,13},{10,... | collective-permute-start | bytes 393224 | tf_op jit(solution)/shard_map/ppermute | solution.py:23
  67.3 6.3 %collective-permute-start.20 = (f32[256,128]{1,0:T(8,128)S(1)}, f32[256,128]{1,0:T(8,128)S(1)}, u32[]{:S(2)}, u32[]{:S(2)}) collective-permute-start(f32[256,128]{1,0:T(8,128)S(1)} %fusion.13.refs_0_), channel_id=1, source_target_pairs={{0,16},{8,24},{16,0},{24,8},{1,17},{9,25},{17,1},{25,9},{2,18},{10... | collective-permute-start | bytes 393224 | tf_op jit(solution)/shard_map/ppermute | solution.py:23
  68.3 5.9 %collective-permute-start.19 = (f32[256,128]{1,0:T(8,128)S(1)}, f32[256,128]{1,0:T(8,128)S(1)}, u32[]{:S(2)}, u32[]{:S(2)}) collective-permute-start(f32[256,128]{1,0:T(8,128)S(1)} %fusion.13.refs_0_), channel_id=1, source_target_pairs={{0,8},{8,0},{16,24},{24,16},{1,9},{9,1},{17,25},{25,17},{2,10},{10... | collective-permute-start | bytes 393224 | tf_op jit(solution)/shard_map/ppermute | solution.py:23
  69.8 6.3 %collective-permute-start.18 = (f32[256,128]{1,0:T(8,128)S(1)}, f32[256,128]{1,0:T(8,128)S(1)}, u32[]{:S(2)}, u32[]{:S(2)}) collective-permute-start(f32[256,128]{1,0:T(8,128)S(1)} %fusion.13.refs_0_), channel_id=1, source_target_pairs={{0,24},{8,16},{16,8},{24,0},{1,25},{9,17},{17,9},{25,1},{2,26},{10... | collective-permute-start | bytes 393224 | tf_op jit(solution)/shard_map/ppermute | solution.py:23
  77.0 2.0 %collective-permute-start.21 = (f32[1024,128]{1,0:T(8,128)S(1)}, f32[1024,128]{1,0:T(8,128)S(1)}, u32[]{:S(2)}, u32[]{:S(2)}) collective-permute-start(f32[1024,128]{1,0:T(8,128)S(1)} %multiply.23), channel_id=1, source_target_pairs={{0,1},{1,0},{2,3},{3,2},{4,5},{5,4},{6,7},{7,6},{8,9},{9,8},{10,11... | collective-permute-start | bytes 1572872 | tf_op jit(solution)/shard_map/ppermute | solution.py:23
  79.0 6.0 %collective-permute-start.22 = (f32[256,128]{1,0:T(8,128)S(1)}, f32[256,128]{1,0:T(8,128)S(1)}, u32[]{:S(2)}, u32[]{:S(2)}) collective-permute-start(f32[256,128]{1,0:T(8,128)S(1)} %get-tuple-element.9), channel_id=1, source_target_pairs={{0,2},{1,3},{2,0},{3,1},{4,6},{5,7},{6,4},{7,5},{8,10},{9,11},{10,... | collective-permute-start | bytes 393224 | tf_op jit(solution)/shard_map/ppermute | solution.py:23
  79.1 9.1 %collective-permute-start.24 = (f32[256,128]{1,0:T(8,128)S(1)}, f32[256,128]{1,0:T(8,128)S(1)}, u32[]{:S(2)}, u32[]{:S(2)}) collective-permute-start(f32[256,128]{1,0:T(8,128)S(1)} %get-tuple-element.10), channel_id=1, source_target_pairs={{0,6},{1,7},{2,4},{3,5},{4,2},{5,3},{6,0},{7,1},{8,14},{9,15},{10,... | collective-permute-start | bytes 393224 | tf_op jit(solution)/shard_map/ppermute | solution.py:23
  81.0 13.2 %collective-permute-start.23 = (f32[256,128]{1,0:T(8,128)S(1)}, f32[256,128]{1,0:T(8,128)S(1)}, u32[]{:S(2)}, u32[]{:S(2)}) collective-permute-start(f32[256,128]{1,0:T(8,128)S(1)} %get-tuple-element.11), channel_id=1, source_target_pairs={{0,4},{1,5},{2,6},{3,7},{4,0},{5,1},{6,2},{7,3},{8,12},{9,13},{10,... | collective-permute-start | bytes 393224 | tf_op jit(solution)/shard_map/ppermute | solution.py:23

commit v2 on v1

v2 whole, which is shorter than its diff:
```python
import functools

import jax
import jax.numpy as jnp
from jax import lax
from jax.experimental import pallas as pl
from jax.experimental.pallas import tpu as pltpu
from jax.sharding import PartitionSpec as P


STEPS = 3
TILE = 128
EPSILON = 1e-05
RETAIN = 0.8
TELEPORT = 0.2
VMEM = pl.BlockSpec(memory_space=pltpu.VMEM)


def params(mib):
    return pltpu.CompilerParams(vmem_limit_bytes=mib * 1024 * 1024)


def swap(array, axis, size, offset):
    return lax.ppermute(array, axis, [(i, i ^ offset) for i in range(size)])


def prepare_kernel(chunks, rows_ref, cols_ref, present_ref, power_ref, value_ref, out_ref, energy_ref, held, arrived):
    blocks, span, _ = held.shape
    parts = span // TILE

    def copy(i):
        start = pl.multiple_of(rows_ref[i] * span, span)
        return pltpu.make_async_copy(value_ref.at[pl.ds(start, span)], held.at[i], arrived.at[i])

    for i in range(blocks):
        copy(i).start()

    def body(i, carry):
        copy(i).wait()
        for half in range(parts):
            rows = slice(half * TILE, (half + 1) * TILE)
            target_rows = pl.ds(pl.multiple_of(i * span + half * TILE, TILE), TILE)
            row_tile = rows_ref[i] * parts + half
            total = jnp.zeros((TILE, TILE), jnp.float32)
            for chunk in range(chunks):
                for part in range(parts):
                    tile = cols_ref[chunk] * parts + part
                    power = jnp.int32(1) << (power_ref[tile, row_tile] + 3)
                    scale = (present_ref[tile, row_tile] * power).astype(jnp.float32) * 0.125
                    from_cols = pl.ds(pl.multiple_of(tile * TILE, TILE), TILE)
                    scaled = held[i, rows, from_cols].astype(jnp.float32) * scale
                    total += scaled * scaled
                    target = chunk * span + part * TILE
                    out_ref[target_rows, target : target + TILE] = scaled.astype(jnp.bfloat16)
            energy_ref[target_rows, :] = total
        return carry

    lax.fori_loop(0, blocks, body, 0)


def prepare(value, present, power, row_order, col_order, span):
    row_count, col_count = value.shape
    blocks = row_count // span
    smem = pl.BlockSpec(memory_space=pltpu.SMEM)
    return pl.pallas_call(
        functools.partial(prepare_kernel, col_count // span),
        in_specs=[smem] * 4 + [pl.BlockSpec(memory_space=pltpu.HBM)],
        out_specs=[VMEM, VMEM],
        out_shape=[
            jax.ShapeDtypeStruct(value.shape, jnp.bfloat16),
            jax.ShapeDtypeStruct((row_count, TILE), jnp.float32),
        ],
        scratch_shapes=[
            pltpu.VMEM((blocks, span, col_count), jnp.bfloat16),
            pltpu.SemaphoreType.DMA((blocks,)),
        ],
        compiler_params=params(48),
        name="prepare",
    )(row_order, col_order, present.T, power.T, value)


def energy_kernel(total_ref, out_ref):
    total = total_ref[...]
    ones = jnp.ones((8, TILE), jnp.bfloat16)
    sums = jnp.zeros(out_ref.shape, jnp.float32)
    for _ in range(3):
        piece = total.astype(jnp.bfloat16)
        total -= piece.astype(jnp.float32)
        sums += lax.dot_general(
            ones, piece, (((1,), (1,)), ((), ())), preferred_element_type=jnp.float32
        )
    out_ref[...] = sums


def energy_of(total):
    return pl.pallas_call(
        energy_kernel,
        out_shape=jax.ShapeDtypeStruct((8, total.shape[0]), jnp.float32),
        in_specs=[VMEM],
        out_specs=VMEM,
        compiler_params=params(8),
        name="energy",
    )(total)


def inverse_kernel(nodes, energy_ref, out_ref):
    energy = lax.dot_general(
        energy_ref[...],
        jnp.full((8, TILE), 0.125, jnp.float32),
        (((0,), (0,)), ((), ())),
        precision=lax.Precision.HIGHEST,
        preferred_element_type=jnp.float32,
    )
    norm = jnp.sqrt(jnp.float32(nodes)) * jnp.sqrt(energy / nodes + EPSILON)
    out_ref[...] = 1.0 / norm


def inverse_of(energy, nodes):
    return pl.pallas_call(
        functools.partial(inverse_kernel, nodes),
        out_shape=jax.ShapeDtypeStruct((energy.shape[1], TILE), jnp.float32),
        in_specs=[VMEM],
        out_specs=VMEM,
        compiler_params=params(4),
        name="inverse",
    )(energy)


def multiply_kernel(first_row, first, count, add, adjacency_ref, *refs):
    features, refs = refs[:count], refs[count:]
    total_ref = refs[0] if add else None
    out_ref, both_ref = refs[-2:]
    span, width = features[0].shape
    for i in range(count):
        x = features[i][...]
        high = x.astype(jnp.bfloat16)
        rows = slice(i * span, (i + 1) * span)
        both_ref[rows, :width] = high
        both_ref[rows, width:] = (x - high.astype(jnp.float32)).astype(jnp.bfloat16)
    tile = min(out_ref.shape[0], 2048)
    for start in range(0, out_ref.shape[0], tile):
        rows = slice(first_row + start, first_row + start + tile)
        both = jnp.dot(
            adjacency_ref[rows, first * span : (first + count) * span],
            both_ref[...],
            preferred_element_type=jnp.float32,
        )
        sums = both[:, :width] + both[:, width:]
        if add:
            sums += total_ref[rows, :]
        out_ref[start : start + tile, :] = sums


def multiply(adjacency, first_row, row_count, first, features, total=None):
    span, width = features[0].shape
    count = len(features)
    add = total is not None
    return pl.pallas_call(
        functools.partial(multiply_kernel, first_row, first, count, add),
        out_shape=jax.ShapeDtypeStruct((row_count, width), jnp.float32),
        in_specs=[VMEM] * (1 + count + add),
        out_specs=VMEM,
        scratch_shapes=[pltpu.VMEM((count * span, 2 * width), jnp.bfloat16)],
        compiler_params=params(8),
        cost_estimate=pl.CostEstimate(
            flops=4 * row_count * count * span * width,
            bytes_accessed=2 * row_count * count * span,
            transcendentals=0,
        ),
        name="multiply",
    )(adjacency, *features, *([total] if add else []))


def shards(source, value, occupancy, exponent):
    row_size, col_size = lax.axis_size("row"), lax.axis_size("col")
    span = source.shape[0]
    nodes = value.shape[0] * row_size
    row, col = lax.axis_index("row"), lax.axis_index("col")
    groups = col_size // 2
    half = groups * span
    offsets = jnp.arange(groups, dtype=jnp.int32) * 2
    row_order = jnp.concatenate([(col ^ 1) ^ offsets, col ^ offsets])
    col_order = row ^ jnp.arange(row_size, dtype=jnp.int32)

    def owned(parts):
        total = parts[0]
        for d in range(1, groups):
            total += swap(parts[d], "col", col_size, 2 * d)
        return total

    current = source
    for step in range(STEPS):
        features = [current]
        for d in range(1, row_size):
            features.append(swap(current, "row", row_size, d))
        if step == 0:
            adjacency, squares = prepare(
                value, occupancy, exponent, row_order, col_order, span
            )
        first = multiply(adjacency, 0, 2 * half, 0, features[:1])
        if row_size > 2:
            first = multiply(adjacency, 0, 2 * half, 1, features[1:-1], first)
        last = features[-1:]
        other = multiply(adjacency, 0, half, row_size - 1, last, first)
        moved = swap(other, "col", col_size, 1)
        mine = multiply(adjacency, half, half, row_size - 1, last, first)
        product = owned(
            [
                mine[d * span : (d + 1) * span] + moved[d * span : (d + 1) * span]
                for d in range(groups)
            ],
        )
        if step == 0:
            energy = energy_of(squares)
            energy = energy[:, half:] + swap(energy[:, :half], "col", col_size, 1)
            energy = owned([energy[:, d * span : (d + 1) * span] for d in range(groups)])
            inverse = inverse_of(energy, nodes)
        current = jnp.tanh(RETAIN * (product * inverse) + TELEPORT * source)
    return current


def solution(mesh):
    placed = (P(("row", "col"), None), P("row", "col"), P("row", "col"), P("row", "col"))
    return jax.shard_map(
        shards, mesh=mesh, in_specs=placed, out_specs=P(("row", "col"), None), check_vma=False
    )
```

time: 95.1 us -> 88 us (0.925)
  Pallas kernels: 19.8 us -> 10.3 us
  waiting for transfers between devices: 41.6 us -> 46.3 us
  local copies, waits for them, and re-layouts: 3.04 us -> 1.39 us
    pallas_call x12, Pallas kernels: 15 us -> 5.5 us  [multiply(): pl.pallas_call(functools.partial(multiply_kernel, first_row, first, count...]
    ppermute x25, waiting for transfers between devices: 41.6 us -> 46.3 us  [swap(): return lax.ppermute(array, axis, [(i, i ^ offset) for i in range(size)])]
    unnamed x5 -> x6, local copies, waits for them, and re-layouts: 2.95 us -> 1.38 us
    pallas_call x1 -> x2, Pallas kernels: 4.47 us -> 4.42 us  [the longest x1 3.9 us: prepare(): pl.pallas_call(functools.partial(prepare_kernel, col_count // span), in_s...]
  transfers between devices with their start and end apart: 25 -> 25, of which waited for: 15 -> 18; matrix products, arithmetic and copies ran while one was open for 2% -> 0% of each run, Pallas kernels for 18% -> 11%
where the time goes in v2:
time: 88 us; the launch traced here: 87.8 us
  waiting for transfers between devices  46.3 us (53%)
  starting transfers between devices  28.5 us (32%)
  Pallas kernels  10.3 us (12%)
  local copies, waits for them, and re-layouts  1.39 us (2%)
  other arithmetic  1.11 us (1%)
    ppermute x25, waiting for transfers between devices, swap(): return lax.ppermute(array, axis, [(i, i ^ offset) for i in range(size)])  46.3 us
    ppermute x25, starting transfers between devices, swap(): return lax.ppermute(array, axis, [(i, i ^ offset) for i in range(size)])  28.5 us
    pallas_call x12, Pallas kernels, multiply(): pl.pallas_call(functools.partial(multiply_kernel, first_row, first, count...  5.5 us
    pallas_call x1, Pallas kernels, prepare(): pl.pallas_call(functools.partial(prepare_kernel, col_count // span), in_s...  3.9 us
  transfers between devices with their start and end apart: 25, of which 18 were waited for; matrix products, arithmetic and copies ran while one was open for 0% of the time, Pallas kernels for 11%

profile of v2, /device:TPU:0, one launch (start us, length us, event | category | flops | bytes accessed | tf_op | source)
XLA Modules:
  0.0 87.8 jit_solution(12854148801357405300)
XLA Ops:
  0.0 3.0 %collective-permute-start.2 = (f32[256,128]{1,0:T(8,128)}, f32[256,128]{1,0:T(8,128)S(1)}, u32[]{:S(2)}, u32[]{:S(2)}) collective-permute-start(f32[256,128]{1,0:T(8,128)} %refs_0_.1), channel_id=1, source_target_pairs={{0,16},{8,24},{16,0},{24,8},{1,17},{9,25},{17,1},{25,9},{2,18},{10... | collective-permute-start | bytes 393224 | tf_op jit(solution)/shard_map/ppermute | solution.py:24
  3.0 1.5 %collective-permute-start.1 = (f32[256,128]{1,0:T(8,128)}, f32[256,128]{1,0:T(8,128)S(1)}, u32[]{:S(2)}, u32[]{:S(2)}) collective-permute-start(f32[256,128]{1,0:T(8,128)} %refs_0_.1), channel_id=1, source_target_pairs={{0,8},{8,0},{16,24},{24,16},{1,9},{9,1},{17,25},{25,17},{2,10},{10... | collective-permute-start | bytes 393224 | tf_op jit(solution)/shard_map/ppermute | solution.py:24
  4.5 0.0 collective-permute-start
  4.5 0.1 pad_add_fusion.rows_ref
  4.6 0.7 copy-done.1
  5.3 0.7 copy-done.2
  6.0 3.9 %prepare.1 = (bf16[2048,1024]{1,0:T(8,128)(2,1)S(1)}, f32[2048,128]{1,0:T(8,128)S(1)}) custom-call(s32[8]{0:T(128)S(1)} %pad_add_fusion.rows_ref, s32[4]{0:T(128)S(1)} %iota_xor_fusion.cols_ref, s32[8,16]{1,0:T(8,128)S(1)} %bitcast.2, s32[8,16]{1,0:T(8,128)S(1)} %bitcast.3, bf16[2048,1024]{1,0:T(8,128)(2,1)} %value_ref.1), custom_call_target="tpu_custom_call" | custom-call | tf_op jit(solution)/shard_map/prepare/pallas_call | solution.py:65
  9.9 0.5 multiply.12.refs_2_
  10.4 0.7 multiply.13.refs_1_
  11.2 0.3 multiply.15
  11.5 0.1 collective-permute-start.3
  11.6 0.5 energy.1
  12.1 0.5 collective-permute-start.7
  12.6 0.9 collective-permute-done.7
  13.5 2.1 %collective-permute-start.8 = (f32[8,256]{1,0:T(8,128)S(1)}, f32[8,256]{1,0:T(8,128)S(1)}, u32[]{:S(2)}, u32[]{:S(2)}) collective-permute-start(f32[8,256]{1,0:T(8,128)S(1)} %get-tuple-element.18), channel_id=1, source_target_pairs={{0,2},{1,3},{2,0},{3,1},{4,6},{5,7},{6,4},{7,5},{8,10},{9,11},{10,... | collective-permute-start | bytes 24584 | tf_op jit(solution)/shard_map/ppermute | solution.py:24
  15.6 2.5 %collective-permute-start.10 = (f32[8,256]{1,0:T(8,128)S(1)}, f32[8,256]{1,0:T(8,128)S(1)}, u32[]{:S(2)}, u32[]{:S(2)}) collective-permute-start(f32[8,256]{1,0:T(8,128)S(1)} %get-tuple-element.19), channel_id=1, source_target_pairs={{0,6},{1,7},{2,4},{3,5},{4,2},{5,3},{6,0},{7,1},{8,14},{9,15},{10,... | collective-permute-start | bytes 24584 | tf_op jit(solution)/shard_map/ppermute | solution.py:24
  18.1 0.1 collective-permute-start.9
  18.2 0.3 multiply.14
  18.5 0.1 slice_add_fusion.10
  18.6 1.9 %collective-permute-start.4 = (f32[256,128]{1,0:T(8,128)S(1)}, f32[256,128]{1,0:T(8,128)S(1)}, u32[]{:S(2)}, u32[]{:S(2)}) collective-permute-start(f32[256,128]{1,0:T(8,128)S(1)} %get-tuple-element.15), channel_id=1, source_target_pairs={{0,2},{1,3},{2,0},{3,1},{4,6},{5,7},{6,4},{7,5},{8,10},{9,11},{10,... | collective-permute-start | bytes 393224 | tf_op jit(solution)/shard_map/ppermute | solution.py:24
  20.5 2.5 %collective-permute-start.6 = (f32[256,128]{1,0:T(8,128)S(1)}, f32[256,128]{1,0:T(8,128)S(1)}, u32[]{:S(2)}, u32[]{:S(2)}) collective-permute-start(f32[256,128]{1,0:T(8,128)S(1)} %get-tuple-element.16), channel_id=1, source_target_pairs={{0,6},{1,7},{2,4},{3,5},{4,2},{5,3},{6,0},{7,1},{8,14},{9,15},{10,... | collective-permute-start | bytes 393224 | tf_op jit(solution)/shard_map/ppermute | solution.py:24
  23.0 0.4 inverse.1
  23.3 0.7 collective-permute-done.4
  24.0 6.0 %collective-permute-done.6 = f32[256,128]{1,0:T(8,128)S(1)} collective-permute-done((f32[256,128]{1,0:T(8,128)S(1)}, f32[256,128]{1,0:T(8,128)S(1)}, u32[]{:S(2)}, u32[]{:S(2)}) %collective-permute-start.6) | collective-permute-done | bytes 131104 | tf_op jit(solution)/shard_map/ppermute | solution.py:24
  30.0 3.6 %collective-permute-done.5 = f32[256,128]{1,0:T(8,128)S(1)} collective-permute-done((f32[256,128]{1,0:T(8,128)S(1)}, f32[256,128]{1,0:T(8,128)S(1)}, u32[]{:S(2)}, u32[]{:S(2)}) %collective-permute-start.5) | collective-permute-done | bytes 131104 | tf_op jit(solution)/shard_map/ppermute | solution.py:24
  33.6 0.1 fusion.20.refs_0_
  33.7 1.6 %collective-permute-start.13 = (f32[256,128]{1,0:T(8,128)S(1)}, f32[256,128]{1,0:T(8,128)S(1)}, u32[]{:S(2)}, u32[]{:S(2)}) collective-permute-start(f32[256,128]{1,0:T(8,128)S(1)} %fusion.20.refs_0_), channel_id=1, source_target_pairs={{0,16},{8,24},{16,0},{24,8},{1,17},{9,25},{17,1},{25,9},{2,18},{10... | collective-permute-start | bytes 393224 | tf_op jit(solution)/shard_map/ppermute | solution.py:24
  35.3 1.5 %collective-permute-start.12 = (f32[256,128]{1,0:T(8,128)S(1)}, f32[256,128]{1,0:T(8,128)S(1)}, u32[]{:S(2)}, u32[]{:S(2)}) collective-permute-start(f32[256,128]{1,0:T(8,128)S(1)} %fusion.20.refs_0_), channel_id=1, source_target_pairs={{0,8},{8,0},{16,24},{24,16},{1,9},{9,1},{17,25},{25,17},{2,10},{10... | collective-permute-start | bytes 393224 | tf_op jit(solution)/shard_map/ppermute | solution.py:24
  36.8 0.5 collective-permute-start.11
  37.2 0.5 multiply.16.refs_2_
  37.7 1.0 %collective-permute-done.13.refs_1_ = f32[256,128]{1,0:T(8,128)S(1)} collective-permute-done((f32[256,128]{1,0:T(8,128)S(1)}, f32[256,128]{1,0:T(8,128)S(1)}, u32[]{:S(2)}, u32[]{:S(2)}) %collective-permute-start.13) | collective-permute-done | bytes 131104 | tf_op jit(solution)/shard_map/ppermute | solution.py:24
  38.7 2.6 %collective-permute-done.12.refs_0_ = f32[256,128]{1,0:T(8,128)S(1)} collective-permute-done((f32[256,128]{1,0:T(8,128)S(1)}, f32[256,128]{1,0:T(8,128)S(1)}, u32[]{:S(2)}, u32[]{:S(2)}) %collective-permute-start.12) | collective-permute-done | bytes 131104 | tf_op jit(solution)/shard_map/ppermute | solution.py:24
  41.3 0.7 multiply.17.refs_1_
  42.0 0.9 %collective-permute-done.11.refs_0_ = f32[256,128]{1,0:T(8,128)S(1)} collective-permute-done((f32[256,128]{1,0:T(8,128)S(1)}, f32[256,128]{1,0:T(8,128)S(1)}, u32[]{:S(2)}, u32[]{:S(2)}) %collective-permute-start.11) | collective-permute-done | bytes 131104 | tf_op jit(solution)/shard_map/ppermute | solution.py:24
  43.0 0.3 multiply.19
  43.3 0.1 collective-permute-start.14
  43.4 0.3 multiply.18
  43.7 1.6 %collective-permute-done.14 = f32[1024,128]{1,0:T(8,128)S(1)} collective-permute-done((f32[1024,128]{1,0:T(8,128)S(1)}, f32[1024,128]{1,0:T(8,128)S(1)}, u32[]{:S(2)}, u32[]{:S(2)}) %collective-permute-start.14) | collective-permute-done | bytes 524320 | tf_op jit(solution)/shard_map/ppermute | solution.py:24
  45.3 0.1 collective-permute-start.15
  45.4 2.5 %collective-permute-start.17 = (f32[256,128]{1,0:T(8,128)S(1)}, f32[256,128]{1,0:T(8,128)S(1)}, u32[]{:S(2)}, u32[]{:S(2)}) collective-permute-start(f32[256,128]{1,0:T(8,128)S(1)} %get-tuple-element.13), channel_id=1, source_target_pairs={{0,6},{1,7},{2,4},{3,5},{4,2},{5,3},{6,0},{7,1},{8,14},{9,15},{10,... | collective-permute-start | bytes 393224 | tf_op jit(solution)/shard_map/ppermute | solution.py:24
  47.9 0.9 %collective-permute-start.16 = (f32[256,128]{1,0:T(8,128)S(1)}, f32[256,128]{1,0:T(8,128)S(1)}, u32[]{:S(2)}, u32[]{:S(2)}) collective-permute-start(f32[256,128]{1,0:T(8,128)S(1)} %get-tuple-element.14), channel_id=1, source_target_pairs={{0,4},{1,5},{2,6},{3,7},{4,0},{5,1},{6,2},{7,3},{8,12},{9,13},{10,... | collective-permute-start | bytes 393224 | tf_op jit(solution)/shard_map/ppermute | solution.py:24
  48.9 2.0 %collective-permute-done.15 = f32[256,128]{1,0:T(8,128)S(1)} collective-permute-done((f32[256,128]{1,0:T(8,128)S(1)}, f32[256,128]{1,0:T(8,128)S(1)}, u32[]{:S(2)}, u32[]{:S(2)}) %collective-permute-start.15) | collective-permute-done | bytes 131104 | tf_op jit(solution)/shard_map/ppermute | solution.py:24
  50.9 4.2 %collective-permute-done.17 = f32[256,128]{1,0:T(8,128)S(1)} collective-permute-done((f32[256,128]{1,0:T(8,128)S(1)}, f32[256,128]{1,0:T(8,128)S(1)}, u32[]{:S(2)}, u32[]{:S(2)}) %collective-permute-start.17) | collective-permute-done | bytes 131104 | tf_op jit(solution)/shard_map/ppermute | solution.py:24
  55.1 5.4 %collective-permute-done.16 = f32[256,128]{1,0:T(8,128)S(1)} collective-permute-done((f32[256,128]{1,0:T(8,128)S(1)}, f32[256,128]{1,0:T(8,128)S(1)}, u32[]{:S(2)}, u32[]{:S(2)}) %collective-permute-start.16) | collective-permute-done | bytes 131104 | tf_op jit(solution)/shard_map/ppermute | solution.py:24
  60.5 0.1 fusion.13.refs_0_
  60.6 1.2 %collective-permute-start.20 = (f32[256,128]{1,0:T(8,128)S(1)}, f32[256,128]{1,0:T(8,128)S(1)}, u32[]{:S(2)}, u32[]{:S(2)}) collective-permute-start(f32[256,128]{1,0:T(8,128)S(1)} %fusion.13.refs_0_), channel_id=1, source_target_pairs={{0,16},{8,24},{16,0},{24,8},{1,17},{9,25},{17,1},{25,9},{2,18},{10... | collective-permute-start | bytes 393224 | tf_op jit(solution)/shard_map/ppermute | solution.py:24
  61.9 1.5 %collective-permute-start.19 = (f32[256,128]{1,0:T(8,128)S(1)}, f32[256,128]{1,0:T(8,128)S(1)}, u32[]{:S(2)}, u32[]{:S(2)}) collective-permute-start(f32[256,128]{1,0:T(8,128)S(1)} %fusion.13.refs_0_), channel_id=1, source_target_pairs={{0,8},{8,0},{16,24},{24,16},{1,9},{9,1},{17,25},{25,17},{2,10},{10... | collective-permute-start | bytes 393224 | tf_op jit(solution)/shard_map/ppermute | solution.py:24
  63.4 0.8 collective-permute-start.18
  64.2 0.5 multiply.20.refs_2_
  64.6 1.8 %collective-permute-done.20.refs_1_ = f32[256,128]{1,0:T(8,128)S(1)} collective-permute-done((f32[256,128]{1,0:T(8,128)S(1)}, f32[256,128]{1,0:T(8,128)S(1)}, u32[]{:S(2)}, u32[]{:S(2)}) %collective-permute-start.20) | collective-permute-done | bytes 131104 | tf_op jit(solution)/shard_map/ppermute | solution.py:24
  66.4 0.9 %collective-permute-done.19.refs_0_ = f32[256,128]{1,0:T(8,128)S(1)} collective-permute-done((f32[256,128]{1,0:T(8,128)S(1)}, f32[256,128]{1,0:T(8,128)S(1)}, u32[]{:S(2)}, u32[]{:S(2)}) %collective-permute-start.19) | collective-permute-done | bytes 131104 | tf_op jit(solution)/shard_map/ppermute | solution.py:24
  67.4 0.7 multiply.21.refs_1_
  68.1 1.4 %collective-permute-done.18.refs_0_ = f32[256,128]{1,0:T(8,128)S(1)} collective-permute-done((f32[256,128]{1,0:T(8,128)S(1)}, f32[256,128]{1,0:T(8,128)S(1)}, u32[]{:S(2)}, u32[]{:S(2)}) %collective-permute-start.18) | collective-permute-done | bytes 131104 | tf_op jit(solution)/shard_map/ppermute | solution.py:24
  69.5 0.3 multiply.23
  69.8 0.1 collective-permute-start.21
  69.9 0.3 multiply.22
  70.2 1.6 %collective-permute-done.21 = f32[1024,128]{1,0:T(8,128)S(1)} collective-permute-done((f32[1024,128]{1,0:T(8,128)S(1)}, f32[1024,128]{1,0:T(8,128)S(1)}, u32[]{:S(2)}, u32[]{:S(2)}) %collective-permute-start.21) | collective-permute-done | bytes 524320 | tf_op jit(solution)/shard_map/ppermute | solution.py:24
  71.9 0.1 collective-permute-start.22
  71.9 2.3 %collective-permute-start.24 = (f32[256,128]{1,0:T(8,128)S(1)}, f32[256,128]{1,0:T(8,128)S(1)}, u32[]{:S(2)}, u32[]{:S(2)}) collective-permute-start(f32[256,128]{1,0:T(8,128)S(1)} %get-tuple-element.10), channel_id=1, source_target_pairs={{0,6},{1,7},{2,4},{3,5},{4,2},{5,3},{6,0},{7,1},{8,14},{9,15},{10,... | collective-permute-start | bytes 393224 | tf_op jit(solution)/shard_map/ppermute | solution.py:24
  74.2 1.2 %collective-permute-start.23 = (f32[256,128]{1,0:T(8,128)S(1)}, f32[256,128]{1,0:T(8,128)S(1)}, u32[]{:S(2)}, u32[]{:S(2)}) collective-permute-start(f32[256,128]{1,0:T(8,128)S(1)} %get-tuple-element.11), channel_id=1, source_target_pairs={{0,4},{1,5},{2,6},{3,7},{4,0},{5,1},{6,2},{7,3},{8,12},{9,13},{10,... | collective-permute-start | bytes 393224 | tf_op jit(solution)/shard_map/ppermute | solution.py:24
  75.4 2.1 %collective-permute-done.22 = f32[256,128]{1,0:T(8,128)S(1)} collective-permute-done((f32[256,128]{1,0:T(8,128)S(1)}, f32[256,128]{1,0:T(8,128)S(1)}, u32[]{:S(2)}, u32[]{:S(2)}) %collective-permute-start.22) | collective-permute-done | bytes 131104 | tf_op jit(solution)/shard_map/ppermute | solution.py:24
  77.5 3.9 %collective-permute-done.24 = f32[256,128]{1,0:T(8,128)S(1)} collective-permute-done((f32[256,128]{1,0:T(8,128)S(1)}, f32[256,128]{1,0:T(8,128)S(1)}, u32[]{:S(2)}, u32[]{:S(2)}) %collective-permute-start.24) | collective-permute-done | bytes 131104 | tf_op jit(solution)/shard_map/ppermute | solution.py:24
  81.4 5.6 %collective-permute-done.23 = f32[256,128]{1,0:T(8,128)S(1)} collective-permute-done((f32[256,128]{1,0:T(8,128)S(1)}, f32[256,128]{1,0:T(8,128)S(1)}, u32[]{:S(2)}, u32[]{:S(2)}) %collective-permute-start.23) | collective-permute-done | bytes 131104 | tf_op jit(solution)/shard_map/ppermute | solution.py:24
  87.1 0.7 fusion.6
  (20 shorter events, 0.2 us)
Async XLA Ops:
  0.0 9.9 %copy-start = (f32[256,128]{1,0:T(8,128)S(1)}, f32[256,128]{1,0:T(8,128)}, u32[]{:S(2)}) copy-start(f32[256,128]{1,0:T(8,128)} %refs_0_.1) | copy-start | bytes 393220
  0.0 10.4 %collective-permute-start.2 = (f32[256,128]{1,0:T(8,128)}, f32[256,128]{1,0:T(8,128)S(1)}, u32[]{:S(2)}, u32[]{:S(2)}) collective-permute-start(f32[256,128]{1,0:T(8,128)} %refs_0_.1), channel_id=1, source_target_pairs={{0,16},{8,24},{16,0},{24,8},{1,17},{9,25},{17,1},{25,9},{2,18},{10... | collective-permute-start | bytes 393224 | tf_op jit(solution)/shard_map/ppermute | solution.py:24
  3.0 7.4 %collective-permute-start.1 = (f32[256,128]{1,0:T(8,128)}, f32[256,128]{1,0:T(8,128)S(1)}, u32[]{:S(2)}, u32[]{:S(2)}) collective-permute-start(f32[256,128]{1,0:T(8,128)} %refs_0_.1), channel_id=1, source_target_pairs={{0,8},{8,0},{16,24},{24,16},{1,9},{9,1},{17,25},{25,17},{2,10},{10... | collective-permute-start | bytes 393224 | tf_op jit(solution)/shard_map/ppermute | solution.py:24
  4.5 6.7 %collective-permute-start = (f32[256,128]{1,0:T(8,128)}, f32[256,128]{1,0:T(8,128)S(1)}, u32[]{:S(2)}, u32[]{:S(2)}) collective-permute-start(f32[256,128]{1,0:T(8,128)} %refs_0_.1), channel_id=1, source_target_pairs={{0,24},{8,16},{16,8},{24,0},{1,25},{9,17},{17,9},{25,1},{2,26},{10... | collective-permute-start | bytes 393224 | tf_op jit(solution)/shard_map/ppermute | solution.py:24
  4.6 0.7 copy-start.1
  5.3 0.7 copy-start.2
  11.5 7.0 %collective-permute-start.3 = (f32[1024,128]{1,0:T(8,128)S(1)}, f32[1024,128]{1,0:T(8,128)S(1)}, u32[]{:S(2)}, u32[]{:S(2)}) collective-permute-start(f32[1024,128]{1,0:T(8,128)S(1)} %multiply.15), channel_id=1, source_target_pairs={{0,1},{1,0},{2,3},{3,2},{4,5},{5,4},{6,7},{7,6},{8,9},{9,8},{10,11... | collective-permute-start | bytes 1572872 | tf_op jit(solution)/shard_map/ppermute | solution.py:24
  12.1 1.4 %collective-permute-start.7 = (f32[8,1024]{1,0:T(8,128)S(1)}, f32[8,1024]{1,0:T(8,128)S(1)}, u32[]{:S(2)}, u32[]{:S(2)}) collective-permute-start(f32[8,1024]{1,0:T(8,128)S(1)} %slice.129), channel_id=1, source_target_pairs={{0,1},{1,0},{2,3},{3,2},{4,5},{5,4},{6,7},{7,6},{8,9},{9,8},{10,11... | collective-permute-start | bytes 98312 | tf_op jit(solution)/shard_map/ppermute | solution.py:24
  13.5 9.4 %collective-permute-start.8 = (f32[8,256]{1,0:T(8,128)S(1)}, f32[8,256]{1,0:T(8,128)S(1)}, u32[]{:S(2)}, u32[]{:S(2)}) collective-permute-start(f32[8,256]{1,0:T(8,128)S(1)} %get-tuple-element.18), channel_id=1, source_target_pairs={{0,2},{1,3},{2,0},{3,1},{4,6},{5,7},{6,4},{7,5},{8,10},{9,11},{10,... | collective-permute-start | bytes 24584 | tf_op jit(solution)/shard_map/ppermute | solution.py:24
  15.6 7.3 %collective-permute-start.10 = (f32[8,256]{1,0:T(8,128)S(1)}, f32[8,256]{1,0:T(8,128)S(1)}, u32[]{:S(2)}, u32[]{:S(2)}) collective-permute-start(f32[8,256]{1,0:T(8,128)S(1)} %get-tuple-element.19), channel_id=1, source_target_pairs={{0,6},{1,7},{2,4},{3,5},{4,2},{5,3},{6,0},{7,1},{8,14},{9,15},{10,... | collective-permute-start | bytes 24584 | tf_op jit(solution)/shard_map/ppermute | solution.py:24
  18.1 4.9 %collective-permute-start.9 = (f32[8,256]{1,0:T(8,128)S(1)}, f32[8,256]{1,0:T(8,128)S(1)}, u32[]{:S(2)}, u32[]{:S(2)}) collective-permute-start(f32[8,256]{1,0:T(8,128)S(1)} %get-tuple-element.20), channel_id=1, source_target_pairs={{0,4},{1,5},{2,6},{3,7},{4,0},{5,1},{6,2},{7,3},{8,12},{9,13},{10,... | collective-permute-start | bytes 24584 | tf_op jit(solution)/shard_map/ppermute | solution.py:24
  18.6 5.5 %collective-permute-start.4 = (f32[256,128]{1,0:T(8,128)S(1)}, f32[256,128]{1,0:T(8,128)S(1)}, u32[]{:S(2)}, u32[]{:S(2)}) collective-permute-start(f32[256,128]{1,0:T(8,128)S(1)} %get-tuple-element.15), channel_id=1, source_target_pairs={{0,2},{1,3},{2,0},{3,1},{4,6},{5,7},{6,4},{7,5},{8,10},{9,11},{10,... | collective-permute-start | bytes 393224 | tf_op jit(solution)/shard_map/ppermute | solution.py:24
  20.5 9.5 %collective-permute-start.6 = (f32[256,128]{1,0:T(8,128)S(1)}, f32[256,128]{1,0:T(8,128)S(1)}, u32[]{:S(2)}, u32[]{:S(2)}) collective-permute-start(f32[256,128]{1,0:T(8,128)S(1)} %get-tuple-element.16), channel_id=1, source_target_pairs={{0,6},{1,7},{2,4},{3,5},{4,2},{5,3},{6,0},{7,1},{8,14},{9,15},{10,... | collective-permute-start | bytes 393224 | tf_op jit(solution)/shard_map/ppermute | solution.py:24
  22.9 10.7 %collective-permute-start.5 = (f32[256,128]{1,0:T(8,128)S(1)}, f32[256,128]{1,0:T(8,128)S(1)}, u32[]{:S(2)}, u32[]{:S(2)}) collective-permute-start(f32[256,128]{1,0:T(8,128)S(1)} %get-tuple-element.17), channel_id=1, source_target_pairs={{0,4},{1,5},{2,6},{3,7},{4,0},{5,1},{6,2},{7,3},{8,12},{9,13},{10,... | collective-permute-start | bytes 393224 | tf_op jit(solution)/shard_map/ppermute | solution.py:24
  33.7 5.0 %collective-permute-start.13 = (f32[256,128]{1,0:T(8,128)S(1)}, f32[256,128]{1,0:T(8,128)S(1)}, u32[]{:S(2)}, u32[]{:S(2)}) collective-permute-start(f32[256,128]{1,0:T(8,128)S(1)} %fusion.20.refs_0_), channel_id=1, source_target_pairs={{0,16},{8,24},{16,0},{24,8},{1,17},{9,25},{17,1},{25,9},{2,18},{10... | collective-permute-start | bytes 393224 | tf_op jit(solution)/shard_map/ppermute | solution.py:24
  35.3 6.0 %collective-permute-start.12 = (f32[256,128]{1,0:T(8,128)S(1)}, f32[256,128]{1,0:T(8,128)S(1)}, u32[]{:S(2)}, u32[]{:S(2)}) collective-permute-start(f32[256,128]{1,0:T(8,128)S(1)} %fusion.20.refs_0_), channel_id=1, source_target_pairs={{0,8},{8,0},{16,24},{24,16},{1,9},{9,1},{17,25},{25,17},{2,10},{10... | collective-permute-start | bytes 393224 | tf_op jit(solution)/shard_map/ppermute | solution.py:24
  36.8 6.2 %collective-permute-start.11 = (f32[256,128]{1,0:T(8,128)S(1)}, f32[256,128]{1,0:T(8,128)S(1)}, u32[]{:S(2)}, u32[]{:S(2)}) collective-permute-start(f32[256,128]{1,0:T(8,128)S(1)} %fusion.20.refs_0_), channel_id=1, source_target_pairs={{0,24},{8,16},{16,8},{24,0},{1,25},{9,17},{17,9},{25,1},{2,26},{10... | collective-permute-start | bytes 393224 | tf_op jit(solution)/shard_map/ppermute | solution.py:24
  43.3 2.0 %collective-permute-start.14 = (f32[1024,128]{1,0:T(8,128)S(1)}, f32[1024,128]{1,0:T(8,128)S(1)}, u32[]{:S(2)}, u32[]{:S(2)}) collective-permute-start(f32[1024,128]{1,0:T(8,128)S(1)} %multiply.19), channel_id=1, source_target_pairs={{0,1},{1,0},{2,3},{3,2},{4,5},{5,4},{6,7},{7,6},{8,9},{9,8},{10,11... | collective-permute-start | bytes 1572872 | tf_op jit(solution)/shard_map/ppermute | solution.py:24
  45.3 5.6 %collective-permute-start.15 = (f32[256,128]{1,0:T(8,128)S(1)}, f32[256,128]{1,0:T(8,128)S(1)}, u32[]{:S(2)}, u32[]{:S(2)}) collective-permute-start(f32[256,128]{1,0:T(8,128)S(1)} %get-tuple-element.12), channel_id=1, source_target_pairs={{0,2},{1,3},{2,0},{3,1},{4,6},{5,7},{6,4},{7,5},{8,10},{9,11},{10,... | collective-permute-start | bytes 393224 | tf_op jit(solution)/shard_map/ppermute | solution.py:24
  45.4 9.7 %collective-permute-start.17 = (f32[256,128]{1,0:T(8,128)S(1)}, f32[256,128]{1,0:T(8,128)S(1)}, u32[]{:S(2)}, u32[]{:S(2)}) collective-permute-start(f32[256,128]{1,0:T(8,128)S(1)} %get-tuple-element.13), channel_id=1, source_target_pairs={{0,6},{1,7},{2,4},{3,5},{4,2},{5,3},{6,0},{7,1},{8,14},{9,15},{10,... | collective-permute-start | bytes 393224 | tf_op jit(solution)/shard_map/ppermute | solution.py:24
  47.9 12.6 %collective-permute-start.16 = (f32[256,128]{1,0:T(8,128)S(1)}, f32[256,128]{1,0:T(8,128)S(1)}, u32[]{:S(2)}, u32[]{:S(2)}) collective-permute-start(f32[256,128]{1,0:T(8,128)S(1)} %get-tuple-element.14), channel_id=1, source_target_pairs={{0,4},{1,5},{2,6},{3,7},{4,0},{5,1},{6,2},{7,3},{8,12},{9,13},{10,... | collective-permute-start | bytes 393224 | tf_op jit(solution)/shard_map/ppermute | solution.py:24
  60.6 5.8 %collective-permute-start.20 = (f32[256,128]{1,0:T(8,128)S(1)}, f32[256,128]{1,0:T(8,128)S(1)}, u32[]{:S(2)}, u32[]{:S(2)}) collective-permute-start(f32[256,128]{1,0:T(8,128)S(1)} %fusion.13.refs_0_), channel_id=1, source_target_pairs={{0,16},{8,24},{16,0},{24,8},{1,17},{9,25},{17,1},{25,9},{2,18},{10... | collective-permute-start | bytes 393224 | tf_op jit(solution)/shard_map/ppermute | solution.py:24
  61.9 5.5 %collective-permute-start.19 = (f32[256,128]{1,0:T(8,128)S(1)}, f32[256,128]{1,0:T(8,128)S(1)}, u32[]{:S(2)}, u32[]{:S(2)}) collective-permute-start(f32[256,128]{1,0:T(8,128)S(1)} %fusion.13.refs_0_), channel_id=1, source_target_pairs={{0,8},{8,0},{16,24},{24,16},{1,9},{9,1},{17,25},{25,17},{2,10},{10... | collective-permute-start | bytes 393224 | tf_op jit(solution)/shard_map/ppermute | solution.py:24
  63.4 6.1 %collective-permute-start.18 = (f32[256,128]{1,0:T(8,128)S(1)}, f32[256,128]{1,0:T(8,128)S(1)}, u32[]{:S(2)}, u32[]{:S(2)}) collective-permute-start(f32[256,128]{1,0:T(8,128)S(1)} %fusion.13.refs_0_), channel_id=1, source_target_pairs={{0,24},{8,16},{16,8},{24,0},{1,25},{9,17},{17,9},{25,1},{2,26},{10... | collective-permute-start | bytes 393224 | tf_op jit(solution)/shard_map/ppermute | solution.py:24
  69.8 2.0 %collective-permute-start.21 = (f32[1024,128]{1,0:T(8,128)S(1)}, f32[1024,128]{1,0:T(8,128)S(1)}, u32[]{:S(2)}, u32[]{:S(2)}) collective-permute-start(f32[1024,128]{1,0:T(8,128)S(1)} %multiply.23), channel_id=1, source_target_pairs={{0,1},{1,0},{2,3},{3,2},{4,5},{5,4},{6,7},{7,6},{8,9},{9,8},{10,11... | collective-permute-start | bytes 1572872 | tf_op jit(solution)/shard_map/ppermute | solution.py:24
  71.9 5.6 %collective-permute-start.22 = (f32[256,128]{1,0:T(8,128)S(1)}, f32[256,128]{1,0:T(8,128)S(1)}, u32[]{:S(2)}, u32[]{:S(2)}) collective-permute-start(f32[256,128]{1,0:T(8,128)S(1)} %get-tuple-element.9), channel_id=1, source_target_pairs={{0,2},{1,3},{2,0},{3,1},{4,6},{5,7},{6,4},{7,5},{8,10},{9,11},{10,... | collective-permute-start | bytes 393224 | tf_op jit(solution)/shard_map/ppermute | solution.py:24
  71.9 9.5 %collective-permute-start.24 = (f32[256,128]{1,0:T(8,128)S(1)}, f32[256,128]{1,0:T(8,128)S(1)}, u32[]{:S(2)}, u32[]{:S(2)}) collective-permute-start(f32[256,128]{1,0:T(8,128)S(1)} %get-tuple-element.10), channel_id=1, source_target_pairs={{0,6},{1,7},{2,4},{3,5},{4,2},{5,3},{6,0},{7,1},{8,14},{9,15},{10,... | collective-permute-start | bytes 393224 | tf_op jit(solution)/shard_map/ppermute | solution.py:24
  74.2 12.8 %collective-permute-start.23 = (f32[256,128]{1,0:T(8,128)S(1)}, f32[256,128]{1,0:T(8,128)S(1)}, u32[]{:S(2)}, u32[]{:S(2)}) collective-permute-start(f32[256,128]{1,0:T(8,128)S(1)} %get-tuple-element.11), channel_id=1, source_target_pairs={{0,4},{1,5},{2,6},{3,7},{4,0},{5,1},{6,2},{7,3},{8,12},{9,13},{10,... | collective-permute-start | bytes 393224 | tf_op jit(solution)/shard_map/ppermute | solution.py:24

commit v3 on v2

--- a/solution.py
+++ b/solution.py
@@ -24,7 +24,7 @@
     return lax.ppermute(array, axis, [(i, i ^ offset) for i in range(size)])
 
 
-def prepare_kernel(chunks, rows_ref, cols_ref, present_ref, power_ref, value_ref, out_ref, energy_ref, held, arrived):
+def prepare_kernel(chunks, rows_ref, cols_ref, scale_ref, value_ref, out_ref, energy_ref, held, arrived):
     blocks, span, _ = held.shape
     parts = span // TILE
 
@@ -38,21 +38,20 @@
     def body(i, carry):
         copy(i).wait()
         for half in range(parts):
-            rows = slice(half * TILE, (half + 1) * TILE)
-            target_rows = pl.ds(pl.multiple_of(i * span + half * TILE, TILE), TILE)
+            from_rows = slice(half * TILE, (half + 1) * TILE)
+            to_rows = pl.ds(pl.multiple_of(i * span + half * TILE, TILE), TILE)
             row_tile = rows_ref[i] * parts + half
             total = jnp.zeros((TILE, TILE), jnp.float32)
             for chunk in range(chunks):
                 for part in range(parts):
                     tile = cols_ref[chunk] * parts + part
-                    power = jnp.int32(1) << (power_ref[tile, row_tile] + 3)
-                    scale = (present_ref[tile, row_tile] * power).astype(jnp.float32) * 0.125
+                    scale = scale_ref[tile, row_tile].astype(jnp.float32) * 0.125
                     from_cols = pl.ds(pl.multiple_of(tile * TILE, TILE), TILE)
-                    scaled = held[i, rows, from_cols].astype(jnp.float32) * scale
+                    scaled = held[i, from_rows, from_cols].astype(jnp.float32) * scale
                     total += scaled * scaled
                     target = chunk * span + part * TILE
-                    out_ref[target_rows, target : target + TILE] = scaled.astype(jnp.bfloat16)
-            energy_ref[target_rows, :] = total
+                    out_ref[to_rows, target : target + TILE] = scaled.astype(jnp.bfloat16)
+            energy_ref[to_rows, :] = total
         return carry
 
     lax.fori_loop(0, blocks, body, 0)
@@ -62,9 +61,10 @@
     row_count, col_count = value.shape
     blocks = row_count // span
     smem = pl.BlockSpec(memory_space=pltpu.SMEM)
+    table = (present << (power + 3)).T
     return pl.pallas_call(
         functools.partial(prepare_kernel, col_count // span),
-        in_specs=[smem] * 4 + [pl.BlockSpec(memory_space=pltpu.HBM)],
+        in_specs=[smem] * 3 + [pl.BlockSpec(memory_space=pltpu.HBM)],
         out_specs=[VMEM, VMEM],
         out_shape=[
             jax.ShapeDtypeStruct(value.shape, jnp.bfloat16),
@@ -76,26 +76,30 @@
         ],
         compiler_params=params(48),
         name="prepare",
-    )(row_order, col_order, present.T, power.T, value)
-
-
-def energy_kernel(total_ref, out_ref):
+    )(row_order, col_order, table, value)
+
+
+def energy_kernel(span, total_ref, out_ref):
     total = total_ref[...]
     ones = jnp.ones((8, TILE), jnp.bfloat16)
-    sums = jnp.zeros(out_ref.shape, jnp.float32)
+    sums = jnp.zeros((8, total.shape[0]), jnp.float32)
     for _ in range(3):
         piece = total.astype(jnp.bfloat16)
         total -= piece.astype(jnp.float32)
         sums += lax.dot_general(
             ones, piece, (((1,), (1,)), ((), ())), preferred_element_type=jnp.float32
         )
-    out_ref[...] = sums
-
-
-def energy_of(total):
-    return pl.pallas_call(
-        energy_kernel,
-        out_shape=jax.ShapeDtypeStruct((8, total.shape[0]), jnp.float32),
+    out_ref[...] = jnp.zeros_like(out_ref)
+    for block in range(sums.shape[1] // span):
+        for part in range(span // TILE):
+            start = block * span + part * TILE
+            out_ref[block * 8 + part, :] = sums[0, start : start + TILE]
+
+
+def energy_of(total, span):
+    return pl.pallas_call(
+        functools.partial(energy_kernel, span),
+        out_shape=jax.ShapeDtypeStruct((total.shape[0] // span * 8, TILE), jnp.float32),
         in_specs=[VMEM],
         out_specs=VMEM,
         compiler_params=params(8),
@@ -103,27 +107,79 @@
     )(total)
 
 
-def inverse_kernel(nodes, energy_ref, out_ref):
-    energy = lax.dot_general(
-        energy_ref[...],
-        jnp.full((8, TILE), 0.125, jnp.float32),
-        (((0,), (0,)), ((), ())),
-        precision=lax.Precision.HIGHEST,
-        preferred_element_type=jnp.float32,
-    )
-    norm = jnp.sqrt(jnp.float32(nodes)) * jnp.sqrt(energy / nodes + EPSILON)
-    out_ref[...] = 1.0 / norm
-
-
-def inverse_of(energy, nodes):
-    return pl.pallas_call(
-        functools.partial(inverse_kernel, nodes),
-        out_shape=jax.ShapeDtypeStruct((energy.shape[1], TILE), jnp.float32),
+def combine_kernel(groups, mine_ref, moved_ref, energy_ref, energy_moved_ref, *out_refs):
+    span = mine_ref.shape[0] // groups
+    for d in range(groups):
+        rows, small = slice(d * span, (d + 1) * span), slice(d * 8, (d + 1) * 8)
+        mine = slice((groups + d) * 8, (groups + d + 1) * 8)
+        out_refs[d][:span, :] = mine_ref[rows, :] + moved_ref[rows, :]
+        out_refs[d][span:, :] = energy_ref[mine, :] + energy_moved_ref[small, :]
+
+
+def combine(groups, mine, moved, energy, energy_moved):
+    shape = (mine.shape[0] // groups + 8, mine.shape[1])
+    return pl.pallas_call(
+        functools.partial(combine_kernel, groups),
+        out_shape=[jax.ShapeDtypeStruct(shape, jnp.float32)] * groups,
+        in_specs=[VMEM] * 4,
+        out_specs=[VMEM] * groups,
+        compiler_params=params(4),
+        name="combine",
+    )(mine, moved, energy, energy_moved)
+
+
+def finish_kernel(nodes, count, *refs):
+    parts, (source_ref, current_ref, inverse_ref) = refs[:count], refs[count:]
+    span = source_ref.shape[0]
+    energy = parts[0][span:, :]
+    product = parts[0][:span, :]
+    for part in parts[1:]:
+        energy += part[span:, :]
+        product += part[:span, :]
+    row = lax.broadcasted_iota(jnp.int32, (8, TILE), 0)
+    for half in range(span // TILE):
+        rows = slice(half * TILE, (half + 1) * TILE)
+        column = lax.dot_general(
+            energy,
+            (row == half).astype(jnp.float32),
+            (((0,), (0,)), ((), ())),
+            precision=lax.Precision.HIGHEST,
+            preferred_element_type=jnp.float32,
+        )
+        norm = jnp.sqrt(jnp.float32(nodes)) * jnp.sqrt(column / nodes + EPSILON)
+        inverse = 1.0 / norm
+        inverse_ref[rows, :] = inverse
+        current_ref[rows, :] = jnp.tanh(
+            RETAIN * (product[rows, :] * inverse) + TELEPORT * source_ref[rows, :]
+        )
+
+
+def finish(nodes, parts, source):
+    shape = jax.ShapeDtypeStruct(source.shape, jnp.float32)
+    return pl.pallas_call(
+        functools.partial(finish_kernel, nodes, len(parts)),
+        out_shape=[shape, shape],
+        in_specs=[VMEM] * (len(parts) + 1),
+        out_specs=[VMEM, VMEM],
+        compiler_params=params(4),
+        name="finish",
+    )(*parts, source)
+
+
+def fence_kernel(source_ref, out_ref):
+    out_ref[...] = TELEPORT * source_ref[...]
+
+
+def fence(source):
+    return pl.pallas_call(
+        fence_kernel,
+        out_shape=jax.ShapeDtypeStruct(source.shape, jnp.float32),
         in_specs=[VMEM],
         out_specs=VMEM,
         compiler_params=params(4),
-        name="inverse",
-    )(energy)
+        cost_estimate=pl.CostEstimate(flops=10**10, bytes_accessed=10**8, transcendentals=0),
+        name="fence",
+    )(source)
 
 
 def multiply_kernel(first_row, first, count, add, adjacency_ref, *refs):
@@ -182,11 +238,8 @@
     row_order = jnp.concatenate([(col ^ 1) ^ offsets, col ^ offsets])
     col_order = row ^ jnp.arange(row_size, dtype=jnp.int32)
 
-    def owned(parts):
-        total = parts[0]
-        for d in range(1, groups):
-            total += swap(parts[d], "col", col_size, 2 * d)
-        return total
+    def spread(parts):
+        return [parts[0]] + [swap(parts[d], "col", col_size, 2 * d) for d in range(1, groups)]
 
     current = source
     for step in range(STEPS):
@@ -194,9 +247,10 @@
         for d in range(1, row_size):
             features.append(swap(current, "row", row_size, d))
         if step == 0:
-            adjacency, squares = prepare(
-                value, occupancy, exponent, row_order, col_order, span
-            )
+            teleport = fence(source)
+            adjacency, squares = prepare(value, occupancy, exponent, row_order, col_order, span)
+            energy = energy_of(squares, span)
+            energy_moved = swap(energy[: 8 * groups], "col", col_size, 1)
         first = multiply(adjacency, 0, 2 * half, 0, features[:1])
         if row_size > 2:
             first = multiply(adjacency, 0, 2 * half, 1, features[1:-1], first)
@@ -204,18 +258,16 @@
         other = multiply(adjacency, 0, half, row_size - 1, last, first)
         moved = swap(other, "col", col_size, 1)
         mine = multiply(adjacency, half, half, row_size - 1, last, first)
-        product = owned(
-            [
+        if step == 0:
+            sums = combine(groups, mine, moved, energy, energy_moved)
+            current, inverse = finish(nodes, spread(sums), source)
+        else:
+            sums = [
                 mine[d * span : (d + 1) * span] + moved[d * span : (d + 1) * span]
                 for d in range(groups)
-            ],
-        )
-        if step == 0:
-            energy = energy_of(squares)
-            energy = energy[:, half:] + swap(energy[:, :half], "col", col_size, 1)
-            energy = owned([energy[:, d * span : (d + 1) * span] for d in range(groups)])
-            inverse = inverse_of(energy, nodes)
-        current = jnp.tanh(RETAIN * (product * inverse) + TELEPORT * source)
+            ]
+            product = functools.reduce(jnp.add, spread(sums))
+            current = jnp.tanh(RETAIN * (product * inverse) + teleport)
     return current
 
 

time: 88 us -> 84 us (0.955)
  starting transfers between devices: 28.5 us -> 25.8 us
  local copies, waits for them, and re-layouts: 1.39 us -> 0.01 us
    ppermute x25 -> x22, starting transfers between devices: 28.5 us -> 25.8 us  [swap(): return lax.ppermute(array, axis, [(i, i ^ offset) for i in range(size)])]
    unnamed x6 -> x2, local copies, waits for them, and re-layouts: 1.38 us -> 0.01 us
    ppermute x25 -> x22, waiting for transfers between devices: 46.3 us -> 45.9 us  [swap(): return lax.ppermute(array, axis, [(i, i ^ offset) for i in range(size)])]
  transfers between devices with their start and end apart: 25 -> 22, of which waited for: 18 -> 18; matrix products, arithmetic and copies ran while one was open for 0% -> 1% of each run, Pallas kernels for 11% -> 11%
where the time goes in v3:
time: 84 us; the launch traced here: 83.8 us
  waiting for transfers between devices  45.9 us (55%)
  starting transfers between devices  25.8 us (31%)
  Pallas kernels  10.3 us (12%)
  other arithmetic  1.64 us (2%)
    ppermute x22, waiting for transfers between devices, swap(): return lax.ppermute(array, axis, [(i, i ^ offset) for i in range(size)])  45.9 us
    ppermute x22, starting transfers between devices, swap(): return lax.ppermute(array, axis, [(i, i ^ offset) for i in range(size)])  25.8 us
    pallas_call x12, Pallas kernels, multiply(): pl.pallas_call(functools.partial(multiply_kernel, first_row, first, count...  5.51 us
    pallas_call x1, Pallas kernels, prepare(): pl.pallas_call(functools.partial(prepare_kernel, col_count // span), in_s...  3.83 us
  transfers between devices with their start and end apart: 22, of which 18 were waited for; matrix products, arithmetic and copies ran while one was open for 1% of the time, Pallas kernels for 11%

profile of v3, /device:TPU:0, one launch (start us, length us, event | category | flops | bytes accessed | tf_op | source)
XLA Modules:
  0.0 83.8 jit_solution(3974527228012533699)
XLA Ops:
  0.0 3.0 %collective-permute-start.2 = (f32[256,128]{1,0:T(8,128)}, f32[256,128]{1,0:T(8,128)S(1)}, u32[]{:S(2)}, u32[]{:S(2)}) collective-permute-start(f32[256,128]{1,0:T(8,128)} %source_ref.1), channel_id=1, source_target_pairs={{0,16},{8,24},{16,0},{24,8},{1,17},{9,25},{17,1},{25,9},{2,18},{10... | collective-permute-start | bytes 393224 | tf_op jit(solution)/shard_map/ppermute | solution.py:24
  3.0 1.5 %collective-permute-start.1 = (f32[256,128]{1,0:T(8,128)}, f32[256,128]{1,0:T(8,128)S(1)}, u32[]{:S(2)}, u32[]{:S(2)}) collective-permute-start(f32[256,128]{1,0:T(8,128)} %source_ref.1), channel_id=1, source_target_pairs={{0,8},{8,0},{16,24},{24,16},{1,9},{9,1},{17,25},{25,17},{2,10},{10... | collective-permute-start | bytes 393224 | tf_op jit(solution)/shard_map/ppermute | solution.py:24
  4.5 0.0 collective-permute-start
  4.5 0.7 shift-left_bitcast_fusion.scale_ref
  5.2 0.1 pad_add_fusion.rows_ref
  5.3 3.8 %prepare.1 = (bf16[2048,1024]{1,0:T(8,128)(2,1)S(1)}, f32[2048,128]{1,0:T(8,128)S(1)}) custom-call(s32[8]{0:T(128)S(1)} %pad_add_fusion.rows_ref, s32[4]{0:T(128)S(1)} %iota_xor_fusion.cols_ref, s32[8,16]{1,0:T(8,128)S(1)} %shift-left_bitcast_fusion.scale_ref, bf16[2048,1024]{1,0:T(8,128)(2,1)} %value_ref.1), custom_call_target="tpu_custom_call" | custom-call | tf_op jit(solution)/shard_map/prepare/pallas_call | solution.py:65
  9.2 0.5 multiply.12.refs_2_
  9.6 0.0 collective-permute-done.2.refs_1_
  9.6 0.0 collective-permute-done.1.refs_0_
  9.6 0.8 multiply.13.refs_1_
  10.4 0.3 collective-permute-done.refs_0_
  10.8 0.3 multiply.15
  11.1 0.1 collective-permute-start.3
  11.2 0.5 energy.1.energy_ref
  11.7 0.5 collective-permute-start.4
  12.2 0.3 multiply.14.mine_ref
  12.5 0.5 collective-permute-done.4.energy_moved_ref
  13.1 0.1 combine.1
  13.2 1.8 %collective-permute-start.5 = (f32[264,128]{1,0:T(8,128)S(1)}, f32[264,128]{1,0:T(8,128)S(1)}, u32[]{:S(2)}, u32[]{:S(2)}) collective-permute-start(f32[264,128]{1,0:T(8,128)S(1)} %get-tuple-element.16), channel_id=1, source_target_pairs={{0,2},{1,3},{2,0},{3,1},{4,6},{5,7},{6,4},{7,5},{8,10},{9,11},{10,... | collective-permute-start | bytes 405512 | tf_op jit(solution)/shard_map/ppermute | solution.py:24
  15.0 2.6 %collective-permute-start.6 = (f32[264,128]{1,0:T(8,128)S(1)}, f32[264,128]{1,0:T(8,128)S(1)}, u32[]{:S(2)}, u32[]{:S(2)}) collective-permute-start(f32[264,128]{1,0:T(8,128)S(1)} %get-tuple-element.17), channel_id=1, source_target_pairs={{0,4},{1,5},{2,6},{3,7},{4,0},{5,1},{6,2},{7,3},{8,12},{9,13},{10,... | collective-permute-start | bytes 405512 | tf_op jit(solution)/shard_map/ppermute | solution.py:24
  17.6 0.0 collective-permute-start.7
  17.6 3.6 %collective-permute-done.5.refs_1_ = f32[264,128]{1,0:T(8,128)S(1)} collective-permute-done((f32[264,128]{1,0:T(8,128)S(1)}, f32[264,128]{1,0:T(8,128)S(1)}, u32[]{:S(2)}, u32[]{:S(2)}) %collective-permute-start.5) | collective-permute-done | bytes 135200 | tf_op jit(solution)/shard_map/ppermute | solution.py:24
  21.2 7.0 %collective-permute-done.6.refs_2_ = f32[264,128]{1,0:T(8,128)S(1)} collective-permute-done((f32[264,128]{1,0:T(8,128)S(1)}, f32[264,128]{1,0:T(8,128)S(1)}, u32[]{:S(2)}, u32[]{:S(2)}) %collective-permute-start.6) | collective-permute-done | bytes 135200 | tf_op jit(solution)/shard_map/ppermute | solution.py:24
  28.2 0.0 collective-permute-done.7.refs_3_
  28.2 0.4 finish.1
  28.6 1.6 %collective-permute-start.10 = (f32[256,128]{1,0:T(8,128)S(1)}, f32[256,128]{1,0:T(8,128)S(1)}, u32[]{:S(2)}, u32[]{:S(2)}) collective-permute-start(f32[256,128]{1,0:T(8,128)S(1)} %get-tuple-element.19.refs_0_), channel_id=1, source_target_pairs={{0,16},{8,24},{16,0},{24,8},{1,17},{9,25},{17,1},{25,9},{2,18},{10... | collective-permute-start | bytes 393224 | tf_op jit(solution)/shard_map/ppermute | solution.py:24
  30.1 1.5 %collective-permute-start.9 = (f32[256,128]{1,0:T(8,128)S(1)}, f32[256,128]{1,0:T(8,128)S(1)}, u32[]{:S(2)}, u32[]{:S(2)}) collective-permute-start(f32[256,128]{1,0:T(8,128)S(1)} %get-tuple-element.19.refs_0_), channel_id=1, source_target_pairs={{0,8},{8,0},{16,24},{24,16},{1,9},{9,1},{17,25},{25,17},{2,10},{10... | collective-permute-start | bytes 393224 | tf_op jit(solution)/shard_map/ppermute | solution.py:24
  31.6 0.5 collective-permute-start.8
  32.1 0.5 multiply.16.refs_2_
  32.6 2.4 %collective-permute-done.10.refs_1_ = f32[256,128]{1,0:T(8,128)S(1)} collective-permute-done((f32[256,128]{1,0:T(8,128)S(1)}, f32[256,128]{1,0:T(8,128)S(1)}, u32[]{:S(2)}, u32[]{:S(2)}) %collective-permute-start.10) | collective-permute-done | bytes 131104 | tf_op jit(solution)/shard_map/ppermute | solution.py:24
  35.0 0.1 collective-permute-done.9.refs_0_
  35.1 0.7 multiply.17.refs_1_
  35.9 1.6 %collective-permute-done.8.refs_0_ = f32[256,128]{1,0:T(8,128)S(1)} collective-permute-done((f32[256,128]{1,0:T(8,128)S(1)}, f32[256,128]{1,0:T(8,128)S(1)}, u32[]{:S(2)}, u32[]{:S(2)}) %collective-permute-start.8) | collective-permute-done | bytes 131104 | tf_op jit(solution)/shard_map/ppermute | solution.py:24
  37.5 0.3 multiply.19
  37.8 0.1 collective-permute-start.11
  37.9 0.3 multiply.18
  38.2 1.6 %collective-permute-done.11 = f32[1024,128]{1,0:T(8,128)S(1)} collective-permute-done((f32[1024,128]{1,0:T(8,128)S(1)}, f32[1024,128]{1,0:T(8,128)S(1)}, u32[]{:S(2)}, u32[]{:S(2)}) %collective-permute-start.11) | collective-permute-done | bytes 524320 | tf_op jit(solution)/shard_map/ppermute | solution.py:24
  39.8 0.1 slice_add_fusion.6
  39.9 3.0 %collective-permute-start.12 = (f32[256,128]{1,0:T(8,128)S(1)}, f32[256,128]{1,0:T(8,128)S(1)}, u32[]{:S(2)}, u32[]{:S(2)}) collective-permute-start(f32[256,128]{1,0:T(8,128)S(1)} %get-tuple-element.24), channel_id=1, source_target_pairs={{0,2},{1,3},{2,0},{3,1},{4,6},{5,7},{6,4},{7,5},{8,10},{9,11},{10,... | collective-permute-start | bytes 393224 | tf_op jit(solution)/shard_map/ppermute | solution.py:24
  42.8 2.5 %collective-permute-start.14 = (f32[256,128]{1,0:T(8,128)S(1)}, f32[256,128]{1,0:T(8,128)S(1)}, u32[]{:S(2)}, u32[]{:S(2)}) collective-permute-start(f32[256,128]{1,0:T(8,128)S(1)} %get-tuple-element.25), channel_id=1, source_target_pairs={{0,6},{1,7},{2,4},{3,5},{4,2},{5,3},{6,0},{7,1},{8,14},{9,15},{10,... | collective-permute-start | bytes 393224 | tf_op jit(solution)/shard_map/ppermute | solution.py:24
  45.3 0.0 collective-permute-start.13
  45.3 1.3 %collective-permute-done.12 = f32[256,128]{1,0:T(8,128)S(1)} collective-permute-done((f32[256,128]{1,0:T(8,128)S(1)}, f32[256,128]{1,0:T(8,128)S(1)}, u32[]{:S(2)}, u32[]{:S(2)}) %collective-permute-start.12) | collective-permute-done | bytes 131104 | tf_op jit(solution)/shard_map/ppermute | solution.py:24
  46.6 5.9 %collective-permute-done.14 = f32[256,128]{1,0:T(8,128)S(1)} collective-permute-done((f32[256,128]{1,0:T(8,128)S(1)}, f32[256,128]{1,0:T(8,128)S(1)}, u32[]{:S(2)}, u32[]{:S(2)}) %collective-permute-start.14) | collective-permute-done | bytes 131104 | tf_op jit(solution)/shard_map/ppermute | solution.py:24
  52.5 4.1 %collective-permute-done.13 = f32[256,128]{1,0:T(8,128)S(1)} collective-permute-done((f32[256,128]{1,0:T(8,128)S(1)}, f32[256,128]{1,0:T(8,128)S(1)}, u32[]{:S(2)}, u32[]{:S(2)}) %collective-permute-start.13) | collective-permute-done | bytes 131104 | tf_op jit(solution)/shard_map/ppermute | solution.py:24
  56.6 0.1 fusion.13.refs_0_
  56.6 0.9 %collective-permute-start.17 = (f32[256,128]{1,0:T(8,128)S(1)}, f32[256,128]{1,0:T(8,128)S(1)}, u32[]{:S(2)}, u32[]{:S(2)}) collective-permute-start(f32[256,128]{1,0:T(8,128)S(1)} %fusion.13.refs_0_), channel_id=1, source_target_pairs={{0,16},{8,24},{16,0},{24,8},{1,17},{9,25},{17,1},{25,9},{2,18},{10... | collective-permute-start | bytes 393224 | tf_op jit(solution)/shard_map/ppermute | solution.py:24
  57.6 1.5 %collective-permute-start.16 = (f32[256,128]{1,0:T(8,128)S(1)}, f32[256,128]{1,0:T(8,128)S(1)}, u32[]{:S(2)}, u32[]{:S(2)}) collective-permute-start(f32[256,128]{1,0:T(8,128)S(1)} %fusion.13.refs_0_), channel_id=1, source_target_pairs={{0,8},{8,0},{16,24},{24,16},{1,9},{9,1},{17,25},{25,17},{2,10},{10... | collective-permute-start | bytes 393224 | tf_op jit(solution)/shard_map/ppermute | solution.py:24
  59.0 1.2 %collective-permute-start.15 = (f32[256,128]{1,0:T(8,128)S(1)}, f32[256,128]{1,0:T(8,128)S(1)}, u32[]{:S(2)}, u32[]{:S(2)}) collective-permute-start(f32[256,128]{1,0:T(8,128)S(1)} %fusion.13.refs_0_), channel_id=1, source_target_pairs={{0,24},{8,16},{16,8},{24,0},{1,25},{9,17},{17,9},{25,1},{2,26},{10... | collective-permute-start | bytes 393224 | tf_op jit(solution)/shard_map/ppermute | solution.py:24
  60.2 0.5 multiply.20.refs_2_
  60.7 1.7 %collective-permute-done.17.refs_1_ = f32[256,128]{1,0:T(8,128)S(1)} collective-permute-done((f32[256,128]{1,0:T(8,128)S(1)}, f32[256,128]{1,0:T(8,128)S(1)}, u32[]{:S(2)}, u32[]{:S(2)}) %collective-permute-start.17) | collective-permute-done | bytes 131104 | tf_op jit(solution)/shard_map/ppermute | solution.py:24
  62.4 1.1 %collective-permute-done.16.refs_0_ = f32[256,128]{1,0:T(8,128)S(1)} collective-permute-done((f32[256,128]{1,0:T(8,128)S(1)}, f32[256,128]{1,0:T(8,128)S(1)}, u32[]{:S(2)}, u32[]{:S(2)}) %collective-permute-start.16) | collective-permute-done | bytes 131104 | tf_op jit(solution)/shard_map/ppermute | solution.py:24
  63.5 0.7 multiply.21.refs_1_
  64.2 1.4 %collective-permute-done.15.refs_0_ = f32[256,128]{1,0:T(8,128)S(1)} collective-permute-done((f32[256,128]{1,0:T(8,128)S(1)}, f32[256,128]{1,0:T(8,128)S(1)}, u32[]{:S(2)}, u32[]{:S(2)}) %collective-permute-start.15) | collective-permute-done | bytes 131104 | tf_op jit(solution)/shard_map/ppermute | solution.py:24
  65.6 0.3 multiply.23
  65.9 0.1 collective-permute-start.18
  66.0 0.3 multiply.22
  66.3 1.6 %collective-permute-done.18 = f32[1024,128]{1,0:T(8,128)S(1)} collective-permute-done((f32[1024,128]{1,0:T(8,128)S(1)}, f32[1024,128]{1,0:T(8,128)S(1)}, u32[]{:S(2)}, u32[]{:S(2)}) %collective-permute-start.18) | collective-permute-done | bytes 524320 | tf_op jit(solution)/shard_map/ppermute | solution.py:24
  67.9 0.1 collective-permute-start.19
  68.0 2.3 %collective-permute-start.21 = (f32[256,128]{1,0:T(8,128)S(1)}, f32[256,128]{1,0:T(8,128)S(1)}, u32[]{:S(2)}, u32[]{:S(2)}) collective-permute-start(f32[256,128]{1,0:T(8,128)S(1)} %get-tuple-element.22), channel_id=1, source_target_pairs={{0,6},{1,7},{2,4},{3,5},{4,2},{5,3},{6,0},{7,1},{8,14},{9,15},{10,... | collective-permute-start | bytes 393224 | tf_op jit(solution)/shard_map/ppermute | solution.py:24
  70.3 1.2 %collective-permute-start.20 = (f32[256,128]{1,0:T(8,128)S(1)}, f32[256,128]{1,0:T(8,128)S(1)}, u32[]{:S(2)}, u32[]{:S(2)}) collective-permute-start(f32[256,128]{1,0:T(8,128)S(1)} %get-tuple-element.23), channel_id=1, source_target_pairs={{0,4},{1,5},{2,6},{3,7},{4,0},{5,1},{6,2},{7,3},{8,12},{9,13},{10,... | collective-permute-start | bytes 393224 | tf_op jit(solution)/shard_map/ppermute | solution.py:24
  71.5 2.1 %collective-permute-done.19 = f32[256,128]{1,0:T(8,128)S(1)} collective-permute-done((f32[256,128]{1,0:T(8,128)S(1)}, f32[256,128]{1,0:T(8,128)S(1)}, u32[]{:S(2)}, u32[]{:S(2)}) %collective-permute-start.19) | collective-permute-done | bytes 131104 | tf_op jit(solution)/shard_map/ppermute | solution.py:24
  73.6 3.8 %collective-permute-done.21 = f32[256,128]{1,0:T(8,128)S(1)} collective-permute-done((f32[256,128]{1,0:T(8,128)S(1)}, f32[256,128]{1,0:T(8,128)S(1)}, u32[]{:S(2)}, u32[]{:S(2)}) %collective-permute-start.21) | collective-permute-done | bytes 131104 | tf_op jit(solution)/shard_map/ppermute | solution.py:24
  77.4 5.7 %collective-permute-done.20 = f32[256,128]{1,0:T(8,128)S(1)} collective-permute-done((f32[256,128]{1,0:T(8,128)S(1)}, f32[256,128]{1,0:T(8,128)S(1)}, u32[]{:S(2)}, u32[]{:S(2)}) %collective-permute-start.20) | collective-permute-done | bytes 131104 | tf_op jit(solution)/shard_map/ppermute | solution.py:24
  83.1 0.7 fusion.6
  (8 shorter events, 0.1 us)
Async XLA Ops:
  0.0 9.2 %copy-start = (f32[256,128]{1,0:T(8,128)S(1)}, f32[256,128]{1,0:T(8,128)}, u32[]{:S(2)}) copy-start(f32[256,128]{1,0:T(8,128)} %source_ref.1) | copy-start | bytes 393220
  0.0 9.6 %collective-permute-start.2 = (f32[256,128]{1,0:T(8,128)}, f32[256,128]{1,0:T(8,128)S(1)}, u32[]{:S(2)}, u32[]{:S(2)}) collective-permute-start(f32[256,128]{1,0:T(8,128)} %source_ref.1), channel_id=1, source_target_pairs={{0,16},{8,24},{16,0},{24,8},{1,17},{9,25},{17,1},{25,9},{2,18},{10... | collective-permute-start | bytes 393224 | tf_op jit(solution)/shard_map/ppermute | solution.py:24
  3.0 6.6 %collective-permute-start.1 = (f32[256,128]{1,0:T(8,128)}, f32[256,128]{1,0:T(8,128)S(1)}, u32[]{:S(2)}, u32[]{:S(2)}) collective-permute-start(f32[256,128]{1,0:T(8,128)} %source_ref.1), channel_id=1, source_target_pairs={{0,8},{8,0},{16,24},{24,16},{1,9},{9,1},{17,25},{25,17},{2,10},{10... | collective-permute-start | bytes 393224 | tf_op jit(solution)/shard_map/ppermute | solution.py:24
  4.5 6.3 %collective-permute-start = (f32[256,128]{1,0:T(8,128)}, f32[256,128]{1,0:T(8,128)S(1)}, u32[]{:S(2)}, u32[]{:S(2)}) collective-permute-start(f32[256,128]{1,0:T(8,128)} %source_ref.1), channel_id=1, source_target_pairs={{0,24},{8,16},{16,8},{24,0},{1,25},{9,17},{17,9},{25,1},{2,26},{10... | collective-permute-start | bytes 393224 | tf_op jit(solution)/shard_map/ppermute | solution.py:24
  11.1 2.0 %collective-permute-start.3 = (f32[1024,128]{1,0:T(8,128)S(1)}, f32[1024,128]{1,0:T(8,128)S(1)}, u32[]{:S(2)}, u32[]{:S(2)}) collective-permute-start(f32[1024,128]{1,0:T(8,128)S(1)} %multiply.15), channel_id=1, source_target_pairs={{0,1},{1,0},{2,3},{3,2},{4,5},{5,4},{6,7},{7,6},{8,9},{9,8},{10,11... | collective-permute-start | bytes 1572872 | tf_op jit(solution)/shard_map/ppermute | solution.py:24
  11.7 1.4 %collective-permute-start.4 = (f32[32,128]{1,0:T(8,128)S(1)}, f32[32,128]{1,0:T(8,128)S(1)}, u32[]{:S(2)}, u32[]{:S(2)}) collective-permute-start(f32[32,128]{1,0:T(8,128)S(1)} %slice.68), channel_id=1, source_target_pairs={{0,1},{1,0},{2,3},{3,2},{4,5},{5,4},{6,7},{7,6},{8,9},{9,8},{10,11... | collective-permute-start | bytes 49160 | tf_op jit(solution)/shard_map/ppermute | solution.py:24
  13.2 8.0 %collective-permute-start.5 = (f32[264,128]{1,0:T(8,128)S(1)}, f32[264,128]{1,0:T(8,128)S(1)}, u32[]{:S(2)}, u32[]{:S(2)}) collective-permute-start(f32[264,128]{1,0:T(8,128)S(1)} %get-tuple-element.16), channel_id=1, source_target_pairs={{0,2},{1,3},{2,0},{3,1},{4,6},{5,7},{6,4},{7,5},{8,10},{9,11},{10,... | collective-permute-start | bytes 405512 | tf_op jit(solution)/shard_map/ppermute | solution.py:24
  15.0 13.2 %collective-permute-start.6 = (f32[264,128]{1,0:T(8,128)S(1)}, f32[264,128]{1,0:T(8,128)S(1)}, u32[]{:S(2)}, u32[]{:S(2)}) collective-permute-start(f32[264,128]{1,0:T(8,128)S(1)} %get-tuple-element.17), channel_id=1, source_target_pairs={{0,4},{1,5},{2,6},{3,7},{4,0},{5,1},{6,2},{7,3},{8,12},{9,13},{10,... | collective-permute-start | bytes 405512 | tf_op jit(solution)/shard_map/ppermute | solution.py:24
  17.6 10.6 %collective-permute-start.7 = (f32[264,128]{1,0:T(8,128)S(1)}, f32[264,128]{1,0:T(8,128)S(1)}, u32[]{:S(2)}, u32[]{:S(2)}) collective-permute-start(f32[264,128]{1,0:T(8,128)S(1)} %get-tuple-element.18), channel_id=1, source_target_pairs={{0,6},{1,7},{2,4},{3,5},{4,2},{5,3},{6,0},{7,1},{8,14},{9,15},{10,... | collective-permute-start | bytes 405512 | tf_op jit(solution)/shard_map/ppermute | solution.py:24
  28.6 6.4 %collective-permute-start.10 = (f32[256,128]{1,0:T(8,128)S(1)}, f32[256,128]{1,0:T(8,128)S(1)}, u32[]{:S(2)}, u32[]{:S(2)}) collective-permute-start(f32[256,128]{1,0:T(8,128)S(1)} %get-tuple-element.19.refs_0_), channel_id=1, source_target_pairs={{0,16},{8,24},{16,0},{24,8},{1,17},{9,25},{17,1},{25,9},{2,18},{10... | collective-permute-start | bytes 393224 | tf_op jit(solution)/shard_map/ppermute | solution.py:24
  30.1 5.0 %collective-permute-start.9 = (f32[256,128]{1,0:T(8,128)S(1)}, f32[256,128]{1,0:T(8,128)S(1)}, u32[]{:S(2)}, u32[]{:S(2)}) collective-permute-start(f32[256,128]{1,0:T(8,128)S(1)} %get-tuple-element.19.refs_0_), channel_id=1, source_target_pairs={{0,8},{8,0},{16,24},{24,16},{1,9},{9,1},{17,25},{25,17},{2,10},{10... | collective-permute-start | bytes 393224 | tf_op jit(solution)/shard_map/ppermute | solution.py:24
  31.6 5.9 %collective-permute-start.8 = (f32[256,128]{1,0:T(8,128)S(1)}, f32[256,128]{1,0:T(8,128)S(1)}, u32[]{:S(2)}, u32[]{:S(2)}) collective-permute-start(f32[256,128]{1,0:T(8,128)S(1)} %get-tuple-element.19.refs_0_), channel_id=1, source_target_pairs={{0,24},{8,16},{16,8},{24,0},{1,25},{9,17},{17,9},{25,1},{2,26},{10... | collective-permute-start | bytes 393224 | tf_op jit(solution)/shard_map/ppermute | solution.py:24
  37.8 2.0 %collective-permute-start.11 = (f32[1024,128]{1,0:T(8,128)S(1)}, f32[1024,128]{1,0:T(8,128)S(1)}, u32[]{:S(2)}, u32[]{:S(2)}) collective-permute-start(f32[1024,128]{1,0:T(8,128)S(1)} %multiply.19), channel_id=1, source_target_pairs={{0,1},{1,0},{2,3},{3,2},{4,5},{5,4},{6,7},{7,6},{8,9},{9,8},{10,11... | collective-permute-start | bytes 1572872 | tf_op jit(solution)/shard_map/ppermute | solution.py:24
  39.9 6.8 %collective-permute-start.12 = (f32[256,128]{1,0:T(8,128)S(1)}, f32[256,128]{1,0:T(8,128)S(1)}, u32[]{:S(2)}, u32[]{:S(2)}) collective-permute-start(f32[256,128]{1,0:T(8,128)S(1)} %get-tuple-element.24), channel_id=1, source_target_pairs={{0,2},{1,3},{2,0},{3,1},{4,6},{5,7},{6,4},{7,5},{8,10},{9,11},{10,... | collective-permute-start | bytes 393224 | tf_op jit(solution)/shard_map/ppermute | solution.py:24
  42.8 9.7 %collective-permute-start.14 = (f32[256,128]{1,0:T(8,128)S(1)}, f32[256,128]{1,0:T(8,128)S(1)}, u32[]{:S(2)}, u32[]{:S(2)}) collective-permute-start(f32[256,128]{1,0:T(8,128)S(1)} %get-tuple-element.25), channel_id=1, source_target_pairs={{0,6},{1,7},{2,4},{3,5},{4,2},{5,3},{6,0},{7,1},{8,14},{9,15},{10,... | collective-permute-start | bytes 393224 | tf_op jit(solution)/shard_map/ppermute | solution.py:24
  45.3 11.3 %collective-permute-start.13 = (f32[256,128]{1,0:T(8,128)S(1)}, f32[256,128]{1,0:T(8,128)S(1)}, u32[]{:S(2)}, u32[]{:S(2)}) collective-permute-start(f32[256,128]{1,0:T(8,128)S(1)} %get-tuple-element.26), channel_id=1, source_target_pairs={{0,4},{1,5},{2,6},{3,7},{4,0},{5,1},{6,2},{7,3},{8,12},{9,13},{10,... | collective-permute-start | bytes 393224 | tf_op jit(solution)/shard_map/ppermute | solution.py:24
  56.6 5.7 %collective-permute-start.17 = (f32[256,128]{1,0:T(8,128)S(1)}, f32[256,128]{1,0:T(8,128)S(1)}, u32[]{:S(2)}, u32[]{:S(2)}) collective-permute-start(f32[256,128]{1,0:T(8,128)S(1)} %fusion.13.refs_0_), channel_id=1, source_target_pairs={{0,16},{8,24},{16,0},{24,8},{1,17},{9,25},{17,1},{25,9},{2,18},{10... | collective-permute-start | bytes 393224 | tf_op jit(solution)/shard_map/ppermute | solution.py:24
  57.6 5.9 %collective-permute-start.16 = (f32[256,128]{1,0:T(8,128)S(1)}, f32[256,128]{1,0:T(8,128)S(1)}, u32[]{:S(2)}, u32[]{:S(2)}) collective-permute-start(f32[256,128]{1,0:T(8,128)S(1)} %fusion.13.refs_0_), channel_id=1, source_target_pairs={{0,8},{8,0},{16,24},{24,16},{1,9},{9,1},{17,25},{25,17},{2,10},{10... | collective-permute-start | bytes 393224 | tf_op jit(solution)/shard_map/ppermute | solution.py:24
  59.0 6.5 %collective-permute-start.15 = (f32[256,128]{1,0:T(8,128)S(1)}, f32[256,128]{1,0:T(8,128)S(1)}, u32[]{:S(2)}, u32[]{:S(2)}) collective-permute-start(f32[256,128]{1,0:T(8,128)S(1)} %fusion.13.refs_0_), channel_id=1, source_target_pairs={{0,24},{8,16},{16,8},{24,0},{1,25},{9,17},{17,9},{25,1},{2,26},{10... | collective-permute-start | bytes 393224 | tf_op jit(solution)/shard_map/ppermute | solution.py:24
  65.9 2.0 %collective-permute-start.18 = (f32[1024,128]{1,0:T(8,128)S(1)}, f32[1024,128]{1,0:T(8,128)S(1)}, u32[]{:S(2)}, u32[]{:S(2)}) collective-permute-start(f32[1024,128]{1,0:T(8,128)S(1)} %multiply.23), channel_id=1, source_target_pairs={{0,1},{1,0},{2,3},{3,2},{4,5},{5,4},{6,7},{7,6},{8,9},{9,8},{10,11... | collective-permute-start | bytes 1572872 | tf_op jit(solution)/shard_map/ppermute | solution.py:24
  67.9 5.7 %collective-permute-start.19 = (f32[256,128]{1,0:T(8,128)S(1)}, f32[256,128]{1,0:T(8,128)S(1)}, u32[]{:S(2)}, u32[]{:S(2)}) collective-permute-start(f32[256,128]{1,0:T(8,128)S(1)} %get-tuple-element.21), channel_id=1, source_target_pairs={{0,2},{1,3},{2,0},{3,1},{4,6},{5,7},{6,4},{7,5},{8,10},{9,11},{10,... | collective-permute-start | bytes 393224 | tf_op jit(solution)/shard_map/ppermute | solution.py:24
  68.0 9.4 %collective-permute-start.21 = (f32[256,128]{1,0:T(8,128)S(1)}, f32[256,128]{1,0:T(8,128)S(1)}, u32[]{:S(2)}, u32[]{:S(2)}) collective-permute-start(f32[256,128]{1,0:T(8,128)S(1)} %get-tuple-element.22), channel_id=1, source_target_pairs={{0,6},{1,7},{2,4},{3,5},{4,2},{5,3},{6,0},{7,1},{8,14},{9,15},{10,... | collective-permute-start | bytes 393224 | tf_op jit(solution)/shard_map/ppermute | solution.py:24
  70.3 12.9 %collective-permute-start.20 = (f32[256,128]{1,0:T(8,128)S(1)}, f32[256,128]{1,0:T(8,128)S(1)}, u32[]{:S(2)}, u32[]{:S(2)}) collective-permute-start(f32[256,128]{1,0:T(8,128)S(1)} %get-tuple-element.23), channel_id=1, source_target_pairs={{0,4},{1,5},{2,6},{3,7},{4,0},{5,1},{6,2},{7,3},{8,12},{9,13},{10,... | collective-permute-start | bytes 393224 | tf_op jit(solution)/shard_map/ppermute | solution.py:24

commit v4 on v3

--- a/solution.py
+++ b/solution.py
@@ -24,12 +24,12 @@
     return lax.ppermute(array, axis, [(i, i ^ offset) for i in range(size)])
 
 
-def prepare_kernel(chunks, rows_ref, cols_ref, scale_ref, value_ref, out_ref, energy_ref, held, arrived):
+def prepare_kernel(chunks, order_ref, scale_ref, value_ref, out_ref, energy_ref, held, arrived):
     blocks, span, _ = held.shape
     parts = span // TILE
 
     def copy(i):
-        start = pl.multiple_of(rows_ref[i] * span, span)
+        start = pl.multiple_of(order_ref[i] * span, span)
         return pltpu.make_async_copy(value_ref.at[pl.ds(start, span)], held.at[i], arrived.at[i])
 
     for i in range(blocks):
@@ -40,11 +40,11 @@
         for half in range(parts):
             from_rows = slice(half * TILE, (half + 1) * TILE)
             to_rows = pl.ds(pl.multiple_of(i * span + half * TILE, TILE), TILE)
-            row_tile = rows_ref[i] * parts + half
+            row_tile = order_ref[i] * parts + half
             total = jnp.zeros((TILE, TILE), jnp.float32)
             for chunk in range(chunks):
                 for part in range(parts):
-                    tile = cols_ref[chunk] * parts + part
+                    tile = order_ref[blocks + chunk] * parts + part
                     scale = scale_ref[tile, row_tile].astype(jnp.float32) * 0.125
                     from_cols = pl.ds(pl.multiple_of(tile * TILE, TILE), TILE)
                     scaled = held[i, from_rows, from_cols].astype(jnp.float32) * scale
@@ -57,14 +57,14 @@
     lax.fori_loop(0, blocks, body, 0)
 
 
-def prepare(value, present, power, row_order, col_order, span):
+def prepare(value, present, power, order, span):
     row_count, col_count = value.shape
     blocks = row_count // span
     smem = pl.BlockSpec(memory_space=pltpu.SMEM)
     table = (present << (power + 3)).T
     return pl.pallas_call(
         functools.partial(prepare_kernel, col_count // span),
-        in_specs=[smem] * 3 + [pl.BlockSpec(memory_space=pltpu.HBM)],
+        in_specs=[smem] * 2 + [pl.BlockSpec(memory_space=pltpu.HBM)],
         out_specs=[VMEM, VMEM],
         out_shape=[
             jax.ShapeDtypeStruct(value.shape, jnp.bfloat16),
@@ -76,7 +76,7 @@
         ],
         compiler_params=params(48),
         name="prepare",
-    )(row_order, col_order, table, value)
+    )(order, table, value)
 
 
 def energy_kernel(span, total_ref, out_ref):
@@ -107,22 +107,24 @@
     )(total)
 
 
-def combine_kernel(groups, mine_ref, moved_ref, energy_ref, energy_moved_ref, *out_refs):
-    span = mine_ref.shape[0] // groups
-    for d in range(groups):
-        rows, small = slice(d * span, (d + 1) * span), slice(d * 8, (d + 1) * 8)
-        mine = slice((groups + d) * 8, (groups + d + 1) * 8)
-        out_refs[d][:span, :] = mine_ref[rows, :] + moved_ref[rows, :]
-        out_refs[d][span:, :] = energy_ref[mine, :] + energy_moved_ref[small, :]
-
-
-def combine(groups, mine, moved, energy, energy_moved):
-    shape = (mine.shape[0] // groups + 8, mine.shape[1])
-    return pl.pallas_call(
-        functools.partial(combine_kernel, groups),
-        out_shape=[jax.ShapeDtypeStruct(shape, jnp.float32)] * groups,
+def combine_kernel(first, groups, mine_ref, moved_ref, energy_ref, energy_moved_ref, *out_refs):
+    count = len(out_refs)
+    span = mine_ref.shape[0] // count
+    for i in range(count):
+        rows = slice(i * span, (i + 1) * span)
+        theirs = slice((first + i) * 8, (first + i + 1) * 8)
+        mine = slice((groups + first + i) * 8, (groups + first + i + 1) * 8)
+        out_refs[i][:span, :] = mine_ref[rows, :] + moved_ref[rows, :]
+        out_refs[i][span:, :] = energy_ref[mine, :] + energy_moved_ref[theirs, :]
+
+
+def combine(first, count, groups, mine, moved, energy, energy_moved):
+    shape = (mine.shape[0] // count + 8, mine.shape[1])
+    return pl.pallas_call(
+        functools.partial(combine_kernel, first, groups),
+        out_shape=[jax.ShapeDtypeStruct(shape, jnp.float32)] * count,
         in_specs=[VMEM] * 4,
-        out_specs=[VMEM] * groups,
+        out_specs=[VMEM] * count,
         compiler_params=params(4),
         name="combine",
     )(mine, moved, energy, energy_moved)
@@ -166,20 +168,25 @@
     )(*parts, source)
 
 
-def fence_kernel(source_ref, out_ref):
-    out_ref[...] = TELEPORT * source_ref[...]
-
-
-def fence(source):
-    return pl.pallas_call(
-        fence_kernel,
-        out_shape=jax.ShapeDtypeStruct(source.shape, jnp.float32),
-        in_specs=[VMEM],
-        out_specs=VMEM,
-        compiler_params=params(4),
+def order_kernel(offsets, chunks, out_ref):
+    row, col = lax.axis_index("row"), lax.axis_index("col")
+    blocks = 2 * len(offsets)
+    for side in range(2):
+        for i, offset in enumerate(offsets):
+            out_ref[side * len(offsets) + i] = col ^ (2 * offset + 1 - side)
+    for chunk in range(chunks):
+        out_ref[blocks + chunk] = row ^ chunk
+
+
+def order_of(offsets, chunks):
+    return pl.pallas_call(
+        functools.partial(order_kernel, offsets, chunks),
+        out_shape=jax.ShapeDtypeStruct((2 * len(offsets) + chunks,), jnp.int32),
+        out_specs=pl.BlockSpec(memory_space=pltpu.SMEM),
+        compiler_params=params(1),
         cost_estimate=pl.CostEstimate(flops=10**10, bytes_accessed=10**8, transcendentals=0),
-        name="fence",
-    )(source)
+        name="order",
+    )()
 
 
 def multiply_kernel(first_row, first, count, add, adjacency_ref, *refs):
@@ -227,47 +234,55 @@
     )(adjacency, *features, *([total] if add else []))
 
 
+def far_offsets(groups):
+    return [groups - 1] + list(range(1, groups - 1)) + [0] if groups > 1 else [0]
+
+
 def shards(source, value, occupancy, exponent):
     row_size, col_size = lax.axis_size("row"), lax.axis_size("col")
     span = source.shape[0]
     nodes = value.shape[0] * row_size
-    row, col = lax.axis_index("row"), lax.axis_index("col")
     groups = col_size // 2
     half = groups * span
-    offsets = jnp.arange(groups, dtype=jnp.int32) * 2
-    row_order = jnp.concatenate([(col ^ 1) ^ offsets, col ^ offsets])
-    col_order = row ^ jnp.arange(row_size, dtype=jnp.int32)
-
-    def spread(parts):
-        return [parts[0]] + [swap(parts[d], "col", col_size, 2 * d) for d in range(1, groups)]
-
+    offsets = far_offsets(groups)
+    cuts = [(0, 1), (1, groups - 1)] if groups > 1 else [(0, 1)]
+
+    order = order_of(offsets, row_size)
     current = source
     for step in range(STEPS):
         features = [current]
         for d in range(1, row_size):
             features.append(swap(current, "row", row_size, d))
         if step == 0:
-            teleport = fence(source)
-            adjacency, squares = prepare(value, occupancy, exponent, row_order, col_order, span)
+            adjacency, squares = prepare(value, occupancy, exponent, order, span)
             energy = energy_of(squares, span)
             energy_moved = swap(energy[: 8 * groups], "col", col_size, 1)
         first = multiply(adjacency, 0, 2 * half, 0, features[:1])
         if row_size > 2:
             first = multiply(adjacency, 0, 2 * half, 1, features[1:-1], first)
         last = features[-1:]
-        other = multiply(adjacency, 0, half, row_size - 1, last, first)
-        moved = swap(other, "col", col_size, 1)
-        mine = multiply(adjacency, half, half, row_size - 1, last, first)
+        moved = []
+        for start, count in cuts:
+            other = multiply(adjacency, start * span, count * span, row_size - 1, last, first)
+            moved.append(swap(other, "col", col_size, 1))
+        sums = []
+        for i, (start, count) in enumerate(cuts):
+            mine = multiply(adjacency, half + start * span, count * span, row_size - 1, last, first)
+            if step == 0:
+                sums += combine(start, count, groups, mine, moved[i], energy, energy_moved)
+            else:
+                for d in range(count):
+                    rows = slice(d * span, (d + 1) * span)
+                    sums.append(mine[rows] + moved[i][rows])
+        parts = [
+            swap(part, "col", col_size, 2 * offset) if offset else part
+            for offset, part in zip(offsets, sums)
+        ]
         if step == 0:
-            sums = combine(groups, mine, moved, energy, energy_moved)
-            current, inverse = finish(nodes, spread(sums), source)
+            current, inverse = finish(nodes, parts, source)
         else:
-            sums = [
-                mine[d * span : (d + 1) * span] + moved[d * span : (d + 1) * span]
-                for d in range(groups)
-            ]
-            product = functools.reduce(jnp.add, spread(sums))
-            current = jnp.tanh(RETAIN * (product * inverse) + teleport)
+            product = functools.reduce(jnp.add, parts)
+            current = jnp.tanh(RETAIN * (product * inverse) + TELEPORT * source)
     return current
 
 

time: 84 us -> 80.7 us (0.961)
  waiting for transfers between devices: 45.9 us -> 40.3 us
  Pallas kernels: 10.3 us -> 11.9 us
  starting transfers between devices: 25.8 us -> 27.1 us
    ppermute x22 -> x25, waiting for transfers between devices: 45.9 us -> 40.3 us  [swap(): return lax.ppermute(array, axis, [(i, i ^ offset) for i in range(size)])]
    ppermute x22 -> x25, starting transfers between devices: 25.8 us -> 27.1 us  [swap(): return lax.ppermute(array, axis, [(i, i ^ offset) for i in range(size)])]
    pallas_call x12 -> x18, Pallas kernels: 5.51 us -> 6.56 us  [multiply(): pl.pallas_call(functools.partial(multiply_kernel, first_row, first, count...]
  transfers between devices with their start and end apart: 22 -> 25, of which waited for: 18 -> 19; matrix products, arithmetic and copies ran while one was open for 1% -> 0% of each run, Pallas kernels for 11% -> 13%
where the time goes in v4:
time: 80.7 us; the launch traced here: 80.6 us
  waiting for transfers between devices  40.3 us (50%)
  starting transfers between devices  27.1 us (34%)
  Pallas kernels  11.9 us (15%)
  other arithmetic  0.89 us (1%)
    ppermute x25, waiting for transfers between devices, swap(): return lax.ppermute(array, axis, [(i, i ^ offset) for i in range(size)])  40.3 us
    ppermute x25, starting transfers between devices, swap(): return lax.ppermute(array, axis, [(i, i ^ offset) for i in range(size)])  27.1 us
    pallas_call x18, Pallas kernels, multiply(): pl.pallas_call(functools.partial(multiply_kernel, first_row, first, count...  6.56 us
    pallas_call x1, Pallas kernels, prepare(): pl.pallas_call(functools.partial(prepare_kernel, col_count // span), in_s...  3.84 us
  transfers between devices with their start and end apart: 25, of which 19 were waited for; matrix products, arithmetic and copies ran while one was open for 0% of the time, Pallas kernels for 13%

profile of v4, /device:TPU:0, one launch (start us, length us, event | category | flops | bytes accessed | tf_op | source)
XLA Modules:
  0.0 80.6 jit_solution(3723299191559217704)
XLA Ops:
  0.0 3.0 %collective-permute-start.2 = (f32[256,128]{1,0:T(8,128)}, f32[256,128]{1,0:T(8,128)S(1)}, u32[]{:S(2)}, u32[]{:S(2)}) collective-permute-start(f32[256,128]{1,0:T(8,128)} %refs_4_.1), channel_id=1, source_target_pairs={{0,16},{8,24},{16,0},{24,8},{1,17},{9,25},{17,1},{25,9},{2,18},{10... | collective-permute-start | bytes 393224 | tf_op jit(solution)/shard_map/ppermute | solution.py:24
  3.0 1.5 %collective-permute-start.1 = (f32[256,128]{1,0:T(8,128)}, f32[256,128]{1,0:T(8,128)S(1)}, u32[]{:S(2)}, u32[]{:S(2)}) collective-permute-start(f32[256,128]{1,0:T(8,128)} %refs_4_.1), channel_id=1, source_target_pairs={{0,8},{8,0},{16,24},{24,16},{1,9},{9,1},{17,25},{25,17},{2,10},{10... | collective-permute-start | bytes 393224 | tf_op jit(solution)/shard_map/ppermute | solution.py:24
  4.5 0.6 order.1.order_ref
  5.2 3.8 %prepare.1 = (bf16[2048,1024]{1,0:T(8,128)(2,1)S(1)}, f32[2048,128]{1,0:T(8,128)S(1)}) custom-call(s32[12]{0:T(128)S(1)} %order.1.order_ref, s32[8,16]{1,0:T(8,128)S(1)} %shift-left_bitcast_fusion.scale_ref, bf16[2048,1024]{1,0:T(8,128)(2,1)} %value_ref.1), custom_call_target="tpu_custom_call" | custom-call | tf_op jit(solution)/shard_map/prepare/pallas_call | solution.py:65
  9.0 0.5 multiply.18.refs_2_
  9.6 0.7 multiply.19.refs_1_
  10.3 0.4 collective-permute-done.refs_0_
  10.8 0.3 multiply.23
  11.1 0.1 collective-permute-start.6
  11.1 0.2 multiply.21
  11.4 0.6 collective-permute-start.3
  11.9 0.5 energy.1.energy_ref
  12.5 0.2 multiply.20.mine_ref
  12.7 0.3 multiply.22.mine_ref
  13.0 0.7 collective-permute-done.4.energy_moved_ref
  13.7 3.8 %collective-permute-start.5 = (f32[264,128]{1,0:T(8,128)S(1)}, f32[264,128]{1,0:T(8,128)S(1)}, u32[]{:S(2)}, u32[]{:S(2)}) collective-permute-start(f32[264,128]{1,0:T(8,128)S(1)} %combine.2), channel_id=1, source_target_pairs={{0,6},{1,7},{2,4},{3,5},{4,2},{5,3},{6,0},{7,1},{8,14},{9,15},{10,... | collective-permute-start | bytes 405512 | tf_op jit(solution)/shard_map/ppermute | solution.py:24
  17.6 0.1 collective-permute-start.7
  17.6 0.6 collective-permute-start.8
  18.2 3.8 %collective-permute-done.5.refs_0_ = f32[264,128]{1,0:T(8,128)S(1)} collective-permute-done((f32[264,128]{1,0:T(8,128)S(1)}, f32[264,128]{1,0:T(8,128)S(1)}, u32[]{:S(2)}, u32[]{:S(2)}) %collective-permute-start.5) | collective-permute-done | bytes 135200 | tf_op jit(solution)/shard_map/ppermute | solution.py:24
  22.1 3.4 %collective-permute-done.7.refs_1_ = f32[264,128]{1,0:T(8,128)S(1)} collective-permute-done((f32[264,128]{1,0:T(8,128)S(1)}, f32[264,128]{1,0:T(8,128)S(1)}, u32[]{:S(2)}, u32[]{:S(2)}) %collective-permute-start.7) | collective-permute-done | bytes 135200 | tf_op jit(solution)/shard_map/ppermute | solution.py:24
  25.4 3.9 %collective-permute-done.8.refs_2_ = f32[264,128]{1,0:T(8,128)S(1)} collective-permute-done((f32[264,128]{1,0:T(8,128)S(1)}, f32[264,128]{1,0:T(8,128)S(1)}, u32[]{:S(2)}, u32[]{:S(2)}) %collective-permute-start.8) | collective-permute-done | bytes 135200 | tf_op jit(solution)/shard_map/ppermute | solution.py:24
  29.3 0.4 finish.1
  29.7 1.6 %collective-permute-start.11 = (f32[256,128]{1,0:T(8,128)S(1)}, f32[256,128]{1,0:T(8,128)S(1)}, u32[]{:S(2)}, u32[]{:S(2)}) collective-permute-start(f32[256,128]{1,0:T(8,128)S(1)} %get-tuple-element.17.refs_0_), channel_id=1, source_target_pairs={{0,16},{8,24},{16,0},{24,8},{1,17},{9,25},{17,1},{25,9},{2,18},{10... | collective-permute-start | bytes 393224 | tf_op jit(solution)/shard_map/ppermute | solution.py:24
  31.2 1.5 %collective-permute-start.10 = (f32[256,128]{1,0:T(8,128)S(1)}, f32[256,128]{1,0:T(8,128)S(1)}, u32[]{:S(2)}, u32[]{:S(2)}) collective-permute-start(f32[256,128]{1,0:T(8,128)S(1)} %get-tuple-element.17.refs_0_), channel_id=1, source_target_pairs={{0,8},{8,0},{16,24},{24,16},{1,9},{9,1},{17,25},{25,17},{2,10},{10... | collective-permute-start | bytes 393224 | tf_op jit(solution)/shard_map/ppermute | solution.py:24
  32.7 0.5 collective-permute-start.9
  33.2 0.5 multiply.24.refs_2_
  33.7 1.0 %collective-permute-done.11.refs_1_ = f32[256,128]{1,0:T(8,128)S(1)} collective-permute-done((f32[256,128]{1,0:T(8,128)S(1)}, f32[256,128]{1,0:T(8,128)S(1)}, u32[]{:S(2)}, u32[]{:S(2)}) %collective-permute-start.11) | collective-permute-done | bytes 131104 | tf_op jit(solution)/shard_map/ppermute | solution.py:24
  34.7 2.4 %collective-permute-done.10.refs_0_ = f32[256,128]{1,0:T(8,128)S(1)} collective-permute-done((f32[256,128]{1,0:T(8,128)S(1)}, f32[256,128]{1,0:T(8,128)S(1)}, u32[]{:S(2)}, u32[]{:S(2)}) %collective-permute-start.10) | collective-permute-done | bytes 131104 | tf_op jit(solution)/shard_map/ppermute | solution.py:24
  37.1 0.7 multiply.25.refs_1_
  37.8 1.1 %collective-permute-done.9.refs_0_ = f32[256,128]{1,0:T(8,128)S(1)} collective-permute-done((f32[256,128]{1,0:T(8,128)S(1)}, f32[256,128]{1,0:T(8,128)S(1)}, u32[]{:S(2)}, u32[]{:S(2)}) %collective-permute-start.9) | collective-permute-done | bytes 131104 | tf_op jit(solution)/shard_map/ppermute | solution.py:24
  39.0 0.3 multiply.29
  39.3 0.1 collective-permute-start.14
  39.3 0.2 multiply.27
  39.5 0.6 collective-permute-start.12
  40.1 0.2 multiply.26
  40.3 0.3 multiply.28
  40.6 0.6 collective-permute-done.12
  41.2 2.5 %collective-permute-start.13 = (f32[256,128]{1,0:T(8,128)S(1)}, f32[256,128]{1,0:T(8,128)S(1)}, u32[]{:S(2)}, u32[]{:S(2)}) collective-permute-start(f32[256,128]{1,0:T(8,128)S(1)} %add.56), channel_id=1, source_target_pairs={{0,6},{1,7},{2,4},{3,5},{4,2},{5,3},{6,0},{7,1},{8,14},{9,15},{10,... | collective-permute-start | bytes 393224 | tf_op jit(solution)/shard_map/ppermute | solution.py:24
  43.8 0.1 collective-permute-start.15
  43.9 1.9 %collective-permute-start.16 = (f32[256,128]{1,0:T(8,128)S(1)}, f32[256,128]{1,0:T(8,128)S(1)}, u32[]{:S(2)}, u32[]{:S(2)}) collective-permute-start(f32[256,128]{1,0:T(8,128)S(1)} %get-tuple-element.22), channel_id=1, source_target_pairs={{0,4},{1,5},{2,6},{3,7},{4,0},{5,1},{6,2},{7,3},{8,12},{9,13},{10,... | collective-permute-start | bytes 393224 | tf_op jit(solution)/shard_map/ppermute | solution.py:24
  45.8 3.7 %collective-permute-done.13 = f32[256,128]{1,0:T(8,128)S(1)} collective-permute-done((f32[256,128]{1,0:T(8,128)S(1)}, f32[256,128]{1,0:T(8,128)S(1)}, u32[]{:S(2)}, u32[]{:S(2)}) %collective-permute-start.13) | collective-permute-done | bytes 131104 | tf_op jit(solution)/shard_map/ppermute | solution.py:24
  49.5 4.8 %collective-permute-done.15 = f32[256,128]{1,0:T(8,128)S(1)} collective-permute-done((f32[256,128]{1,0:T(8,128)S(1)}, f32[256,128]{1,0:T(8,128)S(1)}, u32[]{:S(2)}, u32[]{:S(2)}) %collective-permute-start.15) | collective-permute-done | bytes 131104 | tf_op jit(solution)/shard_map/ppermute | solution.py:24
  54.4 1.0 %collective-permute-start.19 = (f32[256,128]{1,0:T(8,128)S(1)}, f32[256,128]{1,0:T(8,128)S(1)}, u32[]{:S(2)}, u32[]{:S(2)}) collective-permute-start(f32[256,128]{1,0:T(8,128)S(1)} %fusion.9.refs_0_), channel_id=1, source_target_pairs={{0,16},{8,24},{16,0},{24,8},{1,17},{9,25},{17,1},{25,9},{2,18},{10... | collective-permute-start | bytes 393224 | tf_op jit(solution)/shard_map/ppermute | solution.py:24
  55.5 1.5 %collective-permute-start.18 = (f32[256,128]{1,0:T(8,128)S(1)}, f32[256,128]{1,0:T(8,128)S(1)}, u32[]{:S(2)}, u32[]{:S(2)}) collective-permute-start(f32[256,128]{1,0:T(8,128)S(1)} %fusion.9.refs_0_), channel_id=1, source_target_pairs={{0,8},{8,0},{16,24},{24,16},{1,9},{9,1},{17,25},{25,17},{2,10},{10... | collective-permute-start | bytes 393224 | tf_op jit(solution)/shard_map/ppermute | solution.py:24
  57.0 1.0 %collective-permute-start.17 = (f32[256,128]{1,0:T(8,128)S(1)}, f32[256,128]{1,0:T(8,128)S(1)}, u32[]{:S(2)}, u32[]{:S(2)}) collective-permute-start(f32[256,128]{1,0:T(8,128)S(1)} %fusion.9.refs_0_), channel_id=1, source_target_pairs={{0,24},{8,16},{16,8},{24,0},{1,25},{9,17},{17,9},{25,1},{2,26},{10... | collective-permute-start | bytes 393224 | tf_op jit(solution)/shard_map/ppermute | solution.py:24
  58.0 0.5 multiply.30.refs_2_
  58.5 1.5 %collective-permute-done.19.refs_1_ = f32[256,128]{1,0:T(8,128)S(1)} collective-permute-done((f32[256,128]{1,0:T(8,128)S(1)}, f32[256,128]{1,0:T(8,128)S(1)}, u32[]{:S(2)}, u32[]{:S(2)}) %collective-permute-start.19) | collective-permute-done | bytes 131104 | tf_op jit(solution)/shard_map/ppermute | solution.py:24
  59.9 1.9 %collective-permute-done.18.refs_0_ = f32[256,128]{1,0:T(8,128)S(1)} collective-permute-done((f32[256,128]{1,0:T(8,128)S(1)}, f32[256,128]{1,0:T(8,128)S(1)}, u32[]{:S(2)}, u32[]{:S(2)}) %collective-permute-start.18) | collective-permute-done | bytes 131104 | tf_op jit(solution)/shard_map/ppermute | solution.py:24
  61.8 0.7 multiply.31.refs_1_
  62.6 1.3 %collective-permute-done.17.refs_0_ = f32[256,128]{1,0:T(8,128)S(1)} collective-permute-done((f32[256,128]{1,0:T(8,128)S(1)}, f32[256,128]{1,0:T(8,128)S(1)}, u32[]{:S(2)}, u32[]{:S(2)}) %collective-permute-start.17) | collective-permute-done | bytes 131104 | tf_op jit(solution)/shard_map/ppermute | solution.py:24
  63.9 0.3 multiply.35
  64.2 0.1 collective-permute-start.22
  64.3 0.2 multiply.33
  64.5 0.6 collective-permute-start.20
  65.1 0.2 multiply.32
  65.3 0.3 multiply.34
  65.6 0.6 collective-permute-done.20
  66.2 1.5 %collective-permute-start.21 = (f32[256,128]{1,0:T(8,128)S(1)}, f32[256,128]{1,0:T(8,128)S(1)}, u32[]{:S(2)}, u32[]{:S(2)}) collective-permute-start(f32[256,128]{1,0:T(8,128)S(1)} %add.64), channel_id=1, source_target_pairs={{0,6},{1,7},{2,4},{3,5},{4,2},{5,3},{6,0},{7,1},{8,14},{9,15},{10,... | collective-permute-start | bytes 393224 | tf_op jit(solution)/shard_map/ppermute | solution.py:24
  67.8 0.3 collective-permute-start.23
  68.1 2.6 %collective-permute-start.24 = (f32[256,128]{1,0:T(8,128)S(1)}, f32[256,128]{1,0:T(8,128)S(1)}, u32[]{:S(2)}, u32[]{:S(2)}) collective-permute-start(f32[256,128]{1,0:T(8,128)S(1)} %get-tuple-element.20), channel_id=1, source_target_pairs={{0,4},{1,5},{2,6},{3,7},{4,0},{5,1},{6,2},{7,3},{8,12},{9,13},{10,... | collective-permute-start | bytes 393224 | tf_op jit(solution)/shard_map/ppermute | solution.py:24
  70.8 3.7 %collective-permute-done.21 = f32[256,128]{1,0:T(8,128)S(1)} collective-permute-done((f32[256,128]{1,0:T(8,128)S(1)}, f32[256,128]{1,0:T(8,128)S(1)}, u32[]{:S(2)}, u32[]{:S(2)}) %collective-permute-start.21) | collective-permute-done | bytes 131104 | tf_op jit(solution)/shard_map/ppermute | solution.py:24
  74.5 3.9 %collective-permute-done.23 = f32[256,128]{1,0:T(8,128)S(1)} collective-permute-done((f32[256,128]{1,0:T(8,128)S(1)}, f32[256,128]{1,0:T(8,128)S(1)}, u32[]{:S(2)}, u32[]{:S(2)}) %collective-permute-start.23) | collective-permute-done | bytes 131104 | tf_op jit(solution)/shard_map/ppermute | solution.py:24
  78.4 1.5 %collective-permute-done.24 = f32[256,128]{1,0:T(8,128)S(1)} collective-permute-done((f32[256,128]{1,0:T(8,128)S(1)}, f32[256,128]{1,0:T(8,128)S(1)}, u32[]{:S(2)}, u32[]{:S(2)}) %collective-permute-start.24) | collective-permute-done | bytes 131104 | tf_op jit(solution)/shard_map/ppermute | solution.py:24
  79.9 0.7 fusion.4
  (24 shorter events, 0.4 us)
Async XLA Ops:
  0.0 5.1 %copy-start.2 = (s32[16,8]{0,1:T(8,128)S(1)}, s32[16,8]{0,1:T(8,128)}, u32[]{:S(2)}) copy-start(s32[16,8]{0,1:T(8,128)} %param.7) | copy-start | bytes 1540
  0.0 5.1 %copy-start.1 = (s32[16,8]{0,1:T(8,128)S(1)}, s32[16,8]{0,1:T(8,128)}, u32[]{:S(2)}) copy-start(s32[16,8]{0,1:T(8,128)} %param.6) | copy-start | bytes 1540
  0.0 9.5 %collective-permute-start.2 = (f32[256,128]{1,0:T(8,128)}, f32[256,128]{1,0:T(8,128)S(1)}, u32[]{:S(2)}, u32[]{:S(2)}) collective-permute-start(f32[256,128]{1,0:T(8,128)} %refs_4_.1), channel_id=1, source_target_pairs={{0,16},{8,24},{16,0},{24,8},{1,17},{9,25},{17,1},{25,9},{2,18},{10... | collective-permute-start | bytes 393224 | tf_op jit(solution)/shard_map/ppermute | solution.py:24
  3.0 6.6 %collective-permute-start.1 = (f32[256,128]{1,0:T(8,128)}, f32[256,128]{1,0:T(8,128)S(1)}, u32[]{:S(2)}, u32[]{:S(2)}) collective-permute-start(f32[256,128]{1,0:T(8,128)} %refs_4_.1), channel_id=1, source_target_pairs={{0,8},{8,0},{16,24},{24,16},{1,9},{9,1},{17,25},{25,17},{2,10},{10... | collective-permute-start | bytes 393224 | tf_op jit(solution)/shard_map/ppermute | solution.py:24
  4.5 6.3 %collective-permute-start = (f32[256,128]{1,0:T(8,128)}, f32[256,128]{1,0:T(8,128)S(1)}, u32[]{:S(2)}, u32[]{:S(2)}) collective-permute-start(f32[256,128]{1,0:T(8,128)} %refs_4_.1), channel_id=1, source_target_pairs={{0,24},{8,16},{16,8},{24,0},{1,25},{9,17},{17,9},{25,1},{2,26},{10... | collective-permute-start | bytes 393224 | tf_op jit(solution)/shard_map/ppermute | solution.py:24
  5.2 3.9 %copy-start = (f32[256,128]{1,0:T(8,128)S(1)}, f32[256,128]{1,0:T(8,128)}, u32[]{:S(2)}) copy-start(f32[256,128]{1,0:T(8,128)} %refs_4_.1) | copy-start | bytes 393220
  11.1 6.4 %collective-permute-start.6 = (f32[768,128]{1,0:T(8,128)S(1)}, f32[768,128]{1,0:T(8,128)S(1)}, u32[]{:S(2)}, u32[]{:S(2)}) collective-permute-start(f32[768,128]{1,0:T(8,128)S(1)} %multiply.23), channel_id=1, source_target_pairs={{0,1},{1,0},{2,3},{3,2},{4,5},{5,4},{6,7},{7,6},{8,9},{9,8},{10,11... | collective-permute-start | bytes 1179656 | tf_op jit(solution)/shard_map/ppermute | solution.py:24
  11.4 2.3 %collective-permute-start.3 = (f32[256,128]{1,0:T(8,128)S(1)}, f32[256,128]{1,0:T(8,128)S(1)}, u32[]{:S(2)}, u32[]{:S(2)}) collective-permute-start(f32[256,128]{1,0:T(8,128)S(1)} %multiply.21), channel_id=1, source_target_pairs={{0,1},{1,0},{2,3},{3,2},{4,5},{5,4},{6,7},{7,6},{8,9},{9,8},{10,11... | collective-permute-start | bytes 393224 | tf_op jit(solution)/shard_map/ppermute | solution.py:24
  12.4 1.2 %collective-permute-start.4 = (f32[32,128]{1,0:T(8,128)S(1)}, f32[32,128]{1,0:T(8,128)S(1)}, u32[]{:S(2)}, u32[]{:S(2)}) collective-permute-start(f32[32,128]{1,0:T(8,128)S(1)} %slice.52), channel_id=1, source_target_pairs={{0,1},{1,0},{2,3},{3,2},{4,5},{5,4},{6,7},{7,6},{8,9},{9,8},{10,11... | collective-permute-start | bytes 49160 | tf_op jit(solution)/shard_map/ppermute | solution.py:24
  13.7 8.4 %collective-permute-start.5 = (f32[264,128]{1,0:T(8,128)S(1)}, f32[264,128]{1,0:T(8,128)S(1)}, u32[]{:S(2)}, u32[]{:S(2)}) collective-permute-start(f32[264,128]{1,0:T(8,128)S(1)} %combine.2), channel_id=1, source_target_pairs={{0,6},{1,7},{2,4},{3,5},{4,2},{5,3},{6,0},{7,1},{8,14},{9,15},{10,... | collective-permute-start | bytes 405512 | tf_op jit(solution)/shard_map/ppermute | solution.py:24
  17.6 7.9 %collective-permute-start.7 = (f32[264,128]{1,0:T(8,128)S(1)}, f32[264,128]{1,0:T(8,128)S(1)}, u32[]{:S(2)}, u32[]{:S(2)}) collective-permute-start(f32[264,128]{1,0:T(8,128)S(1)} %get-tuple-element.14), channel_id=1, source_target_pairs={{0,2},{1,3},{2,0},{3,1},{4,6},{5,7},{6,4},{7,5},{8,10},{9,11},{10,... | collective-permute-start | bytes 405512 | tf_op jit(solution)/shard_map/ppermute | solution.py:24
  17.6 11.6 %collective-permute-start.8 = (f32[264,128]{1,0:T(8,128)S(1)}, f32[264,128]{1,0:T(8,128)S(1)}, u32[]{:S(2)}, u32[]{:S(2)}) collective-permute-start(f32[264,128]{1,0:T(8,128)S(1)} %get-tuple-element.15), channel_id=1, source_target_pairs={{0,4},{1,5},{2,6},{3,7},{4,0},{5,1},{6,2},{7,3},{8,12},{9,13},{10,... | collective-permute-start | bytes 405512 | tf_op jit(solution)/shard_map/ppermute | solution.py:24
  29.7 5.0 %collective-permute-start.11 = (f32[256,128]{1,0:T(8,128)S(1)}, f32[256,128]{1,0:T(8,128)S(1)}, u32[]{:S(2)}, u32[]{:S(2)}) collective-permute-start(f32[256,128]{1,0:T(8,128)S(1)} %get-tuple-element.17.refs_0_), channel_id=1, source_target_pairs={{0,16},{8,24},{16,0},{24,8},{1,17},{9,25},{17,1},{25,9},{2,18},{10... | collective-permute-start | bytes 393224 | tf_op jit(solution)/shard_map/ppermute | solution.py:24
  31.2 5.8 %collective-permute-start.10 = (f32[256,128]{1,0:T(8,128)S(1)}, f32[256,128]{1,0:T(8,128)S(1)}, u32[]{:S(2)}, u32[]{:S(2)}) collective-permute-start(f32[256,128]{1,0:T(8,128)S(1)} %get-tuple-element.17.refs_0_), channel_id=1, source_target_pairs={{0,8},{8,0},{16,24},{24,16},{1,9},{9,1},{17,25},{25,17},{2,10},{10... | collective-permute-start | bytes 393224 | tf_op jit(solution)/shard_map/ppermute | solution.py:24
  32.7 6.2 %collective-permute-start.9 = (f32[256,128]{1,0:T(8,128)S(1)}, f32[256,128]{1,0:T(8,128)S(1)}, u32[]{:S(2)}, u32[]{:S(2)}) collective-permute-start(f32[256,128]{1,0:T(8,128)S(1)} %get-tuple-element.17.refs_0_), channel_id=1, source_target_pairs={{0,24},{8,16},{16,8},{24,0},{1,25},{9,17},{17,9},{25,1},{2,26},{10... | collective-permute-start | bytes 393224 | tf_op jit(solution)/shard_map/ppermute | solution.py:24
  39.3 4.5 %collective-permute-start.14 = (f32[768,128]{1,0:T(8,128)S(1)}, f32[768,128]{1,0:T(8,128)S(1)}, u32[]{:S(2)}, u32[]{:S(2)}) collective-permute-start(f32[768,128]{1,0:T(8,128)S(1)} %multiply.29), channel_id=1, source_target_pairs={{0,1},{1,0},{2,3},{3,2},{4,5},{5,4},{6,7},{7,6},{8,9},{9,8},{10,11... | collective-permute-start | bytes 1179656 | tf_op jit(solution)/shard_map/ppermute | solution.py:24
  39.5 1.7 %collective-permute-start.12 = (f32[256,128]{1,0:T(8,128)S(1)}, f32[256,128]{1,0:T(8,128)S(1)}, u32[]{:S(2)}, u32[]{:S(2)}) collective-permute-start(f32[256,128]{1,0:T(8,128)S(1)} %multiply.27), channel_id=1, source_target_pairs={{0,1},{1,0},{2,3},{3,2},{4,5},{5,4},{6,7},{7,6},{8,9},{9,8},{10,11... | collective-permute-start | bytes 393224 | tf_op jit(solution)/shard_map/ppermute | solution.py:24
  41.2 8.3 %collective-permute-start.13 = (f32[256,128]{1,0:T(8,128)S(1)}, f32[256,128]{1,0:T(8,128)S(1)}, u32[]{:S(2)}, u32[]{:S(2)}) collective-permute-start(f32[256,128]{1,0:T(8,128)S(1)} %add.56), channel_id=1, source_target_pairs={{0,6},{1,7},{2,4},{3,5},{4,2},{5,3},{6,0},{7,1},{8,14},{9,15},{10,... | collective-permute-start | bytes 393224 | tf_op jit(solution)/shard_map/ppermute | solution.py:24
  43.8 10.5 %collective-permute-start.15 = (f32[256,128]{1,0:T(8,128)S(1)}, f32[256,128]{1,0:T(8,128)S(1)}, u32[]{:S(2)}, u32[]{:S(2)}) collective-permute-start(f32[256,128]{1,0:T(8,128)S(1)} %get-tuple-element.21), channel_id=1, source_target_pairs={{0,2},{1,3},{2,0},{3,1},{4,6},{5,7},{6,4},{7,5},{8,10},{9,11},{10,... | collective-permute-start | bytes 393224 | tf_op jit(solution)/shard_map/ppermute | solution.py:24
  43.9 10.5 %collective-permute-start.16 = (f32[256,128]{1,0:T(8,128)S(1)}, f32[256,128]{1,0:T(8,128)S(1)}, u32[]{:S(2)}, u32[]{:S(2)}) collective-permute-start(f32[256,128]{1,0:T(8,128)S(1)} %get-tuple-element.22), channel_id=1, source_target_pairs={{0,4},{1,5},{2,6},{3,7},{4,0},{5,1},{6,2},{7,3},{8,12},{9,13},{10,... | collective-permute-start | bytes 393224 | tf_op jit(solution)/shard_map/ppermute | solution.py:24
  54.4 5.5 %collective-permute-start.19 = (f32[256,128]{1,0:T(8,128)S(1)}, f32[256,128]{1,0:T(8,128)S(1)}, u32[]{:S(2)}, u32[]{:S(2)}) collective-permute-start(f32[256,128]{1,0:T(8,128)S(1)} %fusion.9.refs_0_), channel_id=1, source_target_pairs={{0,16},{8,24},{16,0},{24,8},{1,17},{9,25},{17,1},{25,9},{2,18},{10... | collective-permute-start | bytes 393224 | tf_op jit(solution)/shard_map/ppermute | solution.py:24
  55.5 6.4 %collective-permute-start.18 = (f32[256,128]{1,0:T(8,128)S(1)}, f32[256,128]{1,0:T(8,128)S(1)}, u32[]{:S(2)}, u32[]{:S(2)}) collective-permute-start(f32[256,128]{1,0:T(8,128)S(1)} %fusion.9.refs_0_), channel_id=1, source_target_pairs={{0,8},{8,0},{16,24},{24,16},{1,9},{9,1},{17,25},{25,17},{2,10},{10... | collective-permute-start | bytes 393224 | tf_op jit(solution)/shard_map/ppermute | solution.py:24
  57.0 6.9 %collective-permute-start.17 = (f32[256,128]{1,0:T(8,128)S(1)}, f32[256,128]{1,0:T(8,128)S(1)}, u32[]{:S(2)}, u32[]{:S(2)}) collective-permute-start(f32[256,128]{1,0:T(8,128)S(1)} %fusion.9.refs_0_), channel_id=1, source_target_pairs={{0,24},{8,16},{16,8},{24,0},{1,25},{9,17},{17,9},{25,1},{2,26},{10... | collective-permute-start | bytes 393224 | tf_op jit(solution)/shard_map/ppermute | solution.py:24
  64.2 3.5 %collective-permute-start.22 = (f32[768,128]{1,0:T(8,128)S(1)}, f32[768,128]{1,0:T(8,128)S(1)}, u32[]{:S(2)}, u32[]{:S(2)}) collective-permute-start(f32[768,128]{1,0:T(8,128)S(1)} %multiply.35), channel_id=1, source_target_pairs={{0,1},{1,0},{2,3},{3,2},{4,5},{5,4},{6,7},{7,6},{8,9},{9,8},{10,11... | collective-permute-start | bytes 1179656 | tf_op jit(solution)/shard_map/ppermute | solution.py:24
  64.5 1.7 %collective-permute-start.20 = (f32[256,128]{1,0:T(8,128)S(1)}, f32[256,128]{1,0:T(8,128)S(1)}, u32[]{:S(2)}, u32[]{:S(2)}) collective-permute-start(f32[256,128]{1,0:T(8,128)S(1)} %multiply.33), channel_id=1, source_target_pairs={{0,1},{1,0},{2,3},{3,2},{4,5},{5,4},{6,7},{7,6},{8,9},{9,8},{10,11... | collective-permute-start | bytes 393224 | tf_op jit(solution)/shard_map/ppermute | solution.py:24
  66.2 8.3 %collective-permute-start.21 = (f32[256,128]{1,0:T(8,128)S(1)}, f32[256,128]{1,0:T(8,128)S(1)}, u32[]{:S(2)}, u32[]{:S(2)}) collective-permute-start(f32[256,128]{1,0:T(8,128)S(1)} %add.64), channel_id=1, source_target_pairs={{0,6},{1,7},{2,4},{3,5},{4,2},{5,3},{6,0},{7,1},{8,14},{9,15},{10,... | collective-permute-start | bytes 393224 | tf_op jit(solution)/shard_map/ppermute | solution.py:24
  67.8 10.6 %collective-permute-start.23 = (f32[256,128]{1,0:T(8,128)S(1)}, f32[256,128]{1,0:T(8,128)S(1)}, u32[]{:S(2)}, u32[]{:S(2)}) collective-permute-start(f32[256,128]{1,0:T(8,128)S(1)} %get-tuple-element.19), channel_id=1, source_target_pairs={{0,2},{1,3},{2,0},{3,1},{4,6},{5,7},{6,4},{7,5},{8,10},{9,11},{10,... | collective-permute-start | bytes 393224 | tf_op jit(solution)/shard_map/ppermute | solution.py:24
  68.1 11.8 %collective-permute-start.24 = (f32[256,128]{1,0:T(8,128)S(1)}, f32[256,128]{1,0:T(8,128)S(1)}, u32[]{:S(2)}, u32[]{:S(2)}) collective-permute-start(f32[256,128]{1,0:T(8,128)S(1)} %get-tuple-element.20), channel_id=1, source_target_pairs={{0,4},{1,5},{2,6},{3,7},{4,0},{5,1},{6,2},{7,3},{8,12},{9,13},{10,... | collective-permute-start | bytes 393224 | tf_op jit(solution)/shard_map/ppermute | solution.py:24

commit v5 on v4

--- a/solution.py
+++ b/solution.py
@@ -24,47 +24,56 @@
     return lax.ppermute(array, axis, [(i, i ^ offset) for i in range(size)])
 
 
-def prepare_kernel(chunks, order_ref, scale_ref, value_ref, out_ref, energy_ref, held, arrived):
+def prepare_kernel(offsets, chunks, fence_ref, present_ref, power_ref, value_ref, out_ref, energy_ref, held, scales, arrived):
     blocks, span, _ = held.shape
     parts = span // TILE
-
-    def copy(i):
-        start = pl.multiple_of(order_ref[i] * span, span)
-        return pltpu.make_async_copy(value_ref.at[pl.ds(start, span)], held.at[i], arrived.at[i])
+    row, col = lax.axis_index("row"), lax.axis_index("col")
+    sources = [col ^ (2 * offset + 1 - side) for side in range(2) for offset in offsets]
+
+    def copy(i, chunk):
+        rows = pl.ds(pl.multiple_of(sources[i] * span, span), span)
+        cols = pl.ds(pl.multiple_of((row ^ chunk) * span, span), span)
+        target = held.at[i, :, pl.ds(chunk * span, span)]
+        return pltpu.make_async_copy(value_ref.at[rows, cols], target, arrived.at[i, chunk])
 
     for i in range(blocks):
-        copy(i).start()
-
-    def body(i, carry):
-        copy(i).wait()
+        for chunk in range(chunks):
+            copy(i, chunk).start()
+    table = (present_ref[...] << (power_ref[...] + 3)).astype(jnp.float32) * 0.125
+    shape = (table.shape[0], scales.shape[1])
+    owner = lax.broadcasted_iota(jnp.int32, shape, 1) // TILE
+    spread = owner == lax.broadcasted_iota(jnp.int32, shape, 0)
+    scales[...] = lax.dot_general(
+        table.astype(jnp.bfloat16),
+        spread.astype(jnp.bfloat16),
+        (((0,), (0,)), ((), ())),
+        preferred_element_type=jnp.float32,
+    )
+    for i in range(blocks):
+        for chunk in range(chunks):
+            copy(i, chunk).wait()
         for half in range(parts):
             from_rows = slice(half * TILE, (half + 1) * TILE)
-            to_rows = pl.ds(pl.multiple_of(i * span + half * TILE, TILE), TILE)
-            row_tile = order_ref[i] * parts + half
+            to_rows = slice(i * span + half * TILE, i * span + (half + 1) * TILE)
+            row_tile = pl.ds(sources[i] * parts + half, 1)
             total = jnp.zeros((TILE, TILE), jnp.float32)
             for chunk in range(chunks):
+                cols = slice(chunk * span, (chunk + 1) * span)
+                from_cols = pl.ds(pl.multiple_of((row ^ chunk) * span, span), span)
+                scaled = held[i, from_rows, cols].astype(jnp.float32) * scales[row_tile, from_cols]
+                out_ref[to_rows, cols] = scaled.astype(jnp.bfloat16)
+                squares = scaled * scaled
                 for part in range(parts):
-                    tile = order_ref[blocks + chunk] * parts + part
-                    scale = scale_ref[tile, row_tile].astype(jnp.float32) * 0.125
-                    from_cols = pl.ds(pl.multiple_of(tile * TILE, TILE), TILE)
-                    scaled = held[i, from_rows, from_cols].astype(jnp.float32) * scale
-                    total += scaled * scaled
-                    target = chunk * span + part * TILE
-                    out_ref[to_rows, target : target + TILE] = scaled.astype(jnp.bfloat16)
+                    total += squares[:, part * TILE : (part + 1) * TILE]
             energy_ref[to_rows, :] = total
-        return carry
-
-    lax.fori_loop(0, blocks, body, 0)
-
-
-def prepare(value, present, power, order, span):
+
+
+def prepare(value, present, power, fence, offsets, span):
     row_count, col_count = value.shape
-    blocks = row_count // span
-    smem = pl.BlockSpec(memory_space=pltpu.SMEM)
-    table = (present << (power + 3)).T
-    return pl.pallas_call(
-        functools.partial(prepare_kernel, col_count // span),
-        in_specs=[smem] * 2 + [pl.BlockSpec(memory_space=pltpu.HBM)],
+    blocks, chunks = row_count // span, col_count // span
+    return pl.pallas_call(
+        functools.partial(prepare_kernel, offsets, chunks),
+        in_specs=[VMEM] * 3 + [pl.BlockSpec(memory_space=pltpu.HBM)],
         out_specs=[VMEM, VMEM],
         out_shape=[
             jax.ShapeDtypeStruct(value.shape, jnp.bfloat16),
@@ -72,11 +81,12 @@
         ],
         scratch_shapes=[
             pltpu.VMEM((blocks, span, col_count), jnp.bfloat16),
-            pltpu.SemaphoreType.DMA((blocks,)),
+            pltpu.VMEM((row_count // TILE, col_count), jnp.float32),
+            pltpu.SemaphoreType.DMA((blocks, chunks)),
         ],
         compiler_params=params(48),
         name="prepare",
-    )(order, table, value)
+    )(fence, present.T, power.T, value)
 
 
 def energy_kernel(span, total_ref, out_ref):
@@ -168,24 +178,18 @@
     )(*parts, source)
 
 
-def order_kernel(offsets, chunks, out_ref):
-    row, col = lax.axis_index("row"), lax.axis_index("col")
-    blocks = 2 * len(offsets)
-    for side in range(2):
-        for i, offset in enumerate(offsets):
-            out_ref[side * len(offsets) + i] = col ^ (2 * offset + 1 - side)
-    for chunk in range(chunks):
-        out_ref[blocks + chunk] = row ^ chunk
-
-
-def order_of(offsets, chunks):
-    return pl.pallas_call(
-        functools.partial(order_kernel, offsets, chunks),
-        out_shape=jax.ShapeDtypeStruct((2 * len(offsets) + chunks,), jnp.int32),
-        out_specs=pl.BlockSpec(memory_space=pltpu.SMEM),
+def fence_kernel(out_ref):
+    out_ref[...] = jnp.zeros_like(out_ref)
+
+
+def fence():
+    return pl.pallas_call(
+        fence_kernel,
+        out_shape=jax.ShapeDtypeStruct((8, TILE), jnp.float32),
+        out_specs=VMEM,
         compiler_params=params(1),
         cost_estimate=pl.CostEstimate(flops=10**10, bytes_accessed=10**8, transcendentals=0),
-        name="order",
+        name="fence",
     )()
 
 
@@ -247,14 +251,16 @@
     offsets = far_offsets(groups)
     cuts = [(0, 1), (1, groups - 1)] if groups > 1 else [(0, 1)]
 
-    order = order_of(offsets, row_size)
+    started = fence()
     current = source
     for step in range(STEPS):
         features = [current]
         for d in range(1, row_size):
             features.append(swap(current, "row", row_size, d))
         if step == 0:
-            adjacency, squares = prepare(value, occupancy, exponent, order, span)
+            adjacency, squares = prepare(
+                value, occupancy, exponent, started, offsets, span
+            )
             energy = energy_of(squares, span)
             energy_moved = swap(energy[: 8 * groups], "col", col_size, 1)
         first = multiply(adjacency, 0, 2 * half, 0, features[:1])

time: 80.7 us -> 80.8 us (level)
  waiting for transfers between devices: 40.3 us -> 42 us
  Pallas kernels: 11.9 us -> 10.3 us
    ppermute x25, waiting for transfers between devices: 40.3 us -> 42 us  [swap(): return lax.ppermute(array, axis, [(i, i ^ offset) for i in range(size)])]
    pallas_call x2, Pallas kernels: 4.43 us -> 2.77 us  [the longest x1 2.77 us: prepare(): pl.pallas_call(functools.partial(prepare_kernel, offsets, chunks), in_spe...]
  transfers between devices with their start and end apart: 25 -> 25, of which waited for: 19 -> 19; matrix products, arithmetic and copies ran while one was open for 0% -> 0% of each run, Pallas kernels for 13% -> 11%
where the time goes in v5:
time: 80.8 us; the launch traced here: 80.6 us
  waiting for transfers between devices  42 us (52%)
  starting transfers between devices  27.1 us (34%)
  Pallas kernels  10.3 us (13%)
  other arithmetic  0.92 us (1%)
    ppermute x25, waiting for transfers between devices, swap(): return lax.ppermute(array, axis, [(i, i ^ offset) for i in range(size)])  42 us
    ppermute x25, starting transfers between devices, swap(): return lax.ppermute(array, axis, [(i, i ^ offset) for i in range(size)])  27.1 us
    pallas_call x18, Pallas kernels, multiply(): pl.pallas_call(functools.partial(multiply_kernel, first_row, first, count...  6.54 us
    pallas_call x1, Pallas kernels, prepare(): pl.pallas_call(functools.partial(prepare_kernel, offsets, chunks), in_spe...  2.77 us
  transfers between devices with their start and end apart: 25, of which 19 were waited for; matrix products, arithmetic and copies ran while one was open for 0% of the time, Pallas kernels for 11%

profile of v5, /device:TPU:0, one launch (start us, length us, event | category | flops | bytes accessed | tf_op | source)
XLA Modules:
  0.0 80.6 jit_solution(6448648461950122192)
XLA Ops:
  0.0 3.0 %collective-permute-start.2 = (f32[256,128]{1,0:T(8,128)}, f32[256,128]{1,0:T(8,128)S(1)}, u32[]{:S(2)}, u32[]{:S(2)}) collective-permute-start(f32[256,128]{1,0:T(8,128)} %refs_4_.1), channel_id=1, source_target_pairs={{0,16},{8,24},{16,0},{24,8},{1,17},{9,25},{17,1},{25,9},{2,18},{10... | collective-permute-start | bytes 393224 | tf_op jit(solution)/shard_map/ppermute | solution.py:24
  3.0 1.5 %collective-permute-start.1 = (f32[256,128]{1,0:T(8,128)}, f32[256,128]{1,0:T(8,128)S(1)}, u32[]{:S(2)}, u32[]{:S(2)}) collective-permute-start(f32[256,128]{1,0:T(8,128)} %refs_4_.1), channel_id=1, source_target_pairs={{0,8},{8,0},{16,24},{24,16},{1,9},{9,1},{17,25},{25,17},{2,10},{10... | collective-permute-start | bytes 393224 | tf_op jit(solution)/shard_map/ppermute | solution.py:24
  4.6 2.8 %prepare.1 = (bf16[2048,1024]{1,0:T(8,128)(2,1)S(1)}, f32[2048,128]{1,0:T(8,128)S(1)}) custom-call(f32[8,128]{1,0:T(8,128)S(1)} %fence.1.fence_ref, s32[8,16]{1,0:T(8,128)S(1)} %bitcast.2, s32[8,16]{1,0:T(8,128)S(1)} %bitcast.3, bf16[2048,1024]{1,0:T(8,128)(2,1)} %value_ref.1), custom_call_target="tpu_custom_call" | custom-call | tf_op jit(solution)/shard_map/prepare/pallas_call | solution.py:74
  7.3 0.5 multiply.18.refs_2_
  7.8 1.8 %collective-permute-done.1.refs_0_ = f32[256,128]{1,0:T(8,128)S(1)} collective-permute-done((f32[256,128]{1,0:T(8,128)}, f32[256,128]{1,0:T(8,128)S(1)}, u32[]{:S(2)}, u32[]{:S(2)}) %collective-permute-start.1) | collective-permute-done | bytes 131104 | tf_op jit(solution)/shard_map/ppermute | solution.py:24
  9.6 0.7 multiply.19.refs_1_
  10.3 0.4 collective-permute-done.refs_0_
  10.8 0.3 multiply.23
  11.1 0.1 collective-permute-start.6
  11.1 0.2 multiply.21
  11.4 0.6 collective-permute-start.3
  11.9 0.5 energy.1.energy_ref
  12.5 0.2 multiply.20.mine_ref
  12.7 0.3 multiply.22.mine_ref
  13.0 0.7 collective-permute-done.4.energy_moved_ref
  13.7 3.8 %collective-permute-start.5 = (f32[264,128]{1,0:T(8,128)S(1)}, f32[264,128]{1,0:T(8,128)S(1)}, u32[]{:S(2)}, u32[]{:S(2)}) collective-permute-start(f32[264,128]{1,0:T(8,128)S(1)} %combine.2), channel_id=1, source_target_pairs={{0,6},{1,7},{2,4},{3,5},{4,2},{5,3},{6,0},{7,1},{8,14},{9,15},{10,... | collective-permute-start | bytes 405512 | tf_op jit(solution)/shard_map/ppermute | solution.py:24
  17.6 0.1 collective-permute-start.7
  17.6 0.6 collective-permute-start.8
  18.3 3.8 %collective-permute-done.5.refs_0_ = f32[264,128]{1,0:T(8,128)S(1)} collective-permute-done((f32[264,128]{1,0:T(8,128)S(1)}, f32[264,128]{1,0:T(8,128)S(1)}, u32[]{:S(2)}, u32[]{:S(2)}) %collective-permute-start.5) | collective-permute-done | bytes 135200 | tf_op jit(solution)/shard_map/ppermute | solution.py:24
  22.0 3.4 %collective-permute-done.7.refs_1_ = f32[264,128]{1,0:T(8,128)S(1)} collective-permute-done((f32[264,128]{1,0:T(8,128)S(1)}, f32[264,128]{1,0:T(8,128)S(1)}, u32[]{:S(2)}, u32[]{:S(2)}) %collective-permute-start.7) | collective-permute-done | bytes 135200 | tf_op jit(solution)/shard_map/ppermute | solution.py:24
  25.4 3.9 %collective-permute-done.8.refs_2_ = f32[264,128]{1,0:T(8,128)S(1)} collective-permute-done((f32[264,128]{1,0:T(8,128)S(1)}, f32[264,128]{1,0:T(8,128)S(1)}, u32[]{:S(2)}, u32[]{:S(2)}) %collective-permute-start.8) | collective-permute-done | bytes 135200 | tf_op jit(solution)/shard_map/ppermute | solution.py:24
  29.3 0.4 finish.1
  29.7 1.6 %collective-permute-start.11 = (f32[256,128]{1,0:T(8,128)S(1)}, f32[256,128]{1,0:T(8,128)S(1)}, u32[]{:S(2)}, u32[]{:S(2)}) collective-permute-start(f32[256,128]{1,0:T(8,128)S(1)} %get-tuple-element.17.refs_0_), channel_id=1, source_target_pairs={{0,16},{8,24},{16,0},{24,8},{1,17},{9,25},{17,1},{25,9},{2,18},{10... | collective-permute-start | bytes 393224 | tf_op jit(solution)/shard_map/ppermute | solution.py:24
  31.2 1.5 %collective-permute-start.10 = (f32[256,128]{1,0:T(8,128)S(1)}, f32[256,128]{1,0:T(8,128)S(1)}, u32[]{:S(2)}, u32[]{:S(2)}) collective-permute-start(f32[256,128]{1,0:T(8,128)S(1)} %get-tuple-element.17.refs_0_), channel_id=1, source_target_pairs={{0,8},{8,0},{16,24},{24,16},{1,9},{9,1},{17,25},{25,17},{2,10},{10... | collective-permute-start | bytes 393224 | tf_op jit(solution)/shard_map/ppermute | solution.py:24
  32.7 0.5 collective-permute-start.9
  33.2 0.5 multiply.24.refs_2_
  33.7 1.0 %collective-permute-done.11.refs_1_ = f32[256,128]{1,0:T(8,128)S(1)} collective-permute-done((f32[256,128]{1,0:T(8,128)S(1)}, f32[256,128]{1,0:T(8,128)S(1)}, u32[]{:S(2)}, u32[]{:S(2)}) %collective-permute-start.11) | collective-permute-done | bytes 131104 | tf_op jit(solution)/shard_map/ppermute | solution.py:24
  34.7 2.4 %collective-permute-done.10.refs_0_ = f32[256,128]{1,0:T(8,128)S(1)} collective-permute-done((f32[256,128]{1,0:T(8,128)S(1)}, f32[256,128]{1,0:T(8,128)S(1)}, u32[]{:S(2)}, u32[]{:S(2)}) %collective-permute-start.10) | collective-permute-done | bytes 131104 | tf_op jit(solution)/shard_map/ppermute | solution.py:24
  37.1 0.7 multiply.25.refs_1_
  37.8 1.1 %collective-permute-done.9.refs_0_ = f32[256,128]{1,0:T(8,128)S(1)} collective-permute-done((f32[256,128]{1,0:T(8,128)S(1)}, f32[256,128]{1,0:T(8,128)S(1)}, u32[]{:S(2)}, u32[]{:S(2)}) %collective-permute-start.9) | collective-permute-done | bytes 131104 | tf_op jit(solution)/shard_map/ppermute | solution.py:24
  39.0 0.3 multiply.29
  39.3 0.1 collective-permute-start.14
  39.3 0.2 multiply.27
  39.6 0.6 collective-permute-start.12
  40.1 0.2 multiply.26
  40.3 0.3 multiply.28
  40.6 0.6 collective-permute-done.12
  41.3 2.5 %collective-permute-start.13 = (f32[256,128]{1,0:T(8,128)S(1)}, f32[256,128]{1,0:T(8,128)S(1)}, u32[]{:S(2)}, u32[]{:S(2)}) collective-permute-start(f32[256,128]{1,0:T(8,128)S(1)} %add.48), channel_id=1, source_target_pairs={{0,6},{1,7},{2,4},{3,5},{4,2},{5,3},{6,0},{7,1},{8,14},{9,15},{10,... | collective-permute-start | bytes 393224 | tf_op jit(solution)/shard_map/ppermute | solution.py:24
  43.9 1.9 %collective-permute-start.16 = (f32[256,128]{1,0:T(8,128)S(1)}, f32[256,128]{1,0:T(8,128)S(1)}, u32[]{:S(2)}, u32[]{:S(2)}) collective-permute-start(f32[256,128]{1,0:T(8,128)S(1)} %get-tuple-element.22), channel_id=1, source_target_pairs={{0,4},{1,5},{2,6},{3,7},{4,0},{5,1},{6,2},{7,3},{8,12},{9,13},{10,... | collective-permute-start | bytes 393224 | tf_op jit(solution)/shard_map/ppermute | solution.py:24
  45.8 3.7 %collective-permute-done.13 = f32[256,128]{1,0:T(8,128)S(1)} collective-permute-done((f32[256,128]{1,0:T(8,128)S(1)}, f32[256,128]{1,0:T(8,128)S(1)}, u32[]{:S(2)}, u32[]{:S(2)}) %collective-permute-start.13) | collective-permute-done | bytes 131104 | tf_op jit(solution)/shard_map/ppermute | solution.py:24
  49.5 4.8 %collective-permute-done.15 = f32[256,128]{1,0:T(8,128)S(1)} collective-permute-done((f32[256,128]{1,0:T(8,128)S(1)}, f32[256,128]{1,0:T(8,128)S(1)}, u32[]{:S(2)}, u32[]{:S(2)}) %collective-permute-start.15) | collective-permute-done | bytes 131104 | tf_op jit(solution)/shard_map/ppermute | solution.py:24
  54.4 0.1 fusion.9.refs_0_
  54.4 1.0 %collective-permute-start.19 = (f32[256,128]{1,0:T(8,128)S(1)}, f32[256,128]{1,0:T(8,128)S(1)}, u32[]{:S(2)}, u32[]{:S(2)}) collective-permute-start(f32[256,128]{1,0:T(8,128)S(1)} %fusion.9.refs_0_), channel_id=1, source_target_pairs={{0,16},{8,24},{16,0},{24,8},{1,17},{9,25},{17,1},{25,9},{2,18},{10... | collective-permute-start | bytes 393224 | tf_op jit(solution)/shard_map/ppermute | solution.py:24
  55.5 1.5 %collective-permute-start.18 = (f32[256,128]{1,0:T(8,128)S(1)}, f32[256,128]{1,0:T(8,128)S(1)}, u32[]{:S(2)}, u32[]{:S(2)}) collective-permute-start(f32[256,128]{1,0:T(8,128)S(1)} %fusion.9.refs_0_), channel_id=1, source_target_pairs={{0,8},{8,0},{16,24},{24,16},{1,9},{9,1},{17,25},{25,17},{2,10},{10... | collective-permute-start | bytes 393224 | tf_op jit(solution)/shard_map/ppermute | solution.py:24
  57.0 1.0 %collective-permute-start.17 = (f32[256,128]{1,0:T(8,128)S(1)}, f32[256,128]{1,0:T(8,128)S(1)}, u32[]{:S(2)}, u32[]{:S(2)}) collective-permute-start(f32[256,128]{1,0:T(8,128)S(1)} %fusion.9.refs_0_), channel_id=1, source_target_pairs={{0,24},{8,16},{16,8},{24,0},{1,25},{9,17},{17,9},{25,1},{2,26},{10... | collective-permute-start | bytes 393224 | tf_op jit(solution)/shard_map/ppermute | solution.py:24
  58.0 0.5 multiply.30.refs_2_
  58.5 1.5 %collective-permute-done.19.refs_1_ = f32[256,128]{1,0:T(8,128)S(1)} collective-permute-done((f32[256,128]{1,0:T(8,128)S(1)}, f32[256,128]{1,0:T(8,128)S(1)}, u32[]{:S(2)}, u32[]{:S(2)}) %collective-permute-start.19) | collective-permute-done | bytes 131104 | tf_op jit(solution)/shard_map/ppermute | solution.py:24
  59.9 1.9 %collective-permute-done.18.refs_0_ = f32[256,128]{1,0:T(8,128)S(1)} collective-permute-done((f32[256,128]{1,0:T(8,128)S(1)}, f32[256,128]{1,0:T(8,128)S(1)}, u32[]{:S(2)}, u32[]{:S(2)}) %collective-permute-start.18) | collective-permute-done | bytes 131104 | tf_op jit(solution)/shard_map/ppermute | solution.py:24
  61.8 0.7 multiply.31.refs_1_
  62.6 1.3 %collective-permute-done.17.refs_0_ = f32[256,128]{1,0:T(8,128)S(1)} collective-permute-done((f32[256,128]{1,0:T(8,128)S(1)}, f32[256,128]{1,0:T(8,128)S(1)}, u32[]{:S(2)}, u32[]{:S(2)}) %collective-permute-start.17) | collective-permute-done | bytes 131104 | tf_op jit(solution)/shard_map/ppermute | solution.py:24
  63.9 0.3 multiply.35
  64.2 0.1 collective-permute-start.22
  64.3 0.2 multiply.33
  64.5 0.6 collective-permute-start.20
  65.1 0.2 multiply.32
  65.3 0.3 multiply.34
  65.6 0.6 collective-permute-done.20
  66.2 1.6 %collective-permute-start.21 = (f32[256,128]{1,0:T(8,128)S(1)}, f32[256,128]{1,0:T(8,128)S(1)}, u32[]{:S(2)}, u32[]{:S(2)}) collective-permute-start(f32[256,128]{1,0:T(8,128)S(1)} %add.56), channel_id=1, source_target_pairs={{0,6},{1,7},{2,4},{3,5},{4,2},{5,3},{6,0},{7,1},{8,14},{9,15},{10,... | collective-permute-start | bytes 393224 | tf_op jit(solution)/shard_map/ppermute | solution.py:24
  67.8 0.3 collective-permute-start.23
  68.1 2.6 %collective-permute-start.24 = (f32[256,128]{1,0:T(8,128)S(1)}, f32[256,128]{1,0:T(8,128)S(1)}, u32[]{:S(2)}, u32[]{:S(2)}) collective-permute-start(f32[256,128]{1,0:T(8,128)S(1)} %get-tuple-element.20), channel_id=1, source_target_pairs={{0,4},{1,5},{2,6},{3,7},{4,0},{5,1},{6,2},{7,3},{8,12},{9,13},{10,... | collective-permute-start | bytes 393224 | tf_op jit(solution)/shard_map/ppermute | solution.py:24
  70.8 3.7 %collective-permute-done.21 = f32[256,128]{1,0:T(8,128)S(1)} collective-permute-done((f32[256,128]{1,0:T(8,128)S(1)}, f32[256,128]{1,0:T(8,128)S(1)}, u32[]{:S(2)}, u32[]{:S(2)}) %collective-permute-start.21) | collective-permute-done | bytes 131104 | tf_op jit(solution)/shard_map/ppermute | solution.py:24
  74.5 3.9 %collective-permute-done.23 = f32[256,128]{1,0:T(8,128)S(1)} collective-permute-done((f32[256,128]{1,0:T(8,128)S(1)}, f32[256,128]{1,0:T(8,128)S(1)}, u32[]{:S(2)}, u32[]{:S(2)}) %collective-permute-start.23) | collective-permute-done | bytes 131104 | tf_op jit(solution)/shard_map/ppermute | solution.py:24
  78.4 1.5 %collective-permute-done.24 = f32[256,128]{1,0:T(8,128)S(1)} collective-permute-done((f32[256,128]{1,0:T(8,128)S(1)}, f32[256,128]{1,0:T(8,128)S(1)}, u32[]{:S(2)}, u32[]{:S(2)}) %collective-permute-start.24) | collective-permute-done | bytes 131104 | tf_op jit(solution)/shard_map/ppermute | solution.py:24
  79.9 0.7 fusion.4
  (23 shorter events, 0.4 us)
Async XLA Ops:
  0.0 4.5 %copy-start.2 = (s32[16,8]{0,1:T(8,128)S(1)}, s32[16,8]{0,1:T(8,128)}, u32[]{:S(2)}) copy-start(s32[16,8]{0,1:T(8,128)} %param.7) | copy-start | bytes 1540
  0.0 4.5 %copy-start.1 = (s32[16,8]{0,1:T(8,128)S(1)}, s32[16,8]{0,1:T(8,128)}, u32[]{:S(2)}) copy-start(s32[16,8]{0,1:T(8,128)} %param.6) | copy-start | bytes 1540
  0.0 7.8 %collective-permute-start.2 = (f32[256,128]{1,0:T(8,128)}, f32[256,128]{1,0:T(8,128)S(1)}, u32[]{:S(2)}, u32[]{:S(2)}) collective-permute-start(f32[256,128]{1,0:T(8,128)} %refs_4_.1), channel_id=1, source_target_pairs={{0,16},{8,24},{16,0},{24,8},{1,17},{9,25},{17,1},{25,9},{2,18},{10... | collective-permute-start | bytes 393224 | tf_op jit(solution)/shard_map/ppermute | solution.py:24
  3.0 6.6 %collective-permute-start.1 = (f32[256,128]{1,0:T(8,128)}, f32[256,128]{1,0:T(8,128)S(1)}, u32[]{:S(2)}, u32[]{:S(2)}) collective-permute-start(f32[256,128]{1,0:T(8,128)} %refs_4_.1), channel_id=1, source_target_pairs={{0,8},{8,0},{16,24},{24,16},{1,9},{9,1},{17,25},{25,17},{2,10},{10... | collective-permute-start | bytes 393224 | tf_op jit(solution)/shard_map/ppermute | solution.py:24
  4.5 6.3 %collective-permute-start = (f32[256,128]{1,0:T(8,128)}, f32[256,128]{1,0:T(8,128)S(1)}, u32[]{:S(2)}, u32[]{:S(2)}) collective-permute-start(f32[256,128]{1,0:T(8,128)} %refs_4_.1), channel_id=1, source_target_pairs={{0,24},{8,16},{16,8},{24,0},{1,25},{9,17},{17,9},{25,1},{2,26},{10... | collective-permute-start | bytes 393224 | tf_op jit(solution)/shard_map/ppermute | solution.py:24
  4.5 2.8 %copy-start = (f32[256,128]{1,0:T(8,128)S(1)}, f32[256,128]{1,0:T(8,128)}, u32[]{:S(2)}) copy-start(f32[256,128]{1,0:T(8,128)} %refs_4_.1) | copy-start | bytes 393220
  11.1 6.5 %collective-permute-start.6 = (f32[768,128]{1,0:T(8,128)S(1)}, f32[768,128]{1,0:T(8,128)S(1)}, u32[]{:S(2)}, u32[]{:S(2)}) collective-permute-start(f32[768,128]{1,0:T(8,128)S(1)} %multiply.23), channel_id=1, source_target_pairs={{0,1},{1,0},{2,3},{3,2},{4,5},{5,4},{6,7},{7,6},{8,9},{9,8},{10,11... | collective-permute-start | bytes 1179656 | tf_op jit(solution)/shard_map/ppermute | solution.py:24
  11.4 2.3 %collective-permute-start.3 = (f32[256,128]{1,0:T(8,128)S(1)}, f32[256,128]{1,0:T(8,128)S(1)}, u32[]{:S(2)}, u32[]{:S(2)}) collective-permute-start(f32[256,128]{1,0:T(8,128)S(1)} %multiply.21), channel_id=1, source_target_pairs={{0,1},{1,0},{2,3},{3,2},{4,5},{5,4},{6,7},{7,6},{8,9},{9,8},{10,11... | collective-permute-start | bytes 393224 | tf_op jit(solution)/shard_map/ppermute | solution.py:24
  12.4 1.2 %collective-permute-start.4 = (f32[32,128]{1,0:T(8,128)S(1)}, f32[32,128]{1,0:T(8,128)S(1)}, u32[]{:S(2)}, u32[]{:S(2)}) collective-permute-start(f32[32,128]{1,0:T(8,128)S(1)} %slice.52), channel_id=1, source_target_pairs={{0,1},{1,0},{2,3},{3,2},{4,5},{5,4},{6,7},{7,6},{8,9},{9,8},{10,11... | collective-permute-start | bytes 49160 | tf_op jit(solution)/shard_map/ppermute | solution.py:24
  13.7 8.4 %collective-permute-start.5 = (f32[264,128]{1,0:T(8,128)S(1)}, f32[264,128]{1,0:T(8,128)S(1)}, u32[]{:S(2)}, u32[]{:S(2)}) collective-permute-start(f32[264,128]{1,0:T(8,128)S(1)} %combine.2), channel_id=1, source_target_pairs={{0,6},{1,7},{2,4},{3,5},{4,2},{5,3},{6,0},{7,1},{8,14},{9,15},{10,... | collective-permute-start | bytes 405512 | tf_op jit(solution)/shard_map/ppermute | solution.py:24
  17.6 7.8 %collective-permute-start.7 = (f32[264,128]{1,0:T(8,128)S(1)}, f32[264,128]{1,0:T(8,128)S(1)}, u32[]{:S(2)}, u32[]{:S(2)}) collective-permute-start(f32[264,128]{1,0:T(8,128)S(1)} %get-tuple-element.14), channel_id=1, source_target_pairs={{0,2},{1,3},{2,0},{3,1},{4,6},{5,7},{6,4},{7,5},{8,10},{9,11},{10,... | collective-permute-start | bytes 405512 | tf_op jit(solution)/shard_map/ppermute | solution.py:24
  17.6 11.6 %collective-permute-start.8 = (f32[264,128]{1,0:T(8,128)S(1)}, f32[264,128]{1,0:T(8,128)S(1)}, u32[]{:S(2)}, u32[]{:S(2)}) collective-permute-start(f32[264,128]{1,0:T(8,128)S(1)} %get-tuple-element.15), channel_id=1, source_target_pairs={{0,4},{1,5},{2,6},{3,7},{4,0},{5,1},{6,2},{7,3},{8,12},{9,13},{10,... | collective-permute-start | bytes 405512 | tf_op jit(solution)/shard_map/ppermute | solution.py:24
  29.7 5.0 %collective-permute-start.11 = (f32[256,128]{1,0:T(8,128)S(1)}, f32[256,128]{1,0:T(8,128)S(1)}, u32[]{:S(2)}, u32[]{:S(2)}) collective-permute-start(f32[256,128]{1,0:T(8,128)S(1)} %get-tuple-element.17.refs_0_), channel_id=1, source_target_pairs={{0,16},{8,24},{16,0},{24,8},{1,17},{9,25},{17,1},{25,9},{2,18},{10... | collective-permute-start | bytes 393224 | tf_op jit(solution)/shard_map/ppermute | solution.py:24
  31.2 5.8 %collective-permute-start.10 = (f32[256,128]{1,0:T(8,128)S(1)}, f32[256,128]{1,0:T(8,128)S(1)}, u32[]{:S(2)}, u32[]{:S(2)}) collective-permute-start(f32[256,128]{1,0:T(8,128)S(1)} %get-tuple-element.17.refs_0_), channel_id=1, source_target_pairs={{0,8},{8,0},{16,24},{24,16},{1,9},{9,1},{17,25},{25,17},{2,10},{10... | collective-permute-start | bytes 393224 | tf_op jit(solution)/shard_map/ppermute | solution.py:24
  32.7 6.2 %collective-permute-start.9 = (f32[256,128]{1,0:T(8,128)S(1)}, f32[256,128]{1,0:T(8,128)S(1)}, u32[]{:S(2)}, u32[]{:S(2)}) collective-permute-start(f32[256,128]{1,0:T(8,128)S(1)} %get-tuple-element.17.refs_0_), channel_id=1, source_target_pairs={{0,24},{8,16},{16,8},{24,0},{1,25},{9,17},{17,9},{25,1},{2,26},{10... | collective-permute-start | bytes 393224 | tf_op jit(solution)/shard_map/ppermute | solution.py:24
  39.3 4.5 %collective-permute-start.14 = (f32[768,128]{1,0:T(8,128)S(1)}, f32[768,128]{1,0:T(8,128)S(1)}, u32[]{:S(2)}, u32[]{:S(2)}) collective-permute-start(f32[768,128]{1,0:T(8,128)S(1)} %multiply.29), channel_id=1, source_target_pairs={{0,1},{1,0},{2,3},{3,2},{4,5},{5,4},{6,7},{7,6},{8,9},{9,8},{10,11... | collective-permute-start | bytes 1179656 | tf_op jit(solution)/shard_map/ppermute | solution.py:24
  39.6 1.7 %collective-permute-start.12 = (f32[256,128]{1,0:T(8,128)S(1)}, f32[256,128]{1,0:T(8,128)S(1)}, u32[]{:S(2)}, u32[]{:S(2)}) collective-permute-start(f32[256,128]{1,0:T(8,128)S(1)} %multiply.27), channel_id=1, source_target_pairs={{0,1},{1,0},{2,3},{3,2},{4,5},{5,4},{6,7},{7,6},{8,9},{9,8},{10,11... | collective-permute-start | bytes 393224 | tf_op jit(solution)/shard_map/ppermute | solution.py:24
  41.3 8.3 %collective-permute-start.13 = (f32[256,128]{1,0:T(8,128)S(1)}, f32[256,128]{1,0:T(8,128)S(1)}, u32[]{:S(2)}, u32[]{:S(2)}) collective-permute-start(f32[256,128]{1,0:T(8,128)S(1)} %add.48), channel_id=1, source_target_pairs={{0,6},{1,7},{2,4},{3,5},{4,2},{5,3},{6,0},{7,1},{8,14},{9,15},{10,... | collective-permute-start | bytes 393224 | tf_op jit(solution)/shard_map/ppermute | solution.py:24
  43.8 10.5 %collective-permute-start.15 = (f32[256,128]{1,0:T(8,128)S(1)}, f32[256,128]{1,0:T(8,128)S(1)}, u32[]{:S(2)}, u32[]{:S(2)}) collective-permute-start(f32[256,128]{1,0:T(8,128)S(1)} %get-tuple-element.21), channel_id=1, source_target_pairs={{0,2},{1,3},{2,0},{3,1},{4,6},{5,7},{6,4},{7,5},{8,10},{9,11},{10,... | collective-permute-start | bytes 393224 | tf_op jit(solution)/shard_map/ppermute | solution.py:24
  43.9 10.5 %collective-permute-start.16 = (f32[256,128]{1,0:T(8,128)S(1)}, f32[256,128]{1,0:T(8,128)S(1)}, u32[]{:S(2)}, u32[]{:S(2)}) collective-permute-start(f32[256,128]{1,0:T(8,128)S(1)} %get-tuple-element.22), channel_id=1, source_target_pairs={{0,4},{1,5},{2,6},{3,7},{4,0},{5,1},{6,2},{7,3},{8,12},{9,13},{10,... | collective-permute-start | bytes 393224 | tf_op jit(solution)/shard_map/ppermute | solution.py:24
  54.4 5.5 %collective-permute-start.19 = (f32[256,128]{1,0:T(8,128)S(1)}, f32[256,128]{1,0:T(8,128)S(1)}, u32[]{:S(2)}, u32[]{:S(2)}) collective-permute-start(f32[256,128]{1,0:T(8,128)S(1)} %fusion.9.refs_0_), channel_id=1, source_target_pairs={{0,16},{8,24},{16,0},{24,8},{1,17},{9,25},{17,1},{25,9},{2,18},{10... | collective-permute-start | bytes 393224 | tf_op jit(solution)/shard_map/ppermute | solution.py:24
  55.5 6.4 %collective-permute-start.18 = (f32[256,128]{1,0:T(8,128)S(1)}, f32[256,128]{1,0:T(8,128)S(1)}, u32[]{:S(2)}, u32[]{:S(2)}) collective-permute-start(f32[256,128]{1,0:T(8,128)S(1)} %fusion.9.refs_0_), channel_id=1, source_target_pairs={{0,8},{8,0},{16,24},{24,16},{1,9},{9,1},{17,25},{25,17},{2,10},{10... | collective-permute-start | bytes 393224 | tf_op jit(solution)/shard_map/ppermute | solution.py:24
  57.0 7.0 %collective-permute-start.17 = (f32[256,128]{1,0:T(8,128)S(1)}, f32[256,128]{1,0:T(8,128)S(1)}, u32[]{:S(2)}, u32[]{:S(2)}) collective-permute-start(f32[256,128]{1,0:T(8,128)S(1)} %fusion.9.refs_0_), channel_id=1, source_target_pairs={{0,24},{8,16},{16,8},{24,0},{1,25},{9,17},{17,9},{25,1},{2,26},{10... | collective-permute-start | bytes 393224 | tf_op jit(solution)/shard_map/ppermute | solution.py:24
  64.2 3.6 %collective-permute-start.22 = (f32[768,128]{1,0:T(8,128)S(1)}, f32[768,128]{1,0:T(8,128)S(1)}, u32[]{:S(2)}, u32[]{:S(2)}) collective-permute-start(f32[768,128]{1,0:T(8,128)S(1)} %multiply.35), channel_id=1, source_target_pairs={{0,1},{1,0},{2,3},{3,2},{4,5},{5,4},{6,7},{7,6},{8,9},{9,8},{10,11... | collective-permute-start | bytes 1179656 | tf_op jit(solution)/shard_map/ppermute | solution.py:24
  64.5 1.7 %collective-permute-start.20 = (f32[256,128]{1,0:T(8,128)S(1)}, f32[256,128]{1,0:T(8,128)S(1)}, u32[]{:S(2)}, u32[]{:S(2)}) collective-permute-start(f32[256,128]{1,0:T(8,128)S(1)} %multiply.33), channel_id=1, source_target_pairs={{0,1},{1,0},{2,3},{3,2},{4,5},{5,4},{6,7},{7,6},{8,9},{9,8},{10,11... | collective-permute-start | bytes 393224 | tf_op jit(solution)/shard_map/ppermute | solution.py:24
  66.2 8.3 %collective-permute-start.21 = (f32[256,128]{1,0:T(8,128)S(1)}, f32[256,128]{1,0:T(8,128)S(1)}, u32[]{:S(2)}, u32[]{:S(2)}) collective-permute-start(f32[256,128]{1,0:T(8,128)S(1)} %add.56), channel_id=1, source_target_pairs={{0,6},{1,7},{2,4},{3,5},{4,2},{5,3},{6,0},{7,1},{8,14},{9,15},{10,... | collective-permute-start | bytes 393224 | tf_op jit(solution)/shard_map/ppermute | solution.py:24
  67.8 10.6 %collective-permute-start.23 = (f32[256,128]{1,0:T(8,128)S(1)}, f32[256,128]{1,0:T(8,128)S(1)}, u32[]{:S(2)}, u32[]{:S(2)}) collective-permute-start(f32[256,128]{1,0:T(8,128)S(1)} %get-tuple-element.19), channel_id=1, source_target_pairs={{0,2},{1,3},{2,0},{3,1},{4,6},{5,7},{6,4},{7,5},{8,10},{9,11},{10,... | collective-permute-start | bytes 393224 | tf_op jit(solution)/shard_map/ppermute | solution.py:24
  68.1 11.8 %collective-permute-start.24 = (f32[256,128]{1,0:T(8,128)S(1)}, f32[256,128]{1,0:T(8,128)S(1)}, u32[]{:S(2)}, u32[]{:S(2)}) collective-permute-start(f32[256,128]{1,0:T(8,128)S(1)} %get-tuple-element.20), channel_id=1, source_target_pairs={{0,4},{1,5},{2,6},{3,7},{4,0},{5,1},{6,2},{7,3},{8,12},{9,13},{10,... | collective-permute-start | bytes 393224 | tf_op jit(solution)/shard_map/ppermute | solution.py:24

commit v6 on v5

--- a/solution.py
+++ b/solution.py
@@ -24,15 +24,15 @@
     return lax.ppermute(array, axis, [(i, i ^ offset) for i in range(size)])
 
 
-def prepare_kernel(offsets, chunks, fence_ref, present_ref, power_ref, value_ref, out_ref, energy_ref, held, scales, arrived):
+def prepare_kernel(offsets, near, fence_ref, present_ref, power_ref, value_ref, out_ref, energy_ref, held, scales, arrived):
     blocks, span, _ = held.shape
-    parts = span // TILE
+    parts, chunks = span // TILE, len(near)
     row, col = lax.axis_index("row"), lax.axis_index("col")
     sources = [col ^ (2 * offset + 1 - side) for side in range(2) for offset in offsets]
 
     def copy(i, chunk):
         rows = pl.ds(pl.multiple_of(sources[i] * span, span), span)
-        cols = pl.ds(pl.multiple_of((row ^ chunk) * span, span), span)
+        cols = pl.ds(pl.multiple_of((row ^ near[chunk]) * span, span), span)
         target = held.at[i, :, pl.ds(chunk * span, span)]
         return pltpu.make_async_copy(value_ref.at[rows, cols], target, arrived.at[i, chunk])
 
@@ -59,7 +59,7 @@
             total = jnp.zeros((TILE, TILE), jnp.float32)
             for chunk in range(chunks):
                 cols = slice(chunk * span, (chunk + 1) * span)
-                from_cols = pl.ds(pl.multiple_of((row ^ chunk) * span, span), span)
+                from_cols = pl.ds(pl.multiple_of((row ^ near[chunk]) * span, span), span)
                 scaled = held[i, from_rows, cols].astype(jnp.float32) * scales[row_tile, from_cols]
                 out_ref[to_rows, cols] = scaled.astype(jnp.bfloat16)
                 squares = scaled * scaled
@@ -68,11 +68,11 @@
             energy_ref[to_rows, :] = total
 
 
-def prepare(value, present, power, fence, offsets, span):
+def prepare(value, present, power, fence, offsets, near, span):
     row_count, col_count = value.shape
     blocks, chunks = row_count // span, col_count // span
     return pl.pallas_call(
-        functools.partial(prepare_kernel, offsets, chunks),
+        functools.partial(prepare_kernel, offsets, near),
         in_specs=[VMEM] * 3 + [pl.BlockSpec(memory_space=pltpu.HBM)],
         out_specs=[VMEM, VMEM],
         out_shape=[
@@ -238,6 +238,10 @@
     )(adjacency, *features, *([total] if add else []))
 
 
+def near_offsets(size):
+    return [size - 1] + list(range(1, size - 1))
+
+
 def far_offsets(groups):
     return [groups - 1] + list(range(1, groups - 1)) + [0] if groups > 1 else [0]
 
@@ -248,18 +252,18 @@
     nodes = value.shape[0] * row_size
     groups = col_size // 2
     half = groups * span
-    offsets = far_offsets(groups)
+    offsets, near = far_offsets(groups), near_offsets(row_size)
     cuts = [(0, 1), (1, groups - 1)] if groups > 1 else [(0, 1)]
 
     started = fence()
     current = source
     for step in range(STEPS):
         features = [current]
-        for d in range(1, row_size):
+        for d in near:
             features.append(swap(current, "row", row_size, d))
         if step == 0:
             adjacency, squares = prepare(
-                value, occupancy, exponent, started, offsets, span
+                value, occupancy, exponent, started, offsets, [0] + near, span
             )
             energy = energy_of(squares, span)
             energy_moved = swap(energy[: 8 * groups], "col", col_size, 1)

time: 80.8 us -> 82.6 us (1.022)
  waiting for transfers between devices: 42 us -> 43.9 us
    ppermute x25, waiting for transfers between devices: 42 us -> 43.9 us  [swap(): return lax.ppermute(array, axis, [(i, i ^ offset) for i in range(size)])]
where the time goes in v6:
time: 82.6 us; the launch traced here: 82.4 us
  waiting for transfers between devices  43.9 us (53%)
  starting transfers between devices  27.1 us (33%)
  Pallas kernels  10.3 us (12%)
  other arithmetic  0.92 us (1%)
    ppermute x25, waiting for transfers between devices, swap(): return lax.ppermute(array, axis, [(i, i ^ offset) for i in range(size)])  43.9 us
    ppermute x25, starting transfers between devices, swap(): return lax.ppermute(array, axis, [(i, i ^ offset) for i in range(size)])  27.1 us
    pallas_call x18, Pallas kernels, multiply(): pl.pallas_call(functools.partial(multiply_kernel, first_row, first, count...  6.54 us
    pallas_call x1, Pallas kernels, prepare(): pl.pallas_call(functools.partial(prepare_kernel, offsets, near), in_specs...  2.77 us
  transfers between devices with their start and end apart: 25, of which 19 were waited for; matrix products, arithmetic and copies ran while one was open for 0% of the time, Pallas kernels for 11%

profile of v6, /device:TPU:0, one launch (start us, length us, event | category | flops | bytes accessed | tf_op | source)
XLA Modules:
  0.0 82.4 jit_solution(14214274912675064104)
XLA Ops:
  0.0 3.0 %collective-permute-start.2 = (f32[256,128]{1,0:T(8,128)}, f32[256,128]{1,0:T(8,128)S(1)}, u32[]{:S(2)}, u32[]{:S(2)}) collective-permute-start(f32[256,128]{1,0:T(8,128)} %refs_4_.1), channel_id=1, source_target_pairs={{0,8},{8,0},{16,24},{24,16},{1,9},{9,1},{17,25},{25,17},{2,10},{10... | collective-permute-start | bytes 393224 | tf_op jit(solution)/shard_map/ppermute | solution.py:24
  3.0 1.5 %collective-permute-start.1 = (f32[256,128]{1,0:T(8,128)}, f32[256,128]{1,0:T(8,128)S(1)}, u32[]{:S(2)}, u32[]{:S(2)}) collective-permute-start(f32[256,128]{1,0:T(8,128)} %refs_4_.1), channel_id=1, source_target_pairs={{0,24},{8,16},{16,8},{24,0},{1,25},{9,17},{17,9},{25,1},{2,26},{10... | collective-permute-start | bytes 393224 | tf_op jit(solution)/shard_map/ppermute | solution.py:24
  4.5 2.8 %prepare.1 = (bf16[2048,1024]{1,0:T(8,128)(2,1)S(1)}, f32[2048,128]{1,0:T(8,128)S(1)}) custom-call(f32[8,128]{1,0:T(8,128)S(1)} %fence.1.fence_ref, s32[8,16]{1,0:T(8,128)S(1)} %bitcast.2, s32[8,16]{1,0:T(8,128)S(1)} %bitcast.3, bf16[2048,1024]{1,0:T(8,128)(2,1)} %value_ref.1), custom_call_target="tpu_custom_call" | custom-call | tf_op jit(solution)/shard_map/prepare/pallas_call | solution.py:74
  7.3 0.5 multiply.18.refs_2_
  7.8 3.0 %collective-permute-done.1.refs_0_ = f32[256,128]{1,0:T(8,128)S(1)} collective-permute-done((f32[256,128]{1,0:T(8,128)}, f32[256,128]{1,0:T(8,128)S(1)}, u32[]{:S(2)}, u32[]{:S(2)}) %collective-permute-start.1) | collective-permute-done | bytes 131104 | tf_op jit(solution)/shard_map/ppermute | solution.py:24
  10.8 0.7 multiply.19.refs_1_
  11.5 0.6 collective-permute-done.refs_0_
  12.2 0.3 multiply.23
  12.4 0.1 collective-permute-start.6
  12.5 0.2 multiply.21
  12.7 0.6 collective-permute-start.3
  13.3 0.5 energy.1.energy_ref
  13.9 0.2 multiply.20.mine_ref
  14.1 0.3 multiply.22.mine_ref
  14.4 0.7 collective-permute-done.4.energy_moved_ref
  15.1 3.7 %collective-permute-start.5 = (f32[264,128]{1,0:T(8,128)S(1)}, f32[264,128]{1,0:T(8,128)S(1)}, u32[]{:S(2)}, u32[]{:S(2)}) collective-permute-start(f32[264,128]{1,0:T(8,128)S(1)} %combine.2), channel_id=1, source_target_pairs={{0,6},{1,7},{2,4},{3,5},{4,2},{5,3},{6,0},{7,1},{8,14},{9,15},{10,... | collective-permute-start | bytes 405512 | tf_op jit(solution)/shard_map/ppermute | solution.py:24
  18.8 0.1 collective-permute-start.7
  18.9 0.8 collective-permute-start.8
  19.7 3.8 %collective-permute-done.5.refs_0_ = f32[264,128]{1,0:T(8,128)S(1)} collective-permute-done((f32[264,128]{1,0:T(8,128)S(1)}, f32[264,128]{1,0:T(8,128)S(1)}, u32[]{:S(2)}, u32[]{:S(2)}) %collective-permute-start.5) | collective-permute-done | bytes 135200 | tf_op jit(solution)/shard_map/ppermute | solution.py:24
  23.4 3.2 %collective-permute-done.7.refs_1_ = f32[264,128]{1,0:T(8,128)S(1)} collective-permute-done((f32[264,128]{1,0:T(8,128)S(1)}, f32[264,128]{1,0:T(8,128)S(1)}, u32[]{:S(2)}, u32[]{:S(2)}) %collective-permute-start.7) | collective-permute-done | bytes 135200 | tf_op jit(solution)/shard_map/ppermute | solution.py:24
  26.6 3.8 %collective-permute-done.8.refs_2_ = f32[264,128]{1,0:T(8,128)S(1)} collective-permute-done((f32[264,128]{1,0:T(8,128)S(1)}, f32[264,128]{1,0:T(8,128)S(1)}, u32[]{:S(2)}, u32[]{:S(2)}) %collective-permute-start.8) | collective-permute-done | bytes 135200 | tf_op jit(solution)/shard_map/ppermute | solution.py:24
  30.5 0.4 finish.1
  30.9 1.6 %collective-permute-start.11 = (f32[256,128]{1,0:T(8,128)S(1)}, f32[256,128]{1,0:T(8,128)S(1)}, u32[]{:S(2)}, u32[]{:S(2)}) collective-permute-start(f32[256,128]{1,0:T(8,128)S(1)} %get-tuple-element.17.refs_0_), channel_id=1, source_target_pairs={{0,8},{8,0},{16,24},{24,16},{1,9},{9,1},{17,25},{25,17},{2,10},{10... | collective-permute-start | bytes 393224 | tf_op jit(solution)/shard_map/ppermute | solution.py:24
  32.4 0.5 collective-permute-start.10
  32.9 1.5 %collective-permute-start.9 = (f32[256,128]{1,0:T(8,128)S(1)}, f32[256,128]{1,0:T(8,128)S(1)}, u32[]{:S(2)}, u32[]{:S(2)}) collective-permute-start(f32[256,128]{1,0:T(8,128)S(1)} %get-tuple-element.17.refs_0_), channel_id=1, source_target_pairs={{0,16},{8,24},{16,0},{24,8},{1,17},{9,25},{17,1},{25,9},{2,18},{10... | collective-permute-start | bytes 393224 | tf_op jit(solution)/shard_map/ppermute | solution.py:24
  34.4 0.5 multiply.24.refs_2_
  34.9 2.2 %collective-permute-done.11.refs_1_ = f32[256,128]{1,0:T(8,128)S(1)} collective-permute-done((f32[256,128]{1,0:T(8,128)S(1)}, f32[256,128]{1,0:T(8,128)S(1)}, u32[]{:S(2)}, u32[]{:S(2)}) %collective-permute-start.11) | collective-permute-done | bytes 131104 | tf_op jit(solution)/shard_map/ppermute | solution.py:24
  37.1 1.7 %collective-permute-done.10.refs_0_ = f32[256,128]{1,0:T(8,128)S(1)} collective-permute-done((f32[256,128]{1,0:T(8,128)S(1)}, f32[256,128]{1,0:T(8,128)S(1)}, u32[]{:S(2)}, u32[]{:S(2)}) %collective-permute-start.10) | collective-permute-done | bytes 131104 | tf_op jit(solution)/shard_map/ppermute | solution.py:24
  38.8 0.7 multiply.25.refs_1_
  39.5 0.4 collective-permute-done.9.refs_0_
  39.9 0.3 multiply.29
  40.2 0.1 collective-permute-start.14
  40.3 0.2 multiply.27
  40.5 0.6 collective-permute-start.12
  41.1 0.2 multiply.26
  41.3 0.3 multiply.28
  41.6 0.6 collective-permute-done.12
  42.2 2.5 %collective-permute-start.13 = (f32[256,128]{1,0:T(8,128)S(1)}, f32[256,128]{1,0:T(8,128)S(1)}, u32[]{:S(2)}, u32[]{:S(2)}) collective-permute-start(f32[256,128]{1,0:T(8,128)S(1)} %add.48), channel_id=1, source_target_pairs={{0,6},{1,7},{2,4},{3,5},{4,2},{5,3},{6,0},{7,1},{8,14},{9,15},{10,... | collective-permute-start | bytes 393224 | tf_op jit(solution)/shard_map/ppermute | solution.py:24
  44.9 1.9 %collective-permute-start.16 = (f32[256,128]{1,0:T(8,128)S(1)}, f32[256,128]{1,0:T(8,128)S(1)}, u32[]{:S(2)}, u32[]{:S(2)}) collective-permute-start(f32[256,128]{1,0:T(8,128)S(1)} %get-tuple-element.22), channel_id=1, source_target_pairs={{0,4},{1,5},{2,6},{3,7},{4,0},{5,1},{6,2},{7,3},{8,12},{9,13},{10,... | collective-permute-start | bytes 393224 | tf_op jit(solution)/shard_map/ppermute | solution.py:24
  46.8 3.7 %collective-permute-done.13 = f32[256,128]{1,0:T(8,128)S(1)} collective-permute-done((f32[256,128]{1,0:T(8,128)S(1)}, f32[256,128]{1,0:T(8,128)S(1)}, u32[]{:S(2)}, u32[]{:S(2)}) %collective-permute-start.13) | collective-permute-done | bytes 131104 | tf_op jit(solution)/shard_map/ppermute | solution.py:24
  50.5 4.8 %collective-permute-done.15 = f32[256,128]{1,0:T(8,128)S(1)} collective-permute-done((f32[256,128]{1,0:T(8,128)S(1)}, f32[256,128]{1,0:T(8,128)S(1)}, u32[]{:S(2)}, u32[]{:S(2)}) %collective-permute-start.15) | collective-permute-done | bytes 131104 | tf_op jit(solution)/shard_map/ppermute | solution.py:24
  55.3 0.1 fusion.9.refs_0_
  55.4 1.4 %collective-permute-start.19 = (f32[256,128]{1,0:T(8,128)S(1)}, f32[256,128]{1,0:T(8,128)S(1)}, u32[]{:S(2)}, u32[]{:S(2)}) collective-permute-start(f32[256,128]{1,0:T(8,128)S(1)} %fusion.9.refs_0_), channel_id=1, source_target_pairs={{0,8},{8,0},{16,24},{24,16},{1,9},{9,1},{17,25},{25,17},{2,10},{10... | collective-permute-start | bytes 393224 | tf_op jit(solution)/shard_map/ppermute | solution.py:24
  56.9 1.5 %collective-permute-start.18 = (f32[256,128]{1,0:T(8,128)S(1)}, f32[256,128]{1,0:T(8,128)S(1)}, u32[]{:S(2)}, u32[]{:S(2)}) collective-permute-start(f32[256,128]{1,0:T(8,128)S(1)} %fusion.9.refs_0_), channel_id=1, source_target_pairs={{0,24},{8,16},{16,8},{24,0},{1,25},{9,17},{17,9},{25,1},{2,26},{10... | collective-permute-start | bytes 393224 | tf_op jit(solution)/shard_map/ppermute | solution.py:24
  58.3 0.6 collective-permute-start.17
  59.0 0.5 multiply.30.refs_2_
  59.4 2.2 %collective-permute-done.19.refs_1_ = f32[256,128]{1,0:T(8,128)S(1)} collective-permute-done((f32[256,128]{1,0:T(8,128)S(1)}, f32[256,128]{1,0:T(8,128)S(1)}, u32[]{:S(2)}, u32[]{:S(2)}) %collective-permute-start.19) | collective-permute-done | bytes 131104 | tf_op jit(solution)/shard_map/ppermute | solution.py:24
  61.6 3.0 %collective-permute-done.18.refs_0_ = f32[256,128]{1,0:T(8,128)S(1)} collective-permute-done((f32[256,128]{1,0:T(8,128)S(1)}, f32[256,128]{1,0:T(8,128)S(1)}, u32[]{:S(2)}, u32[]{:S(2)}) %collective-permute-start.18) | collective-permute-done | bytes 131104 | tf_op jit(solution)/shard_map/ppermute | solution.py:24
  64.6 0.7 multiply.31.refs_1_
  65.4 0.6 collective-permute-done.17.refs_0_
  66.0 0.3 multiply.35
  66.3 0.1 collective-permute-start.22
  66.4 0.2 multiply.33
  66.6 0.6 collective-permute-start.20
  67.2 0.2 multiply.32
  67.4 0.3 multiply.34
  67.7 0.6 collective-permute-done.20
  68.3 1.2 %collective-permute-start.21 = (f32[256,128]{1,0:T(8,128)S(1)}, f32[256,128]{1,0:T(8,128)S(1)}, u32[]{:S(2)}, u32[]{:S(2)}) collective-permute-start(f32[256,128]{1,0:T(8,128)S(1)} %add.56), channel_id=1, source_target_pairs={{0,6},{1,7},{2,4},{3,5},{4,2},{5,3},{6,0},{7,1},{8,14},{9,15},{10,... | collective-permute-start | bytes 393224 | tf_op jit(solution)/shard_map/ppermute | solution.py:24
  69.6 0.4 collective-permute-start.23
  70.0 2.9 %collective-permute-start.24 = (f32[256,128]{1,0:T(8,128)S(1)}, f32[256,128]{1,0:T(8,128)S(1)}, u32[]{:S(2)}, u32[]{:S(2)}) collective-permute-start(f32[256,128]{1,0:T(8,128)S(1)} %get-tuple-element.20), channel_id=1, source_target_pairs={{0,4},{1,5},{2,6},{3,7},{4,0},{5,1},{6,2},{7,3},{8,12},{9,13},{10,... | collective-permute-start | bytes 393224 | tf_op jit(solution)/shard_map/ppermute | solution.py:24
  72.9 3.7 %collective-permute-done.21 = f32[256,128]{1,0:T(8,128)S(1)} collective-permute-done((f32[256,128]{1,0:T(8,128)S(1)}, f32[256,128]{1,0:T(8,128)S(1)}, u32[]{:S(2)}, u32[]{:S(2)}) %collective-permute-start.21) | collective-permute-done | bytes 131104 | tf_op jit(solution)/shard_map/ppermute | solution.py:24
  76.6 3.9 %collective-permute-done.23 = f32[256,128]{1,0:T(8,128)S(1)} collective-permute-done((f32[256,128]{1,0:T(8,128)S(1)}, f32[256,128]{1,0:T(8,128)S(1)}, u32[]{:S(2)}, u32[]{:S(2)}) %collective-permute-start.23) | collective-permute-done | bytes 131104 | tf_op jit(solution)/shard_map/ppermute | solution.py:24
  80.5 1.2 %collective-permute-done.24 = f32[256,128]{1,0:T(8,128)S(1)} collective-permute-done((f32[256,128]{1,0:T(8,128)S(1)}, f32[256,128]{1,0:T(8,128)S(1)}, u32[]{:S(2)}, u32[]{:S(2)}) %collective-permute-start.24) | collective-permute-done | bytes 131104 | tf_op jit(solution)/shard_map/ppermute | solution.py:24
  81.7 0.7 fusion.4
  (23 shorter events, 0.4 us)
Async XLA Ops:
  0.0 4.5 %copy-start.2 = (s32[16,8]{0,1:T(8,128)S(1)}, s32[16,8]{0,1:T(8,128)}, u32[]{:S(2)}) copy-start(s32[16,8]{0,1:T(8,128)} %param.7) | copy-start | bytes 1540
  0.0 4.5 %copy-start.1 = (s32[16,8]{0,1:T(8,128)S(1)}, s32[16,8]{0,1:T(8,128)}, u32[]{:S(2)}) copy-start(s32[16,8]{0,1:T(8,128)} %param.6) | copy-start | bytes 1540
  0.0 7.8 %collective-permute-start.2 = (f32[256,128]{1,0:T(8,128)}, f32[256,128]{1,0:T(8,128)S(1)}, u32[]{:S(2)}, u32[]{:S(2)}) collective-permute-start(f32[256,128]{1,0:T(8,128)} %refs_4_.1), channel_id=1, source_target_pairs={{0,8},{8,0},{16,24},{24,16},{1,9},{9,1},{17,25},{25,17},{2,10},{10... | collective-permute-start | bytes 393224 | tf_op jit(solution)/shard_map/ppermute | solution.py:24
  3.0 7.8 %collective-permute-start.1 = (f32[256,128]{1,0:T(8,128)}, f32[256,128]{1,0:T(8,128)S(1)}, u32[]{:S(2)}, u32[]{:S(2)}) collective-permute-start(f32[256,128]{1,0:T(8,128)} %refs_4_.1), channel_id=1, source_target_pairs={{0,24},{8,16},{16,8},{24,0},{1,25},{9,17},{17,9},{25,1},{2,26},{10... | collective-permute-start | bytes 393224 | tf_op jit(solution)/shard_map/ppermute | solution.py:24
  4.5 7.7 %collective-permute-start = (f32[256,128]{1,0:T(8,128)}, f32[256,128]{1,0:T(8,128)S(1)}, u32[]{:S(2)}, u32[]{:S(2)}) collective-permute-start(f32[256,128]{1,0:T(8,128)} %refs_4_.1), channel_id=1, source_target_pairs={{0,16},{8,24},{16,0},{24,8},{1,17},{9,25},{17,1},{25,9},{2,18},{10... | collective-permute-start | bytes 393224 | tf_op jit(solution)/shard_map/ppermute | solution.py:24
  4.5 2.8 %copy-start = (f32[256,128]{1,0:T(8,128)S(1)}, f32[256,128]{1,0:T(8,128)}, u32[]{:S(2)}) copy-start(f32[256,128]{1,0:T(8,128)} %refs_4_.1) | copy-start | bytes 393220
  12.4 6.3 %collective-permute-start.6 = (f32[768,128]{1,0:T(8,128)S(1)}, f32[768,128]{1,0:T(8,128)S(1)}, u32[]{:S(2)}, u32[]{:S(2)}) collective-permute-start(f32[768,128]{1,0:T(8,128)S(1)} %multiply.23), channel_id=1, source_target_pairs={{0,1},{1,0},{2,3},{3,2},{4,5},{5,4},{6,7},{7,6},{8,9},{9,8},{10,11... | collective-permute-start | bytes 1179656 | tf_op jit(solution)/shard_map/ppermute | solution.py:24
  12.7 2.3 %collective-permute-start.3 = (f32[256,128]{1,0:T(8,128)S(1)}, f32[256,128]{1,0:T(8,128)S(1)}, u32[]{:S(2)}, u32[]{:S(2)}) collective-permute-start(f32[256,128]{1,0:T(8,128)S(1)} %multiply.21), channel_id=1, source_target_pairs={{0,1},{1,0},{2,3},{3,2},{4,5},{5,4},{6,7},{7,6},{8,9},{9,8},{10,11... | collective-permute-start | bytes 393224 | tf_op jit(solution)/shard_map/ppermute | solution.py:24
  13.8 1.2 %collective-permute-start.4 = (f32[32,128]{1,0:T(8,128)S(1)}, f32[32,128]{1,0:T(8,128)S(1)}, u32[]{:S(2)}, u32[]{:S(2)}) collective-permute-start(f32[32,128]{1,0:T(8,128)S(1)} %slice.52), channel_id=1, source_target_pairs={{0,1},{1,0},{2,3},{3,2},{4,5},{5,4},{6,7},{7,6},{8,9},{9,8},{10,11... | collective-permute-start | bytes 49160 | tf_op jit(solution)/shard_map/ppermute | solution.py:24
  15.1 8.4 %collective-permute-start.5 = (f32[264,128]{1,0:T(8,128)S(1)}, f32[264,128]{1,0:T(8,128)S(1)}, u32[]{:S(2)}, u32[]{:S(2)}) collective-permute-start(f32[264,128]{1,0:T(8,128)S(1)} %combine.2), channel_id=1, source_target_pairs={{0,6},{1,7},{2,4},{3,5},{4,2},{5,3},{6,0},{7,1},{8,14},{9,15},{10,... | collective-permute-start | bytes 405512 | tf_op jit(solution)/shard_map/ppermute | solution.py:24
  18.8 7.9 %collective-permute-start.7 = (f32[264,128]{1,0:T(8,128)S(1)}, f32[264,128]{1,0:T(8,128)S(1)}, u32[]{:S(2)}, u32[]{:S(2)}) collective-permute-start(f32[264,128]{1,0:T(8,128)S(1)} %get-tuple-element.14), channel_id=1, source_target_pairs={{0,2},{1,3},{2,0},{3,1},{4,6},{5,7},{6,4},{7,5},{8,10},{9,11},{10,... | collective-permute-start | bytes 405512 | tf_op jit(solution)/shard_map/ppermute | solution.py:24
  18.9 11.6 %collective-permute-start.8 = (f32[264,128]{1,0:T(8,128)S(1)}, f32[264,128]{1,0:T(8,128)S(1)}, u32[]{:S(2)}, u32[]{:S(2)}) collective-permute-start(f32[264,128]{1,0:T(8,128)S(1)} %get-tuple-element.15), channel_id=1, source_target_pairs={{0,4},{1,5},{2,6},{3,7},{4,0},{5,1},{6,2},{7,3},{8,12},{9,13},{10,... | collective-permute-start | bytes 405512 | tf_op jit(solution)/shard_map/ppermute | solution.py:24
  30.9 6.2 %collective-permute-start.11 = (f32[256,128]{1,0:T(8,128)S(1)}, f32[256,128]{1,0:T(8,128)S(1)}, u32[]{:S(2)}, u32[]{:S(2)}) collective-permute-start(f32[256,128]{1,0:T(8,128)S(1)} %get-tuple-element.17.refs_0_), channel_id=1, source_target_pairs={{0,8},{8,0},{16,24},{24,16},{1,9},{9,1},{17,25},{25,17},{2,10},{10... | collective-permute-start | bytes 393224 | tf_op jit(solution)/shard_map/ppermute | solution.py:24
  32.4 6.3 %collective-permute-start.10 = (f32[256,128]{1,0:T(8,128)S(1)}, f32[256,128]{1,0:T(8,128)S(1)}, u32[]{:S(2)}, u32[]{:S(2)}) collective-permute-start(f32[256,128]{1,0:T(8,128)S(1)} %get-tuple-element.17.refs_0_), channel_id=1, source_target_pairs={{0,24},{8,16},{16,8},{24,0},{1,25},{9,17},{17,9},{25,1},{2,26},{10... | collective-permute-start | bytes 393224 | tf_op jit(solution)/shard_map/ppermute | solution.py:24
  32.9 7.0 %collective-permute-start.9 = (f32[256,128]{1,0:T(8,128)S(1)}, f32[256,128]{1,0:T(8,128)S(1)}, u32[]{:S(2)}, u32[]{:S(2)}) collective-permute-start(f32[256,128]{1,0:T(8,128)S(1)} %get-tuple-element.17.refs_0_), channel_id=1, source_target_pairs={{0,16},{8,24},{16,0},{24,8},{1,17},{9,25},{17,1},{25,9},{2,18},{10... | collective-permute-start | bytes 393224 | tf_op jit(solution)/shard_map/ppermute | solution.py:24
  40.2 4.5 %collective-permute-start.14 = (f32[768,128]{1,0:T(8,128)S(1)}, f32[768,128]{1,0:T(8,128)S(1)}, u32[]{:S(2)}, u32[]{:S(2)}) collective-permute-start(f32[768,128]{1,0:T(8,128)S(1)} %multiply.29), channel_id=1, source_target_pairs={{0,1},{1,0},{2,3},{3,2},{4,5},{5,4},{6,7},{7,6},{8,9},{9,8},{10,11... | collective-permute-start | bytes 1179656 | tf_op jit(solution)/shard_map/ppermute | solution.py:24
  40.5 1.7 %collective-permute-start.12 = (f32[256,128]{1,0:T(8,128)S(1)}, f32[256,128]{1,0:T(8,128)S(1)}, u32[]{:S(2)}, u32[]{:S(2)}) collective-permute-start(f32[256,128]{1,0:T(8,128)S(1)} %multiply.27), channel_id=1, source_target_pairs={{0,1},{1,0},{2,3},{3,2},{4,5},{5,4},{6,7},{7,6},{8,9},{9,8},{10,11... | collective-permute-start | bytes 393224 | tf_op jit(solution)/shard_map/ppermute | solution.py:24
  42.2 8.3 %collective-permute-start.13 = (f32[256,128]{1,0:T(8,128)S(1)}, f32[256,128]{1,0:T(8,128)S(1)}, u32[]{:S(2)}, u32[]{:S(2)}) collective-permute-start(f32[256,128]{1,0:T(8,128)S(1)} %add.48), channel_id=1, source_target_pairs={{0,6},{1,7},{2,4},{3,5},{4,2},{5,3},{6,0},{7,1},{8,14},{9,15},{10,... | collective-permute-start | bytes 393224 | tf_op jit(solution)/shard_map/ppermute | solution.py:24
  44.8 10.5 %collective-permute-start.15 = (f32[256,128]{1,0:T(8,128)S(1)}, f32[256,128]{1,0:T(8,128)S(1)}, u32[]{:S(2)}, u32[]{:S(2)}) collective-permute-start(f32[256,128]{1,0:T(8,128)S(1)} %get-tuple-element.21), channel_id=1, source_target_pairs={{0,2},{1,3},{2,0},{3,1},{4,6},{5,7},{6,4},{7,5},{8,10},{9,11},{10,... | collective-permute-start | bytes 393224 | tf_op jit(solution)/shard_map/ppermute | solution.py:24
  44.9 10.4 %collective-permute-start.16 = (f32[256,128]{1,0:T(8,128)S(1)}, f32[256,128]{1,0:T(8,128)S(1)}, u32[]{:S(2)}, u32[]{:S(2)}) collective-permute-start(f32[256,128]{1,0:T(8,128)S(1)} %get-tuple-element.22), channel_id=1, source_target_pairs={{0,4},{1,5},{2,6},{3,7},{4,0},{5,1},{6,2},{7,3},{8,12},{9,13},{10,... | collective-permute-start | bytes 393224 | tf_op jit(solution)/shard_map/ppermute | solution.py:24
  55.4 6.2 %collective-permute-start.19 = (f32[256,128]{1,0:T(8,128)S(1)}, f32[256,128]{1,0:T(8,128)S(1)}, u32[]{:S(2)}, u32[]{:S(2)}) collective-permute-start(f32[256,128]{1,0:T(8,128)S(1)} %fusion.9.refs_0_), channel_id=1, source_target_pairs={{0,8},{8,0},{16,24},{24,16},{1,9},{9,1},{17,25},{25,17},{2,10},{10... | collective-permute-start | bytes 393224 | tf_op jit(solution)/shard_map/ppermute | solution.py:24
  56.9 7.8 %collective-permute-start.18 = (f32[256,128]{1,0:T(8,128)S(1)}, f32[256,128]{1,0:T(8,128)S(1)}, u32[]{:S(2)}, u32[]{:S(2)}) collective-permute-start(f32[256,128]{1,0:T(8,128)S(1)} %fusion.9.refs_0_), channel_id=1, source_target_pairs={{0,24},{8,16},{16,8},{24,0},{1,25},{9,17},{17,9},{25,1},{2,26},{10... | collective-permute-start | bytes 393224 | tf_op jit(solution)/shard_map/ppermute | solution.py:24
  58.3 7.7 %collective-permute-start.17 = (f32[256,128]{1,0:T(8,128)S(1)}, f32[256,128]{1,0:T(8,128)S(1)}, u32[]{:S(2)}, u32[]{:S(2)}) collective-permute-start(f32[256,128]{1,0:T(8,128)S(1)} %fusion.9.refs_0_), channel_id=1, source_target_pairs={{0,16},{8,24},{16,0},{24,8},{1,17},{9,25},{17,1},{25,9},{2,18},{10... | collective-permute-start | bytes 393224 | tf_op jit(solution)/shard_map/ppermute | solution.py:24
  66.3 3.2 %collective-permute-start.22 = (f32[768,128]{1,0:T(8,128)S(1)}, f32[768,128]{1,0:T(8,128)S(1)}, u32[]{:S(2)}, u32[]{:S(2)}) collective-permute-start(f32[768,128]{1,0:T(8,128)S(1)} %multiply.35), channel_id=1, source_target_pairs={{0,1},{1,0},{2,3},{3,2},{4,5},{5,4},{6,7},{7,6},{8,9},{9,8},{10,11... | collective-permute-start | bytes 1179656 | tf_op jit(solution)/shard_map/ppermute | solution.py:24
  66.6 1.7 %collective-permute-start.20 = (f32[256,128]{1,0:T(8,128)S(1)}, f32[256,128]{1,0:T(8,128)S(1)}, u32[]{:S(2)}, u32[]{:S(2)}) collective-permute-start(f32[256,128]{1,0:T(8,128)S(1)} %multiply.33), channel_id=1, source_target_pairs={{0,1},{1,0},{2,3},{3,2},{4,5},{5,4},{6,7},{7,6},{8,9},{9,8},{10,11... | collective-permute-start | bytes 393224 | tf_op jit(solution)/shard_map/ppermute | solution.py:24
  68.3 8.3 %collective-permute-start.21 = (f32[256,128]{1,0:T(8,128)S(1)}, f32[256,128]{1,0:T(8,128)S(1)}, u32[]{:S(2)}, u32[]{:S(2)}) collective-permute-start(f32[256,128]{1,0:T(8,128)S(1)} %add.56), channel_id=1, source_target_pairs={{0,6},{1,7},{2,4},{3,5},{4,2},{5,3},{6,0},{7,1},{8,14},{9,15},{10,... | collective-permute-start | bytes 393224 | tf_op jit(solution)/shard_map/ppermute | solution.py:24
  69.6 10.9 %collective-permute-start.23 = (f32[256,128]{1,0:T(8,128)S(1)}, f32[256,128]{1,0:T(8,128)S(1)}, u32[]{:S(2)}, u32[]{:S(2)}) collective-permute-start(f32[256,128]{1,0:T(8,128)S(1)} %get-tuple-element.19), channel_id=1, source_target_pairs={{0,2},{1,3},{2,0},{3,1},{4,6},{5,7},{6,4},{7,5},{8,10},{9,11},{10,... | collective-permute-start | bytes 393224 | tf_op jit(solution)/shard_map/ppermute | solution.py:24
  70.0 11.7 %collective-permute-start.24 = (f32[256,128]{1,0:T(8,128)S(1)}, f32[256,128]{1,0:T(8,128)S(1)}, u32[]{:S(2)}, u32[]{:S(2)}) collective-permute-start(f32[256,128]{1,0:T(8,128)S(1)} %get-tuple-element.20), channel_id=1, source_target_pairs={{0,4},{1,5},{2,6},{3,7},{4,0},{5,1},{6,2},{7,3},{8,12},{9,13},{10,... | collective-permute-start | bytes 393224 | tf_op jit(solution)/shard_map/ppermute | solution.py:24

commit v7 on v6

--- a/solution.py
+++ b/solution.py
@@ -9,6 +9,7 @@
 
 
 STEPS = 3
+STAGGER = 35
 TILE = 128
 EPSILON = 1e-05
 RETAIN = 0.8
@@ -24,11 +25,21 @@
     return lax.ppermute(array, axis, [(i, i ^ offset) for i in range(size)])
 
 
+def swap_far(array, size, offsets):
+    return lax.ppermute(array, "col", [(i, i ^ (2 * offsets[i % 2])) for i in range(size)])
+
+
 def prepare_kernel(offsets, near, fence_ref, present_ref, power_ref, value_ref, out_ref, energy_ref, held, scales, arrived):
     blocks, span, _ = held.shape
     parts, chunks = span // TILE, len(near)
     row, col = lax.axis_index("row"), lax.axis_index("col")
-    sources = [col ^ (2 * offset + 1 - side) for side in range(2) for offset in offsets]
+    odd = lax.rem(col, 2)
+    sources = []
+    for side in range(2):
+        core = odd if side else 1 - odd
+        for even_offset, odd_offset in offsets:
+            offset = even_offset + core * (odd_offset - even_offset)
+            sources.append(col ^ (2 * offset + 1 - side))
 
     def copy(i, chunk):
         rows = pl.ds(pl.multiple_of(sources[i] * span, span), span)
@@ -239,11 +250,37 @@
 
 
 def near_offsets(size):
-    return [size - 1] + list(range(1, size - 1))
+    return list(range(size - 2, 0, -1)) + [size - 1]
 
 
 def far_offsets(groups):
-    return [groups - 1] + list(range(1, groups - 1)) + [0] if groups > 1 else [0]
+    even = list(range(groups - 1, -1, -1))
+    odd = [groups - 1] + list(range(1, groups - 1)) + [0]
+    return list(zip(even, odd))
+
+
+def stagger_kernel(in_ref, out_ref, done):
+    count = 1 + lax.rem(lax.axis_index("col"), 2) * STAGGER
+
+    def body(i, carry):
+        copy = pltpu.make_async_copy(in_ref, out_ref, done)
+        copy.start()
+        copy.wait()
+        return carry
+
+    lax.fori_loop(0, count, body, 0)
+
+
+def stagger(array):
+    return pl.pallas_call(
+        stagger_kernel,
+        out_shape=jax.ShapeDtypeStruct(array.shape, array.dtype),
+        in_specs=[VMEM],
+        out_specs=VMEM,
+        scratch_shapes=[pltpu.SemaphoreType.DMA],
+        compiler_params=params(4),
+        name="stagger",
+    )(array)
 
 
 def shards(source, value, occupancy, exponent):
@@ -284,10 +321,11 @@
                 for d in range(count):
                     rows = slice(d * span, (d + 1) * span)
                     sums.append(mine[rows] + moved[i][rows])
-        parts = [
-            swap(part, "col", col_size, 2 * offset) if offset else part
-            for offset, part in zip(offsets, sums)
-        ]
+        if step < STEPS - 1:
+            sums[0] = stagger(sums[0])
+        parts = sums[-1:]
+        for i in range(groups - 1):
+            parts.append(swap_far(sums[i], col_size, offsets[i]))
         if step == 0:
             current, inverse = finish(nodes, parts, source)
         else:

time: 82.6 us -> 79.6 us (0.964)
  waiting for transfers between devices: 43.9 us -> 35 us
  starting transfers between devices: 27.1 us -> 32.6 us
    ppermute x25 -> x16, waiting for transfers between devices: 43.9 us -> 13.4 us  [swap(): return lax.ppermute(array, axis, [(i, i ^ offset) for i in range(size)])]
    ppermute x0 -> x9, waiting for transfers between devices: none -> 21.6 us  [swap_far(): lax.ppermute(array, 'col', [(i, i ^ 2 * offsets[i % 2]) for i in range(si...]
    ppermute x0 -> x9, starting transfers between devices: none -> 13.5 us  [swap_far(): lax.ppermute(array, 'col', [(i, i ^ 2 * offsets[i % 2]) for i in range(si...]
    ppermute x25 -> x16, starting transfers between devices: 27.1 us -> 19.1 us  [swap(): return lax.ppermute(array, axis, [(i, i ^ offset) for i in range(size)])]
  transfers between devices with their start and end apart: 25 -> 25, of which waited for: 19 -> 16; matrix products, arithmetic and copies ran while one was open for 0% -> 0% of each run, Pallas kernels for 11% -> 12%
where the time goes in v7:
time: 79.6 us; the launch traced here: 79.5 us
  waiting for transfers between devices  35 us (44%)
  starting transfers between devices  32.6 us (41%)
  Pallas kernels  10.7 us (13%)
  other arithmetic  0.9 us (1%)
    ppermute x9, waiting for transfers between devices, swap_far(): lax.ppermute(array, 'col', [(i, i ^ 2 * offsets[i % 2]) for i in range(si...  21.6 us
    ppermute x16, starting transfers between devices, swap(): return lax.ppermute(array, axis, [(i, i ^ offset) for i in range(size)])  19.1 us
    ppermute x9, starting transfers between devices, swap_far(): lax.ppermute(array, 'col', [(i, i ^ 2 * offsets[i % 2]) for i in range(si...  13.5 us
    ppermute x16, waiting for transfers between devices, swap(): return lax.ppermute(array, axis, [(i, i ^ offset) for i in range(size)])  13.4 us
    pallas_call x18, Pallas kernels, multiply(): pl.pallas_call(functools.partial(multiply_kernel, first_row, first, count...  6.54 us
    pallas_call x1, Pallas kernels, prepare(): pl.pallas_call(functools.partial(prepare_kernel, offsets, near), in_specs...  2.77 us
  transfers between devices with their start and end apart: 25, of which 16 were waited for; matrix products, arithmetic and copies ran while one was open for 0% of the time, Pallas kernels for 12%

profile of v7, /device:TPU:0, one launch (start us, length us, event | category | flops | bytes accessed | tf_op | source)
XLA Modules:
  0.0 79.5 jit_solution(7348580855105710293)
XLA Ops:
  0.0 3.0 %collective-permute-start.2 = (f32[256,128]{1,0:T(8,128)}, f32[256,128]{1,0:T(8,128)S(1)}, u32[]{:S(2)}, u32[]{:S(2)}) collective-permute-start(f32[256,128]{1,0:T(8,128)} %refs_4_.1), channel_id=1, source_target_pairs={{0,8},{8,0},{16,24},{24,16},{1,9},{9,1},{17,25},{25,17},{2,10},{10... | collective-permute-start | bytes 393224 | tf_op jit(solution)/shard_map/ppermute | solution.py:25
  3.0 1.5 %collective-permute-start.1 = (f32[256,128]{1,0:T(8,128)}, f32[256,128]{1,0:T(8,128)S(1)}, u32[]{:S(2)}, u32[]{:S(2)}) collective-permute-start(f32[256,128]{1,0:T(8,128)} %refs_4_.1), channel_id=1, source_target_pairs={{0,16},{8,24},{16,0},{24,8},{1,17},{9,25},{17,1},{25,9},{2,18},{10... | collective-permute-start | bytes 393224 | tf_op jit(solution)/shard_map/ppermute | solution.py:25
  4.5 2.8 %prepare.1 = (bf16[2048,1024]{1,0:T(8,128)(2,1)S(1)}, f32[2048,128]{1,0:T(8,128)S(1)}) custom-call(f32[8,128]{1,0:T(8,128)S(1)} %fence.1.fence_ref, s32[8,16]{1,0:T(8,128)S(1)} %bitcast.2, s32[8,16]{1,0:T(8,128)S(1)} %bitcast.3, bf16[2048,1024]{1,0:T(8,128)(2,1)} %value_ref.1), custom_call_target="tpu_custom_call" | custom-call | tf_op jit(solution)/shard_map/prepare/pallas_call | solution.py:85
  7.3 0.5 multiply.18.refs_2_
  7.8 3.2 %collective-permute-done.1.refs_0_ = f32[256,128]{1,0:T(8,128)S(1)} collective-permute-done((f32[256,128]{1,0:T(8,128)}, f32[256,128]{1,0:T(8,128)S(1)}, u32[]{:S(2)}, u32[]{:S(2)}) %collective-permute-start.1) | collective-permute-done | bytes 131104 | tf_op jit(solution)/shard_map/ppermute | solution.py:25
  11.0 0.7 multiply.19.refs_1_
  11.7 0.3 multiply.21
  12.0 0.1 collective-permute-start.3
  12.1 0.2 multiply.23
  12.3 0.6 collective-permute-start.5
  12.9 0.5 energy.1.energy_ref
  13.4 0.2 multiply.22.mine_ref
  13.7 0.3 multiply.20.mine_ref
  13.9 0.7 collective-permute-done.4.energy_moved_ref
  14.6 0.2 stagger.2
  14.8 3.7 %collective-permute-start.6 = (f32[264,128]{1,0:T(8,128)S(1)}, f32[264,128]{1,0:T(8,128)S(1)}, u32[]{:S(2)}, u32[]{:S(2)}) collective-permute-start(f32[264,128]{1,0:T(8,128)S(1)} %stagger.2), channel_id=1, source_target_pairs={{0,6},{1,7},{2,4},{3,5},{4,2},{5,3},{6,0},{7,1},{8,14},{9,15},{10,... | collective-permute-start | bytes 405512 | tf_op jit(solution)/shard_map/ppermute | solution.py:29
  18.6 0.1 collective-permute-start.7
  18.6 0.8 collective-permute-start.8
  19.4 2.4 %collective-permute-done.6.refs_1_ = f32[264,128]{1,0:T(8,128)S(1)} collective-permute-done((f32[264,128]{1,0:T(8,128)S(1)}, f32[264,128]{1,0:T(8,128)S(1)}, u32[]{:S(2)}, u32[]{:S(2)}) %collective-permute-start.6) | collective-permute-done | bytes 135200 | tf_op jit(solution)/shard_map/ppermute | solution.py:29
  21.8 3.8 %collective-permute-done.7.refs_2_ = f32[264,128]{1,0:T(8,128)S(1)} collective-permute-done((f32[264,128]{1,0:T(8,128)S(1)}, f32[264,128]{1,0:T(8,128)S(1)}, u32[]{:S(2)}, u32[]{:S(2)}) %collective-permute-start.7) | collective-permute-done | bytes 135200 | tf_op jit(solution)/shard_map/ppermute | solution.py:29
  25.6 0.4 finish.1
  26.0 0.5 collective-permute-start.11
  26.5 1.6 %collective-permute-start.10 = (f32[256,128]{1,0:T(8,128)S(1)}, f32[256,128]{1,0:T(8,128)S(1)}, u32[]{:S(2)}, u32[]{:S(2)}) collective-permute-start(f32[256,128]{1,0:T(8,128)S(1)} %get-tuple-element.17.refs_0_), channel_id=1, source_target_pairs={{0,16},{8,24},{16,0},{24,8},{1,17},{9,25},{17,1},{25,9},{2,18},{10... | collective-permute-start | bytes 393224 | tf_op jit(solution)/shard_map/ppermute | solution.py:25
  28.1 1.4 %collective-permute-start.9 = (f32[256,128]{1,0:T(8,128)S(1)}, f32[256,128]{1,0:T(8,128)S(1)}, u32[]{:S(2)}, u32[]{:S(2)}) collective-permute-start(f32[256,128]{1,0:T(8,128)S(1)} %get-tuple-element.17.refs_0_), channel_id=1, source_target_pairs={{0,24},{8,16},{16,8},{24,0},{1,25},{9,17},{17,9},{25,1},{2,26},{10... | collective-permute-start | bytes 393224 | tf_op jit(solution)/shard_map/ppermute | solution.py:25
  29.5 0.5 multiply.24.refs_2_
  30.0 1.0 %collective-permute-done.11.refs_1_ = f32[256,128]{1,0:T(8,128)S(1)} collective-permute-done((f32[256,128]{1,0:T(8,128)S(1)}, f32[256,128]{1,0:T(8,128)S(1)}, u32[]{:S(2)}, u32[]{:S(2)}) %collective-permute-start.11) | collective-permute-done | bytes 131104 | tf_op jit(solution)/shard_map/ppermute | solution.py:25
  31.0 0.5 collective-permute-done.10.refs_0_
  31.5 0.7 multiply.25.refs_1_
  32.2 1.7 %collective-permute-done.9.refs_0_ = f32[256,128]{1,0:T(8,128)S(1)} collective-permute-done((f32[256,128]{1,0:T(8,128)S(1)}, f32[256,128]{1,0:T(8,128)S(1)}, u32[]{:S(2)}, u32[]{:S(2)}) %collective-permute-start.9) | collective-permute-done | bytes 131104 | tf_op jit(solution)/shard_map/ppermute | solution.py:25
  34.0 0.3 multiply.27
  34.3 3.9 %collective-permute-start.12 = (f32[768,128]{1,0:T(8,128)S(1)}, f32[768,128]{1,0:T(8,128)S(1)}, u32[]{:S(2)}, u32[]{:S(2)}) collective-permute-start(f32[768,128]{1,0:T(8,128)S(1)} %multiply.27), channel_id=1, source_target_pairs={{0,1},{1,0},{2,3},{3,2},{4,5},{5,4},{6,7},{7,6},{8,9},{9,8},{10,11... | collective-permute-start | bytes 1179656 | tf_op jit(solution)/shard_map/ppermute | solution.py:25
  38.2 0.2 multiply.29
  38.4 0.1 collective-permute-start.13
  38.5 0.2 multiply.28
  38.7 0.3 multiply.26
  39.0 0.8 %collective-permute-done.13 = f32[256,128]{1,0:T(8,128)S(1)} collective-permute-done((f32[256,128]{1,0:T(8,128)S(1)}, f32[256,128]{1,0:T(8,128)S(1)}, u32[]{:S(2)}, u32[]{:S(2)}) %collective-permute-start.13) | collective-permute-done | bytes 131104 | tf_op jit(solution)/shard_map/ppermute | solution.py:25
  39.8 0.2 stagger.3
  40.0 1.3 %collective-permute-start.14 = (f32[256,128]{1,0:T(8,128)S(1)}, f32[256,128]{1,0:T(8,128)S(1)}, u32[]{:S(2)}, u32[]{:S(2)}) collective-permute-start(f32[256,128]{1,0:T(8,128)S(1)} %stagger.3), channel_id=1, source_target_pairs={{0,6},{1,7},{2,4},{3,5},{4,2},{5,3},{6,0},{7,1},{8,14},{9,15},{10,... | collective-permute-start | bytes 393224 | tf_op jit(solution)/shard_map/ppermute | solution.py:29
  41.4 0.6 collective-permute-start.15
  41.9 2.6 %collective-permute-start.16 = (f32[256,128]{1,0:T(8,128)S(1)}, f32[256,128]{1,0:T(8,128)S(1)}, u32[]{:S(2)}, u32[]{:S(2)}) collective-permute-start(f32[256,128]{1,0:T(8,128)S(1)} %get-tuple-element.22), channel_id=1, source_target_pairs={{0,2},{1,5},{2,0},{3,7},{4,6},{5,1},{6,4},{7,3},{8,10},{9,13},{10,... | collective-permute-start | bytes 393224 | tf_op jit(solution)/shard_map/ppermute | solution.py:29
  44.6 2.5 %collective-permute-done.14 = f32[256,128]{1,0:T(8,128)S(1)} collective-permute-done((f32[256,128]{1,0:T(8,128)S(1)}, f32[256,128]{1,0:T(8,128)S(1)}, u32[]{:S(2)}, u32[]{:S(2)}) %collective-permute-start.14) | collective-permute-done | bytes 131104 | tf_op jit(solution)/shard_map/ppermute | solution.py:29
  47.0 3.2 %collective-permute-done.15 = f32[256,128]{1,0:T(8,128)S(1)} collective-permute-done((f32[256,128]{1,0:T(8,128)S(1)}, f32[256,128]{1,0:T(8,128)S(1)}, u32[]{:S(2)}, u32[]{:S(2)}) %collective-permute-start.15) | collective-permute-done | bytes 131104 | tf_op jit(solution)/shard_map/ppermute | solution.py:29
  50.2 0.1 fusion.13.refs_0_
  50.3 1.5 %collective-permute-start.19 = (f32[256,128]{1,0:T(8,128)S(1)}, f32[256,128]{1,0:T(8,128)S(1)}, u32[]{:S(2)}, u32[]{:S(2)}) collective-permute-start(f32[256,128]{1,0:T(8,128)S(1)} %fusion.13.refs_0_), channel_id=1, source_target_pairs={{0,8},{8,0},{16,24},{24,16},{1,9},{9,1},{17,25},{25,17},{2,10},{10... | collective-permute-start | bytes 393224 | tf_op jit(solution)/shard_map/ppermute | solution.py:25
  51.8 1.6 %collective-permute-start.18 = (f32[256,128]{1,0:T(8,128)S(1)}, f32[256,128]{1,0:T(8,128)S(1)}, u32[]{:S(2)}, u32[]{:S(2)}) collective-permute-start(f32[256,128]{1,0:T(8,128)S(1)} %fusion.13.refs_0_), channel_id=1, source_target_pairs={{0,16},{8,24},{16,0},{24,8},{1,17},{9,25},{17,1},{25,9},{2,18},{10... | collective-permute-start | bytes 393224 | tf_op jit(solution)/shard_map/ppermute | solution.py:25
  53.4 0.5 collective-permute-start.17
  53.9 0.5 multiply.30.refs_2_
  54.3 1.0 %collective-permute-done.19.refs_1_ = f32[256,128]{1,0:T(8,128)S(1)} collective-permute-done((f32[256,128]{1,0:T(8,128)S(1)}, f32[256,128]{1,0:T(8,128)S(1)}, u32[]{:S(2)}, u32[]{:S(2)}) %collective-permute-start.19) | collective-permute-done | bytes 131104 | tf_op jit(solution)/shard_map/ppermute | solution.py:25
  55.3 1.5 %collective-permute-done.18.refs_0_ = f32[256,128]{1,0:T(8,128)S(1)} collective-permute-done((f32[256,128]{1,0:T(8,128)S(1)}, f32[256,128]{1,0:T(8,128)S(1)}, u32[]{:S(2)}, u32[]{:S(2)}) %collective-permute-start.18) | collective-permute-done | bytes 131104 | tf_op jit(solution)/shard_map/ppermute | solution.py:25
  56.8 0.7 multiply.31.refs_1_
  57.6 2.2 %collective-permute-done.17.refs_0_ = f32[256,128]{1,0:T(8,128)S(1)} collective-permute-done((f32[256,128]{1,0:T(8,128)S(1)}, f32[256,128]{1,0:T(8,128)S(1)}, u32[]{:S(2)}, u32[]{:S(2)}) %collective-permute-start.17) | collective-permute-done | bytes 131104 | tf_op jit(solution)/shard_map/ppermute | solution.py:25
  59.7 0.3 multiply.33
  60.0 2.8 %collective-permute-start.20 = (f32[768,128]{1,0:T(8,128)S(1)}, f32[768,128]{1,0:T(8,128)S(1)}, u32[]{:S(2)}, u32[]{:S(2)}) collective-permute-start(f32[768,128]{1,0:T(8,128)S(1)} %multiply.33), channel_id=1, source_target_pairs={{0,1},{1,0},{2,3},{3,2},{4,5},{5,4},{6,7},{7,6},{8,9},{9,8},{10,11... | collective-permute-start | bytes 1179656 | tf_op jit(solution)/shard_map/ppermute | solution.py:25
  62.8 0.2 multiply.35
  63.0 0.1 collective-permute-start.21
  63.1 0.2 multiply.34
  63.3 0.3 multiply.32
  63.6 0.8 %collective-permute-done.21 = f32[256,128]{1,0:T(8,128)S(1)} collective-permute-done((f32[256,128]{1,0:T(8,128)S(1)}, f32[256,128]{1,0:T(8,128)S(1)}, u32[]{:S(2)}, u32[]{:S(2)}) %collective-permute-start.21) | collective-permute-done | bytes 131104 | tf_op jit(solution)/shard_map/ppermute | solution.py:25
  64.4 2.3 %collective-permute-start.22 = (f32[256,128]{1,0:T(8,128)S(1)}, f32[256,128]{1,0:T(8,128)S(1)}, u32[]{:S(2)}, u32[]{:S(2)}) collective-permute-start(f32[256,128]{1,0:T(8,128)S(1)} %add.57), channel_id=1, source_target_pairs={{0,6},{1,7},{2,4},{3,5},{4,2},{5,3},{6,0},{7,1},{8,14},{9,15},{10,... | collective-permute-start | bytes 393224 | tf_op jit(solution)/shard_map/ppermute | solution.py:29
  66.8 0.1 collective-permute-start.23
  66.9 2.1 %collective-permute-start.24 = (f32[256,128]{1,0:T(8,128)S(1)}, f32[256,128]{1,0:T(8,128)S(1)}, u32[]{:S(2)}, u32[]{:S(2)}) collective-permute-start(f32[256,128]{1,0:T(8,128)S(1)} %get-tuple-element.20), channel_id=1, source_target_pairs={{0,2},{1,5},{2,0},{3,7},{4,6},{5,1},{6,4},{7,3},{8,10},{9,13},{10,... | collective-permute-start | bytes 393224 | tf_op jit(solution)/shard_map/ppermute | solution.py:29
  69.0 3.7 %collective-permute-done.22 = f32[256,128]{1,0:T(8,128)S(1)} collective-permute-done((f32[256,128]{1,0:T(8,128)S(1)}, f32[256,128]{1,0:T(8,128)S(1)}, u32[]{:S(2)}, u32[]{:S(2)}) %collective-permute-start.22) | collective-permute-done | bytes 131104 | tf_op jit(solution)/shard_map/ppermute | solution.py:29
  72.7 6.1 %collective-permute-done.23 = f32[256,128]{1,0:T(8,128)S(1)} collective-permute-done((f32[256,128]{1,0:T(8,128)S(1)}, f32[256,128]{1,0:T(8,128)S(1)}, u32[]{:S(2)}, u32[]{:S(2)}) %collective-permute-start.23) | collective-permute-done | bytes 131104 | tf_op jit(solution)/shard_map/ppermute | solution.py:29
  78.8 0.7 fusion.6
  (25 shorter events, 0.3 us)
Async XLA Ops:
  0.0 4.5 %copy-start.2 = (s32[16,8]{0,1:T(8,128)S(1)}, s32[16,8]{0,1:T(8,128)}, u32[]{:S(2)}) copy-start(s32[16,8]{0,1:T(8,128)} %param.7) | copy-start | bytes 1540
  0.0 4.5 %copy-start.1 = (s32[16,8]{0,1:T(8,128)S(1)}, s32[16,8]{0,1:T(8,128)}, u32[]{:S(2)}) copy-start(s32[16,8]{0,1:T(8,128)} %param.6) | copy-start | bytes 1540
  0.0 7.8 %collective-permute-start.2 = (f32[256,128]{1,0:T(8,128)}, f32[256,128]{1,0:T(8,128)S(1)}, u32[]{:S(2)}, u32[]{:S(2)}) collective-permute-start(f32[256,128]{1,0:T(8,128)} %refs_4_.1), channel_id=1, source_target_pairs={{0,8},{8,0},{16,24},{24,16},{1,9},{9,1},{17,25},{25,17},{2,10},{10... | collective-permute-start | bytes 393224 | tf_op jit(solution)/shard_map/ppermute | solution.py:25
  3.0 8.0 %collective-permute-start.1 = (f32[256,128]{1,0:T(8,128)}, f32[256,128]{1,0:T(8,128)S(1)}, u32[]{:S(2)}, u32[]{:S(2)}) collective-permute-start(f32[256,128]{1,0:T(8,128)} %refs_4_.1), channel_id=1, source_target_pairs={{0,16},{8,24},{16,0},{24,8},{1,17},{9,25},{17,1},{25,9},{2,18},{10... | collective-permute-start | bytes 393224 | tf_op jit(solution)/shard_map/ppermute | solution.py:25
  4.5 7.2 %collective-permute-start = (f32[256,128]{1,0:T(8,128)}, f32[256,128]{1,0:T(8,128)S(1)}, u32[]{:S(2)}, u32[]{:S(2)}) collective-permute-start(f32[256,128]{1,0:T(8,128)} %refs_4_.1), channel_id=1, source_target_pairs={{0,24},{8,16},{16,8},{24,0},{1,25},{9,17},{17,9},{25,1},{2,26},{10... | collective-permute-start | bytes 393224 | tf_op jit(solution)/shard_map/ppermute | solution.py:25
  4.5 2.8 %copy-start = (f32[256,128]{1,0:T(8,128)S(1)}, f32[256,128]{1,0:T(8,128)}, u32[]{:S(2)}) copy-start(f32[256,128]{1,0:T(8,128)} %refs_4_.1) | copy-start | bytes 393220
  12.0 6.5 %collective-permute-start.3 = (f32[768,128]{1,0:T(8,128)S(1)}, f32[768,128]{1,0:T(8,128)S(1)}, u32[]{:S(2)}, u32[]{:S(2)}) collective-permute-start(f32[768,128]{1,0:T(8,128)S(1)} %multiply.21), channel_id=1, source_target_pairs={{0,1},{1,0},{2,3},{3,2},{4,5},{5,4},{6,7},{7,6},{8,9},{9,8},{10,11... | collective-permute-start | bytes 1179656 | tf_op jit(solution)/shard_map/ppermute | solution.py:25
  12.3 2.3 %collective-permute-start.5 = (f32[256,128]{1,0:T(8,128)S(1)}, f32[256,128]{1,0:T(8,128)S(1)}, u32[]{:S(2)}, u32[]{:S(2)}) collective-permute-start(f32[256,128]{1,0:T(8,128)S(1)} %multiply.23), channel_id=1, source_target_pairs={{0,1},{1,0},{2,3},{3,2},{4,5},{5,4},{6,7},{7,6},{8,9},{9,8},{10,11... | collective-permute-start | bytes 393224 | tf_op jit(solution)/shard_map/ppermute | solution.py:25
  13.4 1.2 %collective-permute-start.4 = (f32[32,128]{1,0:T(8,128)S(1)}, f32[32,128]{1,0:T(8,128)S(1)}, u32[]{:S(2)}, u32[]{:S(2)}) collective-permute-start(f32[32,128]{1,0:T(8,128)S(1)} %slice.52), channel_id=1, source_target_pairs={{0,1},{1,0},{2,3},{3,2},{4,5},{5,4},{6,7},{7,6},{8,9},{9,8},{10,11... | collective-permute-start | bytes 49160 | tf_op jit(solution)/shard_map/ppermute | solution.py:25
  14.8 7.0 %collective-permute-start.6 = (f32[264,128]{1,0:T(8,128)S(1)}, f32[264,128]{1,0:T(8,128)S(1)}, u32[]{:S(2)}, u32[]{:S(2)}) collective-permute-start(f32[264,128]{1,0:T(8,128)S(1)} %stagger.2), channel_id=1, source_target_pairs={{0,6},{1,7},{2,4},{3,5},{4,2},{5,3},{6,0},{7,1},{8,14},{9,15},{10,... | collective-permute-start | bytes 405512 | tf_op jit(solution)/shard_map/ppermute | solution.py:29
  18.6 7.0 %collective-permute-start.7 = (f32[264,128]{1,0:T(8,128)S(1)}, f32[264,128]{1,0:T(8,128)S(1)}, u32[]{:S(2)}, u32[]{:S(2)}) collective-permute-start(f32[264,128]{1,0:T(8,128)S(1)} %get-tuple-element.15), channel_id=1, source_target_pairs={{0,4},{1,3},{2,6},{3,1},{4,0},{5,7},{6,2},{7,5},{8,12},{9,11},{10,... | collective-permute-start | bytes 405512 | tf_op jit(solution)/shard_map/ppermute | solution.py:29
  18.6 6.9 %collective-permute-start.8 = (f32[264,128]{1,0:T(8,128)S(1)}, f32[264,128]{1,0:T(8,128)S(1)}, u32[]{:S(2)}, u32[]{:S(2)}) collective-permute-start(f32[264,128]{1,0:T(8,128)S(1)} %get-tuple-element.16), channel_id=1, source_target_pairs={{0,2},{1,5},{2,0},{3,7},{4,6},{5,1},{6,4},{7,3},{8,10},{9,13},{10,... | collective-permute-start | bytes 405512 | tf_op jit(solution)/shard_map/ppermute | solution.py:29
  26.0 5.0 %collective-permute-start.11 = (f32[256,128]{1,0:T(8,128)S(1)}, f32[256,128]{1,0:T(8,128)S(1)}, u32[]{:S(2)}, u32[]{:S(2)}) collective-permute-start(f32[256,128]{1,0:T(8,128)S(1)} %get-tuple-element.17.refs_0_), channel_id=1, source_target_pairs={{0,8},{8,0},{16,24},{24,16},{1,9},{9,1},{17,25},{25,17},{2,10},{10... | collective-permute-start | bytes 393224 | tf_op jit(solution)/shard_map/ppermute | solution.py:25
  26.5 5.0 %collective-permute-start.10 = (f32[256,128]{1,0:T(8,128)S(1)}, f32[256,128]{1,0:T(8,128)S(1)}, u32[]{:S(2)}, u32[]{:S(2)}) collective-permute-start(f32[256,128]{1,0:T(8,128)S(1)} %get-tuple-element.17.refs_0_), channel_id=1, source_target_pairs={{0,16},{8,24},{16,0},{24,8},{1,17},{9,25},{17,1},{25,9},{2,18},{10... | collective-permute-start | bytes 393224 | tf_op jit(solution)/shard_map/ppermute | solution.py:25
  28.1 5.9 %collective-permute-start.9 = (f32[256,128]{1,0:T(8,128)S(1)}, f32[256,128]{1,0:T(8,128)S(1)}, u32[]{:S(2)}, u32[]{:S(2)}) collective-permute-start(f32[256,128]{1,0:T(8,128)S(1)} %get-tuple-element.17.refs_0_), channel_id=1, source_target_pairs={{0,24},{8,16},{16,8},{24,0},{1,25},{9,17},{17,9},{25,1},{2,26},{10... | collective-permute-start | bytes 393224 | tf_op jit(solution)/shard_map/ppermute | solution.py:25
  34.3 7.1 %collective-permute-start.12 = (f32[768,128]{1,0:T(8,128)S(1)}, f32[768,128]{1,0:T(8,128)S(1)}, u32[]{:S(2)}, u32[]{:S(2)}) collective-permute-start(f32[768,128]{1,0:T(8,128)S(1)} %multiply.27), channel_id=1, source_target_pairs={{0,1},{1,0},{2,3},{3,2},{4,5},{5,4},{6,7},{7,6},{8,9},{9,8},{10,11... | collective-permute-start | bytes 1179656 | tf_op jit(solution)/shard_map/ppermute | solution.py:25
  38.4 1.4 %collective-permute-start.13 = (f32[256,128]{1,0:T(8,128)S(1)}, f32[256,128]{1,0:T(8,128)S(1)}, u32[]{:S(2)}, u32[]{:S(2)}) collective-permute-start(f32[256,128]{1,0:T(8,128)S(1)} %multiply.29), channel_id=1, source_target_pairs={{0,1},{1,0},{2,3},{3,2},{4,5},{5,4},{6,7},{7,6},{8,9},{9,8},{10,11... | collective-permute-start | bytes 393224 | tf_op jit(solution)/shard_map/ppermute | solution.py:25
  40.0 7.0 %collective-permute-start.14 = (f32[256,128]{1,0:T(8,128)S(1)}, f32[256,128]{1,0:T(8,128)S(1)}, u32[]{:S(2)}, u32[]{:S(2)}) collective-permute-start(f32[256,128]{1,0:T(8,128)S(1)} %stagger.3), channel_id=1, source_target_pairs={{0,6},{1,7},{2,4},{3,5},{4,2},{5,3},{6,0},{7,1},{8,14},{9,15},{10,... | collective-permute-start | bytes 393224 | tf_op jit(solution)/shard_map/ppermute | solution.py:29
  41.4 8.8 %collective-permute-start.15 = (f32[256,128]{1,0:T(8,128)S(1)}, f32[256,128]{1,0:T(8,128)S(1)}, u32[]{:S(2)}, u32[]{:S(2)}) collective-permute-start(f32[256,128]{1,0:T(8,128)S(1)} %get-tuple-element.21), channel_id=1, source_target_pairs={{0,4},{1,3},{2,6},{3,1},{4,0},{5,7},{6,2},{7,5},{8,12},{9,11},{10,... | collective-permute-start | bytes 393224 | tf_op jit(solution)/shard_map/ppermute | solution.py:29
  41.9 8.3 %collective-permute-start.16 = (f32[256,128]{1,0:T(8,128)S(1)}, f32[256,128]{1,0:T(8,128)S(1)}, u32[]{:S(2)}, u32[]{:S(2)}) collective-permute-start(f32[256,128]{1,0:T(8,128)S(1)} %get-tuple-element.22), channel_id=1, source_target_pairs={{0,2},{1,5},{2,0},{3,7},{4,6},{5,1},{6,4},{7,3},{8,10},{9,13},{10,... | collective-permute-start | bytes 393224 | tf_op jit(solution)/shard_map/ppermute | solution.py:29
  50.3 5.0 %collective-permute-start.19 = (f32[256,128]{1,0:T(8,128)S(1)}, f32[256,128]{1,0:T(8,128)S(1)}, u32[]{:S(2)}, u32[]{:S(2)}) collective-permute-start(f32[256,128]{1,0:T(8,128)S(1)} %fusion.13.refs_0_), channel_id=1, source_target_pairs={{0,8},{8,0},{16,24},{24,16},{1,9},{9,1},{17,25},{25,17},{2,10},{10... | collective-permute-start | bytes 393224 | tf_op jit(solution)/shard_map/ppermute | solution.py:25
  51.8 5.0 %collective-permute-start.18 = (f32[256,128]{1,0:T(8,128)S(1)}, f32[256,128]{1,0:T(8,128)S(1)}, u32[]{:S(2)}, u32[]{:S(2)}) collective-permute-start(f32[256,128]{1,0:T(8,128)S(1)} %fusion.13.refs_0_), channel_id=1, source_target_pairs={{0,16},{8,24},{16,0},{24,8},{1,17},{9,25},{17,1},{25,9},{2,18},{10... | collective-permute-start | bytes 393224 | tf_op jit(solution)/shard_map/ppermute | solution.py:25
  53.4 6.3 %collective-permute-start.17 = (f32[256,128]{1,0:T(8,128)S(1)}, f32[256,128]{1,0:T(8,128)S(1)}, u32[]{:S(2)}, u32[]{:S(2)}) collective-permute-start(f32[256,128]{1,0:T(8,128)S(1)} %fusion.13.refs_0_), channel_id=1, source_target_pairs={{0,24},{8,16},{16,8},{24,0},{1,25},{9,17},{17,9},{25,1},{2,26},{10... | collective-permute-start | bytes 393224 | tf_op jit(solution)/shard_map/ppermute | solution.py:25
  60.0 6.8 %collective-permute-start.20 = (f32[768,128]{1,0:T(8,128)S(1)}, f32[768,128]{1,0:T(8,128)S(1)}, u32[]{:S(2)}, u32[]{:S(2)}) collective-permute-start(f32[768,128]{1,0:T(8,128)S(1)} %multiply.33), channel_id=1, source_target_pairs={{0,1},{1,0},{2,3},{3,2},{4,5},{5,4},{6,7},{7,6},{8,9},{9,8},{10,11... | collective-permute-start | bytes 1179656 | tf_op jit(solution)/shard_map/ppermute | solution.py:25
  63.0 1.4 %collective-permute-start.21 = (f32[256,128]{1,0:T(8,128)S(1)}, f32[256,128]{1,0:T(8,128)S(1)}, u32[]{:S(2)}, u32[]{:S(2)}) collective-permute-start(f32[256,128]{1,0:T(8,128)S(1)} %multiply.35), channel_id=1, source_target_pairs={{0,1},{1,0},{2,3},{3,2},{4,5},{5,4},{6,7},{7,6},{8,9},{9,8},{10,11... | collective-permute-start | bytes 393224 | tf_op jit(solution)/shard_map/ppermute | solution.py:25
  64.4 8.3 %collective-permute-start.22 = (f32[256,128]{1,0:T(8,128)S(1)}, f32[256,128]{1,0:T(8,128)S(1)}, u32[]{:S(2)}, u32[]{:S(2)}) collective-permute-start(f32[256,128]{1,0:T(8,128)S(1)} %add.57), channel_id=1, source_target_pairs={{0,6},{1,7},{2,4},{3,5},{4,2},{5,3},{6,0},{7,1},{8,14},{9,15},{10,... | collective-permute-start | bytes 393224 | tf_op jit(solution)/shard_map/ppermute | solution.py:29
  66.8 12.0 %collective-permute-start.23 = (f32[256,128]{1,0:T(8,128)S(1)}, f32[256,128]{1,0:T(8,128)S(1)}, u32[]{:S(2)}, u32[]{:S(2)}) collective-permute-start(f32[256,128]{1,0:T(8,128)S(1)} %get-tuple-element.19), channel_id=1, source_target_pairs={{0,4},{1,3},{2,6},{3,1},{4,0},{5,7},{6,2},{7,5},{8,12},{9,11},{10,... | collective-permute-start | bytes 393224 | tf_op jit(solution)/shard_map/ppermute | solution.py:29
  66.9 11.9 %collective-permute-start.24 = (f32[256,128]{1,0:T(8,128)S(1)}, f32[256,128]{1,0:T(8,128)S(1)}, u32[]{:S(2)}, u32[]{:S(2)}) collective-permute-start(f32[256,128]{1,0:T(8,128)S(1)} %get-tuple-element.20), channel_id=1, source_target_pairs={{0,2},{1,5},{2,0},{3,7},{4,6},{5,1},{6,4},{7,3},{8,10},{9,13},{10,... | collective-permute-start | bytes 393224 | tf_op jit(solution)/shard_map/ppermute | solution.py:29
